TPU v7x, 32 devices: a whole 2x2x4 slice. The times are simulated.
32 devices in a mesh: dp: 4 (over z), ctx: 4 (over y, x), tp: 2 (over core).
Axes of the slice: x: 2, y: 2, z: 4, core: 2. Of those that a mesh axis runs over, the one named last changes fastest.
Arguments:
- tokens: bfloat16 [8, 2048, 2048], P('dp', 'ctx'), may hold values from -6 to 6
- cotangent: bfloat16 [8, 2048, 2048], P('dp', 'ctx'), may hold values from -6 to 6
- attention_gain: bfloat16 [2048], P(('dp', 'ctx')), may hold values from 0.5 to 1.5
- attention_bias: bfloat16 [2048], P(('dp', 'ctx')), may hold values from -3 to 3
- feedforward_gain: bfloat16 [2048], P(('dp', 'ctx')), may hold values from 0.5 to 1.5
- feedforward_bias: bfloat16 [2048], P(('dp', 'ctx')), may hold values from -3 to 3
- query_weight: bfloat16 [2048, 2048], P(('dp', 'ctx'), 'tp'), may hold values from -0.1875 to 0.1875
- query_bias: bfloat16 [2048], P('tp'), may hold values from -3 to 3
- key_weight: bfloat16 [2048, 2048], P(('dp', 'ctx'), 'tp'), may hold values from -0.1875 to 0.1875
- value_weight: bfloat16 [2048, 2048], P(('dp', 'ctx'), 'tp'), may hold values from -0.125 to 0.125
- value_bias: bfloat16 [2048], P('tp'), may hold values from -3 to 3
- output_weight: bfloat16 [2048, 2048], P('tp', ('dp', 'ctx')), may hold values from -0.5 to 0.5
- output_bias: bfloat16 [2048], P(('dp', 'ctx')), may hold values from -3 to 3
- up_weight: bfloat16 [2048, 8192], P(('dp', 'ctx'), 'tp'), may hold values from -0.125 to 0.125
- up_bias: bfloat16 [8192], P('tp'), may hold values from -3 to 3
- down_weight: bfloat16 [8192, 2048], P('tp', ('dp', 'ctx')), may hold values from -0.0625 to 0.0625
- down_bias: bfloat16 [2048], P(('dp', 'ctx')), may hold values from -3 to 3
Outputs:
- layer_output: bfloat16 [8, 2048, 2048], P('dp', 'ctx')
- input_gradient: bfloat16 [8, 2048, 2048], P('dp', 'ctx')
- attention_gain_grad: float32 [2048], P(('dp', 'ctx'))
- attention_bias_grad: float32 [2048], P(('dp', 'ctx'))
- feedforward_gain_grad: float32 [2048], P(('dp', 'ctx'))
- feedforward_bias_grad: float32 [2048], P(('dp', 'ctx'))
- query_weight_grad: float32 [2048, 2048], P(('dp', 'ctx'), 'tp')
- query_bias_grad: float32 [2048], P('tp')
- key_weight_grad: float32 [2048, 2048], P(('dp', 'ctx'), 'tp')
- value_weight_grad: float32 [2048, 2048], P(('dp', 'ctx'), 'tp')
- value_bias_grad: float32 [2048], P('tp')
- output_weight_grad: float32 [2048, 2048], P('tp', ('dp', 'ctx'))
- output_bias_grad: float32 [2048], P(('dp', 'ctx'))
- up_weight_grad: float32 [2048, 8192], P(('dp', 'ctx'), 'tp')
- up_bias_grad: float32 [8192], P('tp')
- down_weight_grad: float32 [8192, 2048], P('tp', ('dp', 'ctx'))
- down_bias_grad: float32 [2048], P(('dp', 'ctx'))
All inputs are finite; a program needn't handle non-finite values.
Results may differ from a plain program's by a relative error of at most 0.015.
The roundings to bfloat16 on the way count: a program that leaves them out, or rounds other values in their place, can miss the bound.
Values may be sent and summed in bfloat16 or wider, within the bound.
A program may use at most 384 MiB of HBM per device.

v0:
```python
import jax
import jax.numpy as jnp
from jax import lax
from jax.sharding import PartitionSpec as P

HEAD_DIM = 128
MICRO = 2


EPSILON = 1e-05
NEGATIVE = -1e30


def product(former, latter):
    return jnp.dot(former, latter, preferred_element_type=jnp.float32)


def inner(former, latter):
    return lax.dot_general(
        former, latter, (((0,), (0,)), ((), ())), preferred_element_type=jnp.float32
    )


def across(former, latter):
    return lax.dot_general(
        former, latter, (((1,), (1,)), ((), ())), preferred_element_type=jnp.float32
    )


def normalize(values):
    average = jnp.mean(values, axis=-1, keepdims=True)
    centred = values - average
    spread = lax.rsqrt(jnp.mean(centred * centred, axis=-1, keepdims=True) + EPSILON)
    return (centred * spread, spread)


def norm_back(gradient, normed, spread):
    first_mean = jnp.mean(gradient, axis=-1, keepdims=True)
    second_mean = jnp.mean(gradient * normed, axis=-1, keepdims=True)
    return spread * (gradient - first_mean - normed * second_mean)


def gelu_slope(values):
    cumulative = 0.5 * (1.0 + lax.erf(values * 0.7071067811865476))
    density = jnp.exp(-0.5 * values * values) * 0.3989422804014327
    return cumulative + values * density


def fetch(row_shards, column_shards):
    row_parts = (
        lax.all_gather(row_shards[0], ("dp", "ctx"), axis=0, tiled=True),
        lax.all_gather(row_shards[1], ("dp", "ctx"), axis=0, tiled=True),
        lax.all_gather(row_shards[2], ("dp", "ctx"), axis=0, tiled=True),
        lax.all_gather(row_shards[3], ("dp", "ctx"), axis=0, tiled=True),
        lax.all_gather(row_shards[4], ("dp", "ctx"), axis=0, tiled=True),
        lax.all_gather(row_shards[5], ("dp", "ctx"), axis=0, tiled=True),
        lax.all_gather(row_shards[6], ("dp", "ctx"), axis=0, tiled=True),
        lax.all_gather(row_shards[7], ("dp", "ctx"), axis=0, tiled=True),
        lax.all_gather(row_shards[8], ("dp", "ctx"), axis=0, tiled=True),
        lax.all_gather(row_shards[9], ("dp", "ctx"), axis=0, tiled=True),
    )
    column_parts = (
        lax.all_gather(column_shards[0], ("dp", "ctx"), axis=1, tiled=True),
        lax.all_gather(column_shards[1], ("dp", "ctx"), axis=1, tiled=True),
    )
    return (tuple(row_parts), tuple(column_parts))


def split_heads(matrix):
    return matrix.reshape(matrix.shape[0], matrix.shape[1] // HEAD_DIM, HEAD_DIM)


def attend_forward(member, allowed):
    query_rows, key_rows, value_rows = member
    query_heads = split_heads(query_rows)
    key_heads = split_heads(key_rows)
    value_heads = split_heads(value_rows)
    scaling = HEAD_DIM ** (-0.5)
    scores = (
        jnp.einsum("qhd,khd->hqk", query_heads, key_heads, preferred_element_type=jnp.float32)
        * scaling
    )
    scores = jnp.where(allowed[None, :, :], scores, NEGATIVE)
    highest = jnp.max(scores, axis=-1, keepdims=True)
    exponent = jnp.exp(scores - highest)
    row_total = jnp.sum(exponent, axis=-1, keepdims=True)
    attention = (exponent / row_total).astype(jnp.bfloat16)
    mixed_heads = jnp.einsum(
        "hqk,khd->qhd", attention, value_heads, preferred_element_type=jnp.float32
    )
    log_total = highest[..., 0] + jnp.log(row_total[..., 0])
    return (mixed_heads.reshape(query_rows.shape[0], query_rows.shape[1]), log_total)


def attend_backward(member, allowed):
    query_rows, key_rows, value_rows, mixed_grad, log_total = member
    query_heads = split_heads(query_rows)
    key_heads = split_heads(key_rows)
    value_heads = split_heads(value_rows)
    grad_heads = split_heads(mixed_grad)
    scaling = HEAD_DIM ** (-0.5)
    scores = (
        jnp.einsum("qhd,khd->hqk", query_heads, key_heads, preferred_element_type=jnp.float32)
        * scaling
    )
    scores = jnp.where(allowed[None, :, :], scores, NEGATIVE)
    attention = jnp.exp(scores - log_total[..., None])
    grad_attention = jnp.einsum(
        "qhd,khd->hqk", grad_heads, value_heads, preferred_element_type=jnp.float32
    )
    centre = jnp.sum(attention * grad_attention, axis=-1, keepdims=True)
    grad_scores = (attention * (grad_attention - centre)).astype(jnp.bfloat16)
    rounded = attention.astype(jnp.bfloat16)
    query_grad = (
        jnp.einsum("hqk,khd->qhd", grad_scores, key_heads, preferred_element_type=jnp.float32)
        * scaling
    )
    key_grad = (
        jnp.einsum("hqk,qhd->khd", grad_scores, query_heads, preferred_element_type=jnp.float32)
        * scaling
    )
    value_grad = jnp.einsum("hqk,qhd->khd", rounded, grad_heads, preferred_element_type=jnp.float32)
    query_count, local_width = query_rows.shape
    key_count = key_rows.shape[0]
    return (
        query_grad.reshape(query_count, local_width).astype(jnp.bfloat16),
        key_grad.reshape(key_count, local_width),
        value_grad.reshape(key_count, local_width),
    )


def body(
    tokens,
    cotangent,
    attention_gain,
    attention_bias,
    feedforward_gain,
    feedforward_bias,
    query_weight,
    query_bias,
    key_weight,
    value_weight,
    value_bias,
    output_weight,
    output_bias,
    up_weight,
    up_bias,
    down_weight,
    down_bias,
):
    local_seqs, local_rows, model_width = tokens.shape
    per_batch = local_seqs // MICRO
    local_width = query_weight.shape[1]
    hidden_here = up_weight.shape[1]
    length = local_rows * lax.axis_size("ctx")
    position = lax.axis_index("ctx") * local_rows + jnp.arange(local_rows, dtype=jnp.int32)
    allowed = jnp.arange(length, dtype=jnp.int32)[None, :] <= position[:, None]
    row_shards = (
        attention_gain,
        attention_bias,
        feedforward_gain,
        feedforward_bias,
        output_bias,
        down_bias,
        query_weight,
        key_weight,
        value_weight,
        up_weight,
    )
    column_shards = (output_weight, down_weight)
    query_shift = query_bias.astype(jnp.float32)
    value_shift = value_bias.astype(jnp.float32)
    up_shift = up_bias.astype(jnp.float32)
    gain_one_sum = jnp.zeros((model_width,), jnp.float32)
    bias_one_sum = jnp.zeros((model_width,), jnp.float32)
    gain_two_sum = jnp.zeros((model_width,), jnp.float32)
    bias_two_sum = jnp.zeros((model_width,), jnp.float32)
    output_bias_sum = jnp.zeros((model_width,), jnp.float32)
    down_bias_sum = jnp.zeros((model_width,), jnp.float32)
    query_sum = jnp.zeros((model_width, local_width), jnp.float32)
    key_sum = jnp.zeros((model_width, local_width), jnp.float32)
    value_sum = jnp.zeros((model_width, local_width), jnp.float32)
    output_sum = jnp.zeros((local_width, model_width), jnp.float32)
    up_sum = jnp.zeros((model_width, hidden_here), jnp.float32)
    down_sum = jnp.zeros((hidden_here, model_width), jnp.float32)
    query_bias_sum = jnp.zeros((local_width,), jnp.float32)
    value_bias_sum = jnp.zeros((local_width,), jnp.float32)
    up_bias_sum = jnp.zeros((hidden_here,), jnp.float32)
    outputs = []
    input_grads = []
    for batch_index in range(MICRO):
        rows_full, cols_full = fetch(row_shards, column_shards)
        gain_one = rows_full[0].astype(jnp.float32)
        shift_one = rows_full[1].astype(jnp.float32)
        gain_two = rows_full[2].astype(jnp.float32)
        shift_two = rows_full[3].astype(jnp.float32)
        output_shift = rows_full[4].astype(jnp.float32)
        down_shift = rows_full[5].astype(jnp.float32)
        batch_tokens = tokens[batch_index * per_batch : (batch_index + 1) * per_batch]
        flat_tokens = batch_tokens.astype(jnp.float32).reshape(-1, model_width)
        normed_one, spread_one = normalize(flat_tokens)
        input_one = (normed_one * gain_one + shift_one).astype(jnp.bfloat16)
        queries = (
            (product(input_one, rows_full[6]) + query_shift)
            .astype(jnp.bfloat16)
            .reshape(per_batch, local_rows, local_width)
        )
        key_rows = (
            product(input_one, rows_full[7])
            .astype(jnp.bfloat16)
            .reshape(per_batch, local_rows, local_width)
        )
        value_rows = (
            (product(input_one, rows_full[8]) + value_shift)
            .astype(jnp.bfloat16)
            .reshape(per_batch, local_rows, local_width)
        )
        gathered_keys, gathered_values = (
            lax.all_gather(key_rows, "ctx", axis=1, tiled=True),
            lax.all_gather(value_rows, "ctx", axis=1, tiled=True),
        )
        mixed_heads, log_total = lax.map(
            lambda member: attend_forward(member, allowed),
            (queries, gathered_keys, gathered_values),
        )
        mixed_low = mixed_heads.reshape(-1, local_width).astype(jnp.bfloat16)
        residual = flat_tokens + (lax.psum(product(mixed_low, cols_full[0]), "tp") + output_shift)
        normed_two, spread_two = normalize(residual)
        input_two = (normed_two * gain_two + shift_two).astype(jnp.bfloat16)
        hidden_pre = product(input_two, rows_full[9]) + up_shift
        hidden = jax.nn.gelu(hidden_pre, approximate=False).astype(jnp.bfloat16)
        block_out = residual + (
            lax.psum(product(hidden, cols_full[1]).astype(jnp.bfloat16), "tp").astype(jnp.float32)
            + down_shift
        )
        outputs.append(block_out.astype(jnp.bfloat16).reshape(per_batch, local_rows, model_width))
        barred = lax.optimization_barrier((row_shards, column_shards, block_out))
        rows_full, cols_full = fetch(barred[0], barred[1])
        gain_one = rows_full[0].astype(jnp.float32)
        gain_two = rows_full[2].astype(jnp.float32)
        incoming = cotangent[batch_index * per_batch : (batch_index + 1) * per_batch].reshape(
            -1, model_width
        )
        down_sum = down_sum + inner(hidden, incoming)
        down_bias_sum = down_bias_sum + jnp.sum(incoming.astype(jnp.float32), axis=0)
        hidden_grad = (across(incoming, cols_full[1]) * gelu_slope(hidden_pre)).astype(jnp.bfloat16)
        up_sum = up_sum + inner(input_two, hidden_grad)
        up_bias_sum = up_bias_sum + jnp.sum(hidden_grad.astype(jnp.float32), axis=0)
        second_grad = lax.psum(across(hidden_grad, rows_full[9]), "tp")
        gain_two_sum = gain_two_sum + jnp.sum(second_grad * normed_two, axis=0)
        bias_two_sum = bias_two_sum + jnp.sum(second_grad, axis=0)
        residual_grad = incoming.astype(jnp.float32) + norm_back(
            second_grad * gain_two, normed_two, spread_two
        )
        branch_grad = residual_grad.astype(jnp.bfloat16)
        output_sum = output_sum + inner(mixed_low, branch_grad)
        output_bias_sum = output_bias_sum + jnp.sum(branch_grad.astype(jnp.float32), axis=0)
        mixed_grad = (
            across(branch_grad, cols_full[0])
            .astype(jnp.bfloat16)
            .reshape(per_batch, local_rows, local_width)
        )
        query_grad, key_terms, value_terms = lax.map(
            lambda member: attend_backward(member, allowed),
            (queries, gathered_keys, gathered_values, mixed_grad, log_total),
        )
        key_totals, value_totals = (
            lax.psum_scatter(key_terms, "ctx", scatter_dimension=1, tiled=True),
            lax.psum_scatter(value_terms, "ctx", scatter_dimension=1, tiled=True),
        )
        query_flat = query_grad.reshape(-1, local_width)
        key_flat = key_totals.astype(jnp.bfloat16).reshape(-1, local_width)
        value_flat = value_totals.astype(jnp.bfloat16).reshape(-1, local_width)
        query_sum = query_sum + inner(input_one, query_flat)
        key_sum = key_sum + inner(input_one, key_flat)
        value_sum = value_sum + inner(input_one, value_flat)
        query_bias_sum = query_bias_sum + jnp.sum(query_flat.astype(jnp.float32), axis=0)
        value_bias_sum = value_bias_sum + jnp.sum(value_flat.astype(jnp.float32), axis=0)
        first_terms = (
            across(query_flat, rows_full[6])
            + across(key_flat, rows_full[7])
            + across(value_flat, rows_full[8])
        )
        first_grad = lax.psum(first_terms.astype(jnp.bfloat16), "tp").astype(jnp.float32)
        gain_one_sum = gain_one_sum + jnp.sum(first_grad * normed_one, axis=0)
        bias_one_sum = bias_one_sum + jnp.sum(first_grad, axis=0)
        token_grad = residual_grad + norm_back(first_grad * gain_one, normed_one, spread_one)
        input_grads.append(
            token_grad.astype(jnp.bfloat16).reshape(per_batch, local_rows, model_width)
        )
    row_grads = (
        lax.psum_scatter(gain_one_sum, ("dp", "ctx"), scatter_dimension=0, tiled=True),
        lax.psum_scatter(bias_one_sum, ("dp", "ctx"), scatter_dimension=0, tiled=True),
        lax.psum_scatter(gain_two_sum, ("dp", "ctx"), scatter_dimension=0, tiled=True),
        lax.psum_scatter(bias_two_sum, ("dp", "ctx"), scatter_dimension=0, tiled=True),
        lax.psum_scatter(output_bias_sum, ("dp", "ctx"), scatter_dimension=0, tiled=True),
        lax.psum_scatter(down_bias_sum, ("dp", "ctx"), scatter_dimension=0, tiled=True),
        lax.psum_scatter(query_sum, ("dp", "ctx"), scatter_dimension=0, tiled=True),
        lax.psum_scatter(key_sum, ("dp", "ctx"), scatter_dimension=0, tiled=True),
        lax.psum_scatter(value_sum, ("dp", "ctx"), scatter_dimension=0, tiled=True),
        lax.psum_scatter(up_sum, ("dp", "ctx"), scatter_dimension=0, tiled=True),
    )
    column_grads = (
        lax.psum_scatter(output_sum, ("dp", "ctx"), scatter_dimension=1, tiled=True),
        lax.psum_scatter(down_sum, ("dp", "ctx"), scatter_dimension=1, tiled=True),
    )
    bias_totals = lax.psum((query_bias_sum, value_bias_sum, up_bias_sum), ("dp", "ctx"))
    return (
        jnp.concatenate(outputs, axis=0),
        jnp.concatenate(input_grads, axis=0),
        row_grads[0],
        row_grads[1],
        row_grads[2],
        row_grads[3],
        row_grads[6],
        bias_totals[0],
        row_grads[7],
        row_grads[8],
        bias_totals[1],
        column_grads[0],
        row_grads[4],
        row_grads[9],
        bias_totals[2],
        column_grads[1],
        row_grads[5],
    )


def solution(mesh):
    placed = (
        P("dp", "ctx", None),
        P("dp", "ctx", None),
        P(("dp", "ctx")),
        P(("dp", "ctx")),
        P(("dp", "ctx")),
        P(("dp", "ctx")),
        P(("dp", "ctx"), "tp"),
        P("tp"),
        P(("dp", "ctx"), "tp"),
        P(("dp", "ctx"), "tp"),
        P("tp"),
        P("tp", ("dp", "ctx")),
        P(("dp", "ctx")),
        P(("dp", "ctx"), "tp"),
        P("tp"),
        P("tp", ("dp", "ctx")),
        P(("dp", "ctx")),
    )
    return jax.shard_map(
        body,
        mesh=mesh,
        in_specs=placed,
        out_specs=(
            P("dp", "ctx", None),
            P("dp", "ctx", None),
            P(("dp", "ctx")),
            P(("dp", "ctx")),
            P(("dp", "ctx")),
            P(("dp", "ctx")),
            P(("dp", "ctx"), "tp"),
            P("tp"),
            P(("dp", "ctx"), "tp"),
            P(("dp", "ctx"), "tp"),
            P("tp"),
            P("tp", ("dp", "ctx")),
            P(("dp", "ctx")),
            P(("dp", "ctx"), "tp"),
            P("tp"),
            P("tp", ("dp", "ctx")),
            P(("dp", "ctx")),
        ),
        check_vma=False,
    )
```

profile of v0, /device:TPU:0, one launch (start us, length us, event | category | flops | bytes accessed | tf_op | source)
XLA Modules:
  0.0 5404.7 jit_solution(1549715931108500237)
XLA Ops:
  9.5 42.5 all-gather.5
  52.0 35.9 all-gather.4
  98.6 68.6 %all-gather.37.cloned.1.call-done = bf16[2048,1024]{1,0:T(8,128)(2,1)} async-done(((bf16[128,1024]{1,0:T(8,128)(2,1)}), bf16[2048,1024]{1,0:T(8,128)(2,1)}) %all-gather.37.cloned.1.call-update) | async-done | bytes 4194320 | tf_op jit(solution)/shard_map/all_gather | solution.py:59
  181.5 63.2 %all-gather.39.cloned.1.call-done = bf16[2048,1024]{1,0:T(8,128)(2,1)} async-done(((bf16[128,1024]{1,0:T(8,128)(2,1)}), bf16[2048,1024]{1,0:T(8,128)(2,1)}) %all-gather.39.cloned.1.call-update) | async-done | bytes 4194320 | tf_op jit(solution)/shard_map/all_gather | solution.py:57
  369.9 38.5 all-gather.75.cloned.1.call-done
  414.8 85.4 %all-gather.43.cloned.1.call-done = bf16[1024,2048]{1,0:T(8,128)(2,1)} async-done(((bf16[1024,128]{1,0:T(8,128)(2,1)}), bf16[1024,2048]{1,0:T(8,128)(2,1)}) %all-gather.43.cloned.1.call-update) | async-done | bytes 4194320 | tf_op jit(solution)/shard_map/all_gather | solution.py:63
  575.6 39.5 all-gather.6
  650.8 37.8 all-gather.7
  697.6 111.2 %all-gather.45.cloned.1.call-done = bf16[2048,4096]{1,0:T(8,128)(2,1)} async-done(((bf16[128,4096]{1,0:T(8,128)(2,1)}), bf16[2048,4096]{1,0:T(8,128)(2,1)}) %all-gather.45.cloned.1.call-update) | async-done | bytes 16777232 | tf_op jit(solution)/shard_map/all_gather | solution.py:60
  825.7 50.0 fusion.14
  875.7 183.7 %all-gather.47.cloned.1.call-done = bf16[4096,2048]{1,0:T(8,128)(2,1)} async-done(((bf16[4096,128]{1,0:T(8,128)(2,1)}), bf16[4096,2048]{1,0:T(8,128)(2,1)}) %all-gather.47.cloned.1.call-update) | async-done | bytes 16777232 | tf_op jit(solution)/shard_map/all_gather | solution.py:64
  1084.8 37.6 all-gather.9
  1132.5 243.9 %all-gather.61.cloned.1.call-done = bf16[4096,2048]{1,0:T(8,128)(2,1)} async-done(((bf16[4096,128]{1,0:T(8,128)(2,1)}), bf16[4096,2048]{1,0:T(8,128)(2,1)}) %all-gather.61.cloned.1.call-update) | async-done | bytes 16777232 | tf_op jit(solution)/shard_map/all_gather | solution.py:64
  1395.4 231.8 %all-gather.49.cloned.1.call-done = bf16[4096,2048]{1,0:T(8,128)(2,1)} async-done(((bf16[4096,128]{1,0:T(8,128)(2,1)}), bf16[4096,2048]{1,0:T(8,128)(2,1)}) %all-gather.49.cloned.1.call-update) | async-done | bytes 16777232 | tf_op jit(solution)/shard_map/all_gather | solution.py:64
  1645.9 174.1 %all-gather.63.cloned.1.call-done = bf16[2048,4096]{1,0:T(8,128)(2,1)} async-done(((bf16[128,4096]{1,0:T(8,128)(2,1)}), bf16[2048,4096]{1,0:T(8,128)(2,1)}) %all-gather.63.cloned.1.call-update) | async-done | bytes 16777232 | tf_op jit(solution)/shard_map/all_gather | solution.py:60
  1835.4 177.4 %all-gather.51.cloned.1.call-done = bf16[2048,4096]{1,0:T(8,128)(2,1)} async-done(((bf16[128,4096]{1,0:T(8,128)(2,1)}), bf16[2048,4096]{1,0:T(8,128)(2,1)}) %all-gather.51.cloned.1.call-update) | async-done | bytes 16777232 | tf_op jit(solution)/shard_map/all_gather | solution.py:60
  2030.8 37.6 all-gather.12
  2410.9 71.3 %all-gather.69.cloned.1.call-done = bf16[2048,1024]{1,0:T(8,128)(2,1)} async-done(((bf16[128,1024]{1,0:T(8,128)(2,1)}), bf16[2048,1024]{1,0:T(8,128)(2,1)}) %all-gather.69.cloned.1.call-update) | async-done | bytes 4194320 | tf_op jit(solution)/shard_map/all_gather | solution.py:58
  2482.3 88.4 %reduce-scatter.15.cloned.1.call-done = f32[1,512,1024]{1,2,0:T(8,128)} async-done(((f32[1,2048,1024]{1,2,0:T(8,128)}), f32[1,512,1024]{1,2,0:T(8,128)}) %reduce-scatter.15.cloned.1.call-update) | async-done | bytes 2097168 | tf_op jit(solution)/shard_map/reduce_scatter | solution.py:268
  2577.8 71.6 %all-gather.57.cloned.1.call-done = bf16[2048,1024]{1,0:T(8,128)(2,1)} async-done(((bf16[128,1024]{1,0:T(8,128)(2,1)}), bf16[2048,1024]{1,0:T(8,128)(2,1)}) %all-gather.57.cloned.1.call-update) | async-done | bytes 4194320 | tf_op jit(solution)/shard_map/all_gather | solution.py:58
  2649.4 88.1 %reduce-scatter.11.cloned.1.call-done = f32[1,512,1024]{1,2,0:T(8,128)} async-done(((f32[1,2048,1024]{1,2,0:T(8,128)}), f32[1,512,1024]{1,2,0:T(8,128)}) %reduce-scatter.11.cloned.1.call-update) | async-done | bytes 2097168 | tf_op jit(solution)/shard_map/reduce_scatter | solution.py:268
  2744.8 71.7 %all-gather.71.cloned.1.call-done = bf16[2048,1024]{1,0:T(8,128)(2,1)} async-done(((bf16[128,1024]{1,0:T(8,128)(2,1)}), bf16[2048,1024]{1,0:T(8,128)(2,1)}) %all-gather.71.cloned.1.call-update) | async-done | bytes 4194320 | tf_op jit(solution)/shard_map/all_gather | solution.py:59
  2816.6 88.2 %reduce-scatter.17.cloned.1.call-done = f32[1,512,1024]{1,2,0:T(8,128)} async-done(((f32[1,2048,1024]{1,2,0:T(8,128)}), f32[1,512,1024]{1,2,0:T(8,128)}) %reduce-scatter.17.cloned.1.call-update) | async-done | bytes 2097168 | tf_op jit(solution)/shard_map/reduce_scatter | solution.py:269
  2913.8 69.9 %all-gather.59.cloned.1.call-done = bf16[2048,1024]{1,0:T(8,128)(2,1)} async-done(((bf16[128,1024]{1,0:T(8,128)(2,1)}), bf16[2048,1024]{1,0:T(8,128)(2,1)}) %all-gather.59.cloned.1.call-update) | async-done | bytes 4194320 | tf_op jit(solution)/shard_map/all_gather | solution.py:59
  2983.7 88.1 %reduce-scatter.13.cloned.1.call-done = f32[1,512,1024]{1,2,0:T(8,128)} async-done(((f32[1,2048,1024]{1,2,0:T(8,128)}), f32[1,512,1024]{1,2,0:T(8,128)}) %reduce-scatter.13.cloned.1.call-update) | async-done | bytes 2097168 | tf_op jit(solution)/shard_map/reduce_scatter | solution.py:269
  3081.6 39.4 all-gather.13
  3340.4 122.9 %reduce-scatter.19.cloned.1.call-done = f32[128,1024]{1,0:T(8,128)} async-done(((f32[2048,1024]{1,0:T(8,128)}), f32[128,1024]{1,0:T(8,128)}) %reduce-scatter.19.cloned.1.call-update) | async-done | bytes 524304 | tf_op jit(solution)/shard_map/reduce_scatter | solution.py:298
  3463.3 183.1 %reduce-scatter.25.cloned.1.call-done = f32[1024,128]{1,0:T(8,128)} async-done(((f32[1024,2048]{1,0:T(8,128)}), f32[1024,128]{1,0:T(8,128)}) %reduce-scatter.25.cloned.1.call-update) | async-done | bytes 524304 | tf_op jit(solution)/shard_map/reduce_scatter | solution.py:304
  3646.4 689.0 %reduce-scatter.29.cloned.1.call-done = f32[4096,128]{1,0:T(8,128)} async-done(((f32[4096,2048]{1,0:T(8,128)}), f32[4096,128]{1,0:T(8,128)}) %reduce-scatter.29.cloned.1.call-update) | async-done | bytes 2097168 | tf_op jit(solution)/shard_map/reduce_scatter | solution.py:305
  4335.4 186.4 %reduce-scatter.21.cloned.1.call-done = f32[128,1024]{1,0:T(8,128)} async-done(((f32[2048,1024]{1,0:T(8,128)}), f32[128,1024]{1,0:T(8,128)}) %reduce-scatter.21.cloned.1.call-update) | async-done | bytes 524304 | tf_op jit(solution)/shard_map/reduce_scatter | solution.py:299
  4521.8 183.1 %reduce-scatter.23.cloned.1.call-done = f32[128,1024]{1,0:T(8,128)} async-done(((f32[2048,1024]{1,0:T(8,128)}), f32[128,1024]{1,0:T(8,128)}) %reduce-scatter.23.cloned.1.call-update) | async-done | bytes 524304 | tf_op jit(solution)/shard_map/reduce_scatter | solution.py:300
  4704.9 688.8 %reduce-scatter.27.cloned.1.call-done = f32[128,4096]{1,0:T(8,128)} async-done(((f32[2048,4096]{1,0:T(8,128)}), f32[128,4096]{1,0:T(8,128)}) %reduce-scatter.27.cloned.1.call-update) | async-done | bytes 2097168 | tf_op jit(solution)/shard_map/reduce_scatter | solution.py:301
  (399 shorter events, 999.2 us)
Async XLA Ops:
  8.7 236.0 %all-gather.39.cloned.1.call-start = ((), (), s32[]{:S(2)}) async-start(), calls=%async_computation.11 | async-start | bytes 4456448 | tf_op jit(solution)/shard_map/all_gather | solution.py:57
  9.4 288.9 %all-gather.79.cloned.1.call-start = ((), (), s32[]{:S(2)}) async-start(), calls=%async_computation.41 | async-start | bytes 5242880 | tf_op jit(solution)/shard_map/all_gather | solution.py:219
  98.5 254.8 %all-gather.77.cloned.1.call-start = ((), (), s32[]{:S(2)}) async-start(), calls=%async_computation.40 | async-start | bytes 5242880 | tf_op jit(solution)/shard_map/all_gather | solution.py:220
  173.4 234.9 %all-gather.75.cloned.1.call-start = ((), (), s32[]{:S(2)}) async-start(), calls=%async_computation.39 | async-start | bytes 5242880 | tf_op jit(solution)/shard_map/all_gather | solution.py:219
  179.7 320.5 %all-gather.43.cloned.1.call-start = ((), (), s32[]{:S(2)}) async-start(), calls=%async_computation.13 | async-start | bytes 4456448 | tf_op jit(solution)/shard_map/all_gather | solution.py:63
  180.5 372.6 %all-gather.73.cloned.1.call-start = ((), (), s32[]{:S(2)}) async-start(), calls=%async_computation.38 | async-start | bytes 5242880 | tf_op jit(solution)/shard_map/all_gather | solution.py:220
  265.9 422.7 %all-reduce.21.cloned.1.call-start = ((), (), s32[]{:S(2)}) async-start(), calls=%async_computation.44 | async-start | bytes 16777216 | tf_op jit(solution)/shard_map/psum | solution.py:227
  574.8 484.6 %all-gather.47.cloned.1.call-start = ((), (), s32[]{:S(2)}) async-start(), calls=%async_computation.15 | async-start | bytes 17825792 | tf_op jit(solution)/shard_map/all_gather | solution.py:64
  575.5 546.9 %all-reduce.25.cloned.1.call-start = ((), (), s32[]{:S(2)}) async-start(), calls=%async_computation.46 | async-start | bytes 8388608 | tf_op jit(solution)/shard_map/psum | solution.py:233
  1084.1 292.3 %all-gather.61.cloned.1.call-start = ((), (), s32[]{:S(2)}) async-start(), calls=%async_computation.24 | async-start | bytes 17825792 | tf_op jit(solution)/shard_map/all_gather | solution.py:64
  1130.8 496.4 %all-gather.49.cloned.1.call-start = ((), (), s32[]{:S(2)}) async-start(), calls=%async_computation.16 | async-start | bytes 17825792 | tf_op jit(solution)/shard_map/all_gather | solution.py:64
  1131.3 688.7 %all-gather.63.cloned.1.call-start = ((), (), s32[]{:S(2)}) async-start(), calls=%async_computation.25 | async-start | bytes 17825792 | tf_op jit(solution)/shard_map/all_gather | solution.py:60
  1131.9 880.9 %all-gather.51.cloned.1.call-start = ((), (), s32[]{:S(2)}) async-start(), calls=%async_computation.17 | async-start | bytes 17825792 | tf_op jit(solution)/shard_map/all_gather | solution.py:60
  1132.5 971.3 %all-reduce.19.cloned.1.call-start = ((), (), s32[]{:S(2)}) async-start(), calls=%async_computation.43 | async-start | bytes 16777216 | tf_op jit(solution)/shard_map/psum | solution.py:249
  2029.4 337.4 %all-gather.67.cloned.1.call-start = ((), (), s32[]{:S(2)}) async-start(), calls=%async_computation.27 | async-start | bytes 4456448 | tf_op jit(solution)/shard_map/all_gather | solution.py:57
  2030.0 374.4 %all-gather.55.cloned.1.call-start = ((), (), s32[]{:S(2)}) async-start(), calls=%async_computation.19 | async-start | bytes 4456448 | tf_op jit(solution)/shard_map/all_gather | solution.py:57
  2030.7 451.5 %all-gather.69.cloned.1.call-start = ((), (), s32[]{:S(2)}) async-start(), calls=%async_computation.29 | async-start | bytes 4456448 | tf_op jit(solution)/shard_map/all_gather | solution.py:58
  2103.8 466.9 %reduce-scatter.15.cloned.1.call-start = ((), (), s32[]{:S(2)}) async-start(), calls=%async_computation.28 | async-start | bytes 10485760 | tf_op jit(solution)/shard_map/reduce_scatter | solution.py:268
  2230.1 419.2 %all-gather.57.cloned.1.call-start = ((), (), s32[]{:S(2)}) async-start(), calls=%async_computation.21 | async-start | bytes 4456448 | tf_op jit(solution)/shard_map/all_gather | solution.py:58
  2230.9 506.6 %reduce-scatter.11.cloned.1.call-start = ((), (), s32[]{:S(2)}) async-start(), calls=%async_computation.20 | async-start | bytes 10485760 | tf_op jit(solution)/shard_map/reduce_scatter | solution.py:268
  2319.9 496.7 %all-gather.71.cloned.1.call-start = ((), (), s32[]{:S(2)}) async-start(), calls=%async_computation.31 | async-start | bytes 4456448 | tf_op jit(solution)/shard_map/all_gather | solution.py:59
  2320.4 584.3 %reduce-scatter.17.cloned.1.call-start = ((), (), s32[]{:S(2)}) async-start(), calls=%async_computation.30 | async-start | bytes 10485760 | tf_op jit(solution)/shard_map/reduce_scatter | solution.py:269
  2338.0 645.6 %all-gather.59.cloned.1.call-start = ((), (), s32[]{:S(2)}) async-start(), calls=%async_computation.23 | async-start | bytes 4456448 | tf_op jit(solution)/shard_map/all_gather | solution.py:59
  2338.8 733.0 %reduce-scatter.13.cloned.1.call-start = ((), (), s32[]{:S(2)}) async-start(), calls=%async_computation.22 | async-start | bytes 10485760 | tf_op jit(solution)/shard_map/reduce_scatter | solution.py:269
  2356.0 813.1 %all-reduce.23.cloned.1.call-start = ((), (), s32[]{:S(2)}) async-start(), calls=%async_computation.45 | async-start | bytes 8388608 | tf_op jit(solution)/shard_map/psum | solution.py:284
  3081.1 251.7 %all-reduce.17.cloned.1.call-start = ((), (), s32[]{:S(2)}) async-start(), calls=%async_computation.42 | async-start | bytes 147456
  3176.9 286.4 %reduce-scatter.19.cloned.1.call-start = ((), (), s32[]{:S(2)}) async-start(), calls=%async_computation.32 | async-start | bytes 8912896 | tf_op jit(solution)/shard_map/reduce_scatter | solution.py:298
  3187.0 459.4 %reduce-scatter.25.cloned.1.call-start = ((), (), s32[]{:S(2)}) async-start(), calls=%async_computation.35 | async-start | bytes 8912896 | tf_op jit(solution)/shard_map/reduce_scatter | solution.py:304
  3198.2 1137.1 %reduce-scatter.29.cloned.1.call-start = ((), (), s32[]{:S(2)}) async-start(), calls=%async_computation.37 | async-start | bytes 35651584 | tf_op jit(solution)/shard_map/reduce_scatter | solution.py:305
  3244.4 1277.4 %reduce-scatter.21.cloned.1.call-start = ((), (), s32[]{:S(2)}) async-start(), calls=%async_computation.33 | async-start | bytes 8912896 | tf_op jit(solution)/shard_map/reduce_scatter | solution.py:299
  3256.2 1448.8 %reduce-scatter.23.cloned.1.call-start = ((), (), s32[]{:S(2)}) async-start(), calls=%async_computation.34 | async-start | bytes 8912896 | tf_op jit(solution)/shard_map/reduce_scatter | solution.py:300
  3267.7 2126.1 %reduce-scatter.27.cloned.1.call-start = ((), (), s32[]{:S(2)}) async-start(), calls=%async_computation.36 | async-start | bytes 35651584 | tf_op jit(solution)/shard_map/reduce_scatter | solution.py:301
  (98 other events, 7623.0 us)
Sparse Core Ops, SparseCore 0:
  10.8 78.8 all-gather.40
  92.4 74.7 all-gather.36
  170.0 74.6 all-gather.38
  247.0 51.2 all-gather.78
  300.6 52.6 all-gather.76
  355.6 52.7 all-gather.74
  411.0 89.1 all-gather.42
  615.8 192.9 all-gather.44
  811.5 247.8 all-gather.46
  1130.9 245.4 all-gather.60
  1379.3 247.8 all-gather.48
  1630.2 189.7 all-gather.62
  1823.0 189.7 all-gather.50
  2068.2 90.4 all-gather.64
  2161.8 87.3 all-gather.52
  2252.2 74.2 all-gather.66
  2329.6 74.7 all-gather.54
  2407.5 74.6 all-gather.68
  2485.6 84.9 reduce-scatter.14
  2573.2 76.0 all-gather.56
  2652.4 84.9 reduce-scatter.10
  2740.5 76.0 all-gather.70
  2819.8 84.9 reduce-scatter.16
  2907.5 76.0 all-gather.58
  2986.7 84.9 reduce-scatter.12
  3177.0 105.4 all-reduce.16
  3285.5 177.7 reduce-scatter.18
  3466.1 180.2 reduce-scatter.24
  3649.5 685.8 reduce-scatter.28
  4338.3 183.4 reduce-scatter.20
  4524.6 180.2 reduce-scatter.22
  4707.8 685.8 reduce-scatter.26
  (5 shorter events, 181.8 us)
where the time goes:
time: 5420 us; the launch traced here: 5400 us
  waiting for transfers between devices  4220 us (78%)
  matrix products  601 us (11%)
  blocking collectives  376 us (7%)
  other arithmetic  148 us (3%)
    reduce_scatter x1, waiting for transfers between devices, body(): lax.psum_scatter(down_sum, ('dp', 'ctx'), scatter_dimension=1, tiled=True)  689 us
    reduce_scatter x1, waiting for transfers between devices, body(): lax.psum_scatter(up_sum, ('dp', 'ctx'), scatter_dimension=0, tiled=True)  689 us
    all_gather x3, waiting for transfers between devices, fetch(): lax.all_gather(column_shards[1], ('dp', 'ctx'), axis=1, tiled=True)  659 us
    all_gather x3, waiting for transfers between devices, fetch(): lax.all_gather(row_shards[9], ('dp', 'ctx'), axis=0, tiled=True)  463 us
    all_gather x3, waiting for transfers between devices, fetch(): lax.all_gather(row_shards[8], ('dp', 'ctx'), axis=0, tiled=True)  210 us
    reduce_scatter x1, waiting for transfers between devices, body(): lax.psum_scatter(key_sum, ('dp', 'ctx'), scatter_dimension=0, tiled=True)  186 us
    reduce_scatter x1, waiting for transfers between devices, body(): lax.psum_scatter(output_sum, ('dp', 'ctx'), scatter_dimension=1, tiled=True)  183 us
    reduce_scatter x1, waiting for transfers between devices, body(): lax.psum_scatter(value_sum, ('dp', 'ctx'), scatter_dimension=0, tiled=True)  183 us
  transfers between devices with their start and end apart: 37, of which 30 were waited for; matrix products, arithmetic and copies ran while one was open for 13% of the time, Pallas kernels for 0%

commit v1 on v0

v1 whole, which is shorter than its diff:
```python
import functools

import jax
import jax.numpy as jnp
from jax import lax
from jax.experimental import pallas as pl
from jax.experimental.pallas import tpu as pltpu
from jax.sharding import PartitionSpec as P

HEAD_DIM = 128
EPSILON = 1e-05
NEGATIVE = -1e30
F32 = jnp.float32
BF16 = jnp.bfloat16


def product(former, latter):
    return jnp.dot(former, latter, preferred_element_type=F32)


def inner(former, latter):
    return lax.dot_general(former, latter, (((0,), (0,)), ((), ())), preferred_element_type=F32)


def across(former, latter):
    return lax.dot_general(former, latter, (((1,), (1,)), ((), ())), preferred_element_type=F32)


def normalize(values):
    average = jnp.mean(values, axis=-1, keepdims=True)
    centred = values - average
    spread = lax.rsqrt(jnp.mean(centred * centred, axis=-1, keepdims=True) + EPSILON)
    return (centred * spread, spread)


def norm_back(gradient, normed, spread):
    first_mean = jnp.mean(gradient, axis=-1, keepdims=True)
    second_mean = jnp.mean(gradient * normed, axis=-1, keepdims=True)
    return spread * (gradient - first_mean - normed * second_mean)


def after(values, *earlier):
    return lax.optimization_barrier((values, earlier))[0]


def swap(value, axis, mask):
    size = lax.axis_size(axis)
    return lax.ppermute(value, axis, [(i, i ^ mask) for i in range(size)])


def bit_order(part):
    bits = list(range((lax.axis_size("ctx") - 1).bit_length()))
    return bits if part == 0 else bits[::-1]


def share(parts):
    found = {}
    for part in (0, 1):
        have = {0: parts[part]}
        for bit in bit_order(part):
            mask = 1 << bit
            have.update({r ^ mask: swap(have[r], "ctx", mask) for r in list(have)})
        found.update({(r, part): have[r] for r in have})
    return found


def total(partial):
    sums = []
    for part in (0, 1):
        have = {r: partial[(r, part)] for r in range(lax.axis_size("ctx"))}
        for bit in bit_order(part)[::-1]:
            mask = 1 << bit
            came = {r ^ mask: swap(have[r].astype(BF16), "ctx", mask) for r in have if r & mask}
            have = {r: have[r].astype(F32) + came[r].astype(F32) for r in came}
        sums.append(have[0])
    return jnp.concatenate(sums, axis=0)


def joined(blocks):
    return jnp.concatenate([blocks[key] for key in sorted(blocks)], axis=0)


def halves(rows):
    middle = rows.shape[0] // 2
    return (rows[:middle], rows[middle:])


def exchange(pieces):
    count = pieces.shape[0]
    here = lax.axis_index("ctx")
    result = pieces
    for mask in range(1, count):
        other = here ^ mask
        came = swap(lax.dynamic_index_in_dim(pieces, other, 0, keepdims=False), "ctx", mask)
        result = lax.dynamic_update_index_in_dim(result, came, other, 0)
    return result


def gather_weight(pieces):
    count, rows, columns = pieces.shape
    block = exchange(pieces).reshape(count * rows, columns)
    half = lax.all_gather(block, "dp", axis=0, tiled=True)
    return jnp.concatenate([half, swap(half, "tp", 1)], axis=1)


def scatter_grad(former, latter):
    width = latter.shape[1] // 2
    theirs = inner(former, latter[:, width:]).astype(BF16)
    came = swap(theirs, "tp", 1)
    ours = inner(former, latter[:, :width])
    summed = (ours + came.astype(F32)).astype(BF16)
    rows = lax.psum_scatter(summed, "dp", scatter_dimension=0, tiled=True)
    count = lax.axis_size("ctx")
    return exchange(rows.reshape(count, rows.shape[0] // count, width))


def rows_of(here, block, size):
    return pl.multiple_of(lax.bitwise_xor(here, block) * size, size)


def attend_forward_kernel(size, blocks, here_ref, qkv_ref, out_ref, log_ref, scores_ref):
    here = here_ref[0]
    scaling = HEAD_DIM ** (-0.5)
    behind = lax.broadcasted_iota(jnp.int32, (size, size), 1) <= lax.broadcasted_iota(
        jnp.int32, (size, size), 0
    )
    for i in range(blocks):
        at = rows_of(here, i, size)
        queries = qkv_ref[pl.ds(at, size), 0:HEAD_DIM]
        highest = jnp.full((size, 1), NEGATIVE, F32)
        for j in range(i + 1):
            keys = qkv_ref[pl.ds(rows_of(here, j, size), size), HEAD_DIM : 2 * HEAD_DIM]
            scores = across(queries, keys) * scaling
            if j == i:
                scores = jnp.where(behind, scores, NEGATIVE)
            scores_ref[:, j * size : (j + 1) * size] = scores
            highest = jnp.maximum(highest, jnp.max(scores, axis=1, keepdims=True))
        row_total = jnp.zeros((size, 1), F32)
        mixed = jnp.zeros((size, HEAD_DIM), F32)
        for j in range(i + 1):
            exponent = jnp.exp(scores_ref[:, j * size : (j + 1) * size] - highest)
            row_total = row_total + jnp.sum(exponent, axis=1, keepdims=True)
            values = qkv_ref[pl.ds(rows_of(here, j, size), size), 2 * HEAD_DIM : 3 * HEAD_DIM]
            mixed = mixed + product(exponent.astype(BF16), values)
        out_ref[pl.ds(at, size), :] = (mixed / row_total).astype(BF16)
        log_total = jnp.broadcast_to(highest + jnp.log(row_total), (size, HEAD_DIM))
        log_ref[0, :, pl.ds(at, size)] = log_total.T[0:8, :]


def attend_backward_kernel(
    size, blocks, here_ref, qkv_ref, grad_ref, out_ref, log_ref, result_ref, key_ref, value_ref
):
    here = here_ref[0]
    scaling = HEAD_DIM ** (-0.5)
    behind = lax.broadcasted_iota(jnp.int32, (size, size), 0) <= lax.broadcasted_iota(
        jnp.int32, (size, size), 1
    )
    for i in range(blocks):
        at = rows_of(here, i, size)
        queries = qkv_ref[pl.ds(at, size), 0:HEAD_DIM]
        grads = grad_ref[pl.ds(at, size), :]
        both = grads.astype(F32) * out_ref[pl.ds(at, size), :].astype(F32)
        centre = jnp.sum(both.T, axis=0, keepdims=True)
        log_total = log_ref[0, 0:1, pl.ds(at, size)]
        query_grad = jnp.zeros((size, HEAD_DIM), F32)
        for j in range(i + 1):
            there = rows_of(here, j, size)
            keys = qkv_ref[pl.ds(there, size), HEAD_DIM : 2 * HEAD_DIM]
            values = qkv_ref[pl.ds(there, size), 2 * HEAD_DIM : 3 * HEAD_DIM]
            weights = jnp.exp(across(keys, queries) * scaling - log_total)
            if j == i:
                weights = jnp.where(behind, weights, 0.0)
            slopes = (weights * (across(values, grads) - centre)).astype(BF16)
            value_term = product(weights.astype(BF16), grads)
            key_term = product(slopes, queries)
            query_grad = query_grad + inner(slopes, keys)
            place = slice(j * size, (j + 1) * size)
            if i == j:
                value_ref[place, :] = value_term
                key_ref[place, :] = key_term
            else:
                value_ref[place, :] += value_term
                key_ref[place, :] += key_term
        result_ref[pl.ds(at, size), 0:HEAD_DIM] = (query_grad * scaling).astype(BF16)
    for j in range(blocks):
        there = rows_of(here, j, size)
        place = slice(j * size, (j + 1) * size)
        result_ref[pl.ds(there, size), HEAD_DIM : 2 * HEAD_DIM] = (
            key_ref[place, :] * scaling
        ).astype(BF16)
        result_ref[pl.ds(there, size), 2 * HEAD_DIM : 3 * HEAD_DIM] = value_ref[place, :].astype(
            BF16
        )


def attend_forward(here, qkv, blocks):
    length, width = qkv.shape
    heads = width // (3 * HEAD_DIM)
    size = length // blocks
    pairs = heads * length * (length + size) // 2
    return pl.pallas_call(
        functools.partial(attend_forward_kernel, size, blocks),
        out_shape=(
            jax.ShapeDtypeStruct((length, heads * HEAD_DIM), BF16),
            jax.ShapeDtypeStruct((heads, 8, length), F32),
        ),
        grid_spec=pltpu.PrefetchScalarGridSpec(
            num_scalar_prefetch=1,
            grid=(heads,),
            in_specs=[pl.BlockSpec((length, 3 * HEAD_DIM), lambda h, _: (0, h))],
            out_specs=(
                pl.BlockSpec((length, HEAD_DIM), lambda h, _: (0, h)),
                pl.BlockSpec((1, 8, length), lambda h, _: (h, 0, 0)),
            ),
            scratch_shapes=[pltpu.VMEM((size, length), F32)],
        ),
        compiler_params=pltpu.CompilerParams(vmem_limit_bytes=40 * 1024 * 1024),
        cost_estimate=pl.CostEstimate(
            flops=pairs * HEAD_DIM * 8,
            bytes_accessed=length * width * 2 * 2,
            transcendentals=pairs,
        ),
        name="attend_forward",
    )(here, qkv)


def attend_backward(here, qkv, grads, mixed, log_total, blocks):
    length, width = qkv.shape
    heads = width // (3 * HEAD_DIM)
    size = length // blocks
    pairs = heads * length * (length + size) // 2
    narrow = pl.BlockSpec((length, HEAD_DIM), lambda h, _: (0, h))
    wide = pl.BlockSpec((length, 3 * HEAD_DIM), lambda h, _: (0, h))
    return pl.pallas_call(
        functools.partial(attend_backward_kernel, size, blocks),
        out_shape=jax.ShapeDtypeStruct((length, width), BF16),
        grid_spec=pltpu.PrefetchScalarGridSpec(
            num_scalar_prefetch=1,
            grid=(heads,),
            in_specs=[
                wide,
                narrow,
                narrow,
                pl.BlockSpec((1, 8, length), lambda h, _: (h, 0, 0)),
            ],
            out_specs=wide,
            scratch_shapes=[pltpu.VMEM((length, HEAD_DIM), F32)] * 2,
        ),
        compiler_params=pltpu.CompilerParams(vmem_limit_bytes=40 * 1024 * 1024),
        cost_estimate=pl.CostEstimate(
            flops=pairs * HEAD_DIM * 20,
            bytes_accessed=length * width * 2 * 4,
            transcendentals=pairs,
        ),
        name="attend_backward",
    )(here, qkv, grads, mixed, log_total)


def body(
    tokens,
    cotangent,
    attention_gain,
    attention_bias,
    feedforward_gain,
    feedforward_bias,
    query_weight,
    query_bias,
    key_weight,
    value_weight,
    value_bias,
    output_weight,
    output_bias,
    up_weight,
    up_bias,
    down_weight,
    down_bias,
):
    _, local_rows, model_width = tokens.shape
    ctx, dp = lax.axis_size("ctx"), lax.axis_size("dp")
    here, core = lax.axis_index("ctx"), lax.axis_index("tp")
    shard = lax.axis_index("dp") * ctx + here
    here_ref = jnp.full((1,), here, jnp.int32)
    thin = query_weight.shape[0]
    heads = query_weight.shape[1] // (HEAD_DIM * ctx)
    hidden = up_weight.shape[1] // ctx
    half_rows = local_rows // 2
    units = [(r, part) for r in range(ctx) for part in (0, 1)]
    place = {key: slice(n * half_rows, (n + 1) * half_rows) for n, key in enumerate(units)}

    small = jnp.stack(
        [attention_gain, attention_bias, feedforward_gain, feedforward_bias, output_bias, down_bias]
    ).astype(F32)
    table = jnp.zeros((6, model_width), F32)
    table = lax.dynamic_update_slice(table, small, (0, shard * thin))
    flat = ("dp", "ctx")
    mask = 1
    while mask < dp * ctx:
        table = table + lax.ppermute(table, flat, [(i, i ^ mask) for i in range(dp * ctx)])
        mask *= 2
    gain_one, shift_one, gain_two, shift_two, output_shift, down_shift = [
        table[n : n + 1] for n in range(6)
    ]

    packed = jnp.stack(
        [w.reshape(thin, ctx, heads, HEAD_DIM) for w in (query_weight, key_weight, value_weight)],
        axis=3,
    ).reshape(thin, ctx, heads * 3 * HEAD_DIM)
    qkv_weight = gather_weight(packed.transpose(1, 0, 2))
    out_weight = gather_weight(
        output_weight.reshape(ctx, heads * HEAD_DIM, thin).transpose(0, 2, 1)
    )
    rise_weight = gather_weight(up_weight.reshape(thin, ctx, hidden).transpose(1, 0, 2))
    fall_weight = gather_weight(down_weight.reshape(ctx, hidden, thin).transpose(0, 2, 1))

    def own_columns(vector):
        return lax.dynamic_index_in_dim(vector.reshape(ctx, -1), here, 0, keepdims=False)

    query_shift = own_columns(query_bias).reshape(heads, HEAD_DIM)
    value_shift = own_columns(value_bias).reshape(heads, HEAD_DIM)
    qkv_shift = jnp.stack([query_shift, jnp.zeros_like(query_shift), value_shift], axis=1)
    shifts = jnp.concatenate([qkv_shift.reshape(-1), own_columns(up_bias)])
    other_shifts = swap(shifts, "tp", 1)
    wide = heads * 3 * HEAD_DIM
    qkv_shift = jnp.concatenate([shifts[:wide], other_shifts[:wide]]).astype(F32)
    rise_shift = jnp.concatenate([shifts[wide:], other_shifts[wide:]]).astype(F32)

    inputs = lax.dynamic_index_in_dim(tokens, core, 0, keepdims=False).astype(F32)
    incoming = lax.dynamic_index_in_dim(cotangent, core, 0, keepdims=False)
    normed_one, spread_one = normalize(inputs)
    input_one = (normed_one * gain_one + shift_one).astype(BF16)
    ones = joined(share(halves(input_one)))
    qkv = (product(ones, qkv_weight) + qkv_shift).astype(BF16)
    later = after(incoming, ones)
    grads_in = joined(share(halves(later)))
    mixed, log_total = attend_forward(here_ref, qkv, ctx)
    branch = total({key: across(mixed[place[key]], out_weight) for key in units})
    residual = inputs + (branch + output_shift)

    normed_two, spread_two = normalize(residual)
    input_two = (normed_two * gain_two + shift_two).astype(BF16)
    hidden_back = product(grads_in, fall_weight)
    twos = share(halves(input_two))
    hid, hid_grad, second = {}, {}, {}
    for key in units:
        pre = product(twos[key], rise_weight) + rise_shift
        cumulative = 0.5 * (1.0 + lax.erf(pre * 0.7071067811865476))
        density = jnp.exp(-0.5 * pre * pre) * 0.3989422804014327
        hid[key] = (pre * cumulative).astype(BF16)
        hid_grad[key] = (hidden_back[place[key]] * (cumulative + pre * density)).astype(BF16)
        second[key] = across(hid_grad[key], rise_weight)
    second_grad = total(second)
    gain_two_sum = jnp.sum(second_grad * normed_two, axis=0)
    bias_two_sum = jnp.sum(second_grad, axis=0)
    wide_incoming = incoming.astype(F32)
    residual_grad = wide_incoming + norm_back(second_grad * gain_two, normed_two, spread_two)
    branch_grad = residual_grad.astype(BF16)
    branch_grads = joined(share(halves(branch_grad)))

    all_hid, all_hid_grad, all_twos = joined(hid), joined(hid_grad), joined(twos)
    fall_grad = scatter_grad(grads_in, all_hid)
    rise_grad = scatter_grad(all_twos, all_hid_grad)
    rise_bias = jnp.sum(all_hid_grad.astype(F32), axis=0)

    mixed_grad = product(branch_grads, out_weight).astype(BF16)
    out_grad = scatter_grad(branch_grads, mixed)
    late_hid = after(all_hid, branch_grads)
    block_out = residual + (
        total({key: across(late_hid[place[key]], fall_weight) for key in units}) + down_shift
    )
    own_out = block_out.astype(BF16)
    qkv_grads = attend_backward(here_ref, qkv, mixed_grad, mixed, log_total, ctx)
    first_grad = total({key: across(qkv_grads[place[key]], qkv_weight) for key in units})
    qkv_grad = scatter_grad(ones, qkv_grads)
    qkv_bias = jnp.sum(qkv_grads.astype(F32), axis=0)
    gain_one_sum = jnp.sum(first_grad * normed_one, axis=0)
    bias_one_sum = jnp.sum(first_grad, axis=0)
    token_grad = residual_grad + norm_back(first_grad * gain_one, normed_one, spread_one)
    own_grad = token_grad.astype(BF16)

    def both_sequences(own):
        other = swap(own, "tp", 1)
        first = core == 0
        return jnp.stack([jnp.where(first, own, other), jnp.where(first, other, own)])

    def spread_columns(vector):
        own, other = jnp.split(vector, 2)
        whole = jnp.zeros((2, ctx, own.shape[0]), F32)
        whole = lax.dynamic_update_slice(whole, own[None, None], (core, here, 0))
        return lax.dynamic_update_slice(whole, other[None, None], (1 - core, here, 0))

    features = jnp.stack(
        [
            gain_one_sum,
            bias_one_sum,
            gain_two_sum,
            bias_two_sum,
            jnp.sum(branch_grad.astype(F32), axis=0),
            jnp.sum(wide_incoming, axis=0),
        ]
    )
    features, qkv_bias, rise_bias = lax.psum(
        (features, spread_columns(qkv_bias), spread_columns(rise_bias)), ("dp", "ctx", "tp")
    )
    features = lax.dynamic_slice(features, (0, shard * thin), (6, thin))
    qkv_bias = lax.dynamic_index_in_dim(qkv_bias, core, 0, keepdims=False)
    qkv_bias = qkv_bias.reshape(ctx * heads, 3, HEAD_DIM)
    rise_bias = lax.dynamic_index_in_dim(rise_bias, core, 0, keepdims=False).reshape(-1)

    qkv_grad = qkv_grad.reshape(ctx, thin, heads, 3, HEAD_DIM).transpose(3, 1, 0, 2, 4)
    qkv_grad = qkv_grad.reshape(3, thin, ctx * heads * HEAD_DIM).astype(F32)
    return (
        both_sequences(own_out),
        both_sequences(own_grad),
        features[0],
        features[1],
        features[2],
        features[3],
        qkv_grad[0],
        qkv_bias[:, 0].reshape(-1),
        qkv_grad[1],
        qkv_grad[2],
        qkv_bias[:, 2].reshape(-1),
        out_grad.transpose(0, 2, 1).reshape(-1, thin).astype(F32),
        features[4],
        rise_grad.transpose(1, 0, 2).reshape(thin, -1).astype(F32),
        rise_bias,
        fall_grad.transpose(0, 2, 1).reshape(-1, thin).astype(F32),
        features[5],
    )


def solution(mesh):
    placed = (
        P("dp", "ctx", None),
        P("dp", "ctx", None),
        P(("dp", "ctx")),
        P(("dp", "ctx")),
        P(("dp", "ctx")),
        P(("dp", "ctx")),
        P(("dp", "ctx"), "tp"),
        P("tp"),
        P(("dp", "ctx"), "tp"),
        P(("dp", "ctx"), "tp"),
        P("tp"),
        P("tp", ("dp", "ctx")),
        P(("dp", "ctx")),
        P(("dp", "ctx"), "tp"),
        P("tp"),
        P("tp", ("dp", "ctx")),
        P(("dp", "ctx")),
    )
    return jax.shard_map(
        body,
        mesh=mesh,
        in_specs=placed,
        out_specs=(
            P("dp", "ctx", None),
            P("dp", "ctx", None),
            P(("dp", "ctx")),
            P(("dp", "ctx")),
            P(("dp", "ctx")),
            P(("dp", "ctx")),
            P(("dp", "ctx"), "tp"),
            P("tp"),
            P(("dp", "ctx"), "tp"),
            P(("dp", "ctx"), "tp"),
            P("tp"),
            P("tp", ("dp", "ctx")),
            P(("dp", "ctx")),
            P(("dp", "ctx"), "tp"),
            P("tp"),
            P("tp", ("dp", "ctx")),
            P(("dp", "ctx")),
        ),
        check_vma=False,
    )
```

time: 5420 us -> 1130 us (0.21)
  waiting for transfers between devices: 4220 us -> 490 us
  blocking collectives: 376 us -> 0 us
  matrix products: 601 us -> 315 us
  other arithmetic: 148 us -> 52.4 us
  starting transfers between devices: 3.09 us -> 86.8 us
  local copies, waits for them, and re-layouts: 41 us -> 112 us
    reduce_scatter x10 -> x4, waiting for transfers between devices: 2410 us -> 130 us  [scatter_grad(): rows = lax.psum_scatter(summed, 'dp', scatter_dimension=0, tiled=True)]
    all_gather x22 -> x4, waiting for transfers between devices: 1800 us -> 0.01 us  [gather_weight(): half = lax.all_gather(block, 'dp', axis=0, tiled=True)]
    all_gather x10 -> x0, blocking collectives: 376 us -> none  [the longest x3 111 us: fetch(): lax.all_gather(row_shards[2], ('dp', 'ctx'), axis=0, tiled=True)]
    ppermute x0 -> x87, waiting for transfers between devices: none -> 360 us  [the longest x83 346 us: swap(): return lax.ppermute(value, axis, [(i, i ^ mask) for i in range(size)])]
    dot_general x24 -> x11, matrix products: 328 us -> 95 us  [product(): return jnp.dot(former, latter, preferred_element_type=F32)]
    ppermute x0 -> x87, starting transfers between devices: none -> 85.9 us  [the longest x83 78.2 us: swap(): return lax.ppermute(value, axis, [(i, i ^ mask) for i in range(size)])]
    dot_general x12 -> x8, matrix products: 146 us -> 88 us  [inner(): lax.dot_general(former, latter, (((0,), (0,)), ((), ())), preferred_eleme...]
    dot_general x12 -> x32, matrix products: 126 us -> 132 us  [across(): lax.dot_general(former, latter, (((1,), (1,)), ((), ())), preferred_eleme...]
  transfers between devices with their start and end apart: 37 -> 96, of which waited for: 30 -> 46; matrix products, arithmetic and copies ran while one was open for 13% -> 40% of each run, Pallas kernels for 0% -> 5%
where the time goes in v1:
time: 1130 us; the launch traced here: 1120 us
  waiting for transfers between devices  490 us (43%)
  matrix products  315 us (28%)
  local copies, waits for them, and re-layouts  112 us (10%)
  starting transfers between devices  86.8 us (8%)
  other arithmetic  52.4 us (5%)
  Pallas kernels  52.2 us (5%)
  between operations  15.9 us (1%)
    ppermute x83, waiting for transfers between devices, swap(): return lax.ppermute(value, axis, [(i, i ^ mask) for i in range(size)])  346 us
    dot_general x32, matrix products, across(): lax.dot_general(former, latter, (((1,), (1,)), ((), ())), preferred_eleme...  132 us
    reduce_scatter x4, waiting for transfers between devices, scatter_grad(): rows = lax.psum_scatter(summed, 'dp', scatter_dimension=0, tiled=True)  130 us
    dot_general x11, matrix products, product(): return jnp.dot(former, latter, preferred_element_type=F32)  95 us
    dot_general x8, matrix products, inner(): lax.dot_general(former, latter, (((0,), (0,)), ((), ())), preferred_eleme...  88 us
    ppermute x83, starting transfers between devices, swap(): return lax.ppermute(value, axis, [(i, i ^ mask) for i in range(size)])  78.2 us
    unnamed x201, local copies, waits for them, and re-layouts  56 us
    pallas_call x1, Pallas kernels, attend_backward(): pl.pallas_call(functools.partial(attend_backward_kernel, size, blocks), o...  31.9 us
  transfers between devices with their start and end apart: 96, of which 46 were waited for; matrix products, arithmetic and copies ran while one was open for 40% of the time, Pallas kernels for 5%

profile of v1, /device:TPU:0, one launch (start us, length us, event | category | flops | bytes accessed | tf_op | source)
XLA Modules:
  0.0 1124.8 jit_solution(5544721006719595825)
XLA Ops:
  90.8 12.5 %collective-permute-done.4 = bf16[256,2048]{1,0:T(8,128)(2,1)} collective-permute-done((bf16[256,2048]{1,0:T(8,128)(2,1)}, bf16[256,2048]{1,0:T(8,128)(2,1)}, u32[]{:S(2)}, u32[]{:S(2)}) %collective-permute-start.4) | collective-permute-done | bytes 1048608 | tf_op jit(solution)/shard_map/ppermute | solution.py:48
  103.2 22.5 %collective-permute-done.25 = bf16[128,1024]{1,0:T(8,128)(2,1)} collective-permute-done((bf16[128,1024]{1,0:T(8,128)(2,1)}, bf16[128,1024]{1,0:T(8,128)(2,1)}, u32[]{:S(2)}, u32[]{:S(2)}) %collective-permute-start.25) | collective-permute-done | bytes 262176 | tf_op jit(solution)/shard_map/ppermute | solution.py:48
  161.3 11.7 %collective-permute-done.38 = bf16[256,2048]{1,0:T(8,128)(2,1)} collective-permute-done((bf16[256,2048]{1,0:T(8,128)(2,1)}, bf16[256,2048]{1,0:T(8,128)(2,1)}, u32[]{:S(2)}, u32[]{:S(2)}) %collective-permute-start.38) | collective-permute-done | bytes 1048608 | tf_op jit(solution)/shard_map/ppermute | solution.py:48
  177.9 18.8 %collective-permute-done.36 = bf16[256,2048]{1,0:T(8,128)(2,1)} collective-permute-done((bf16[256,2048]{1,0:T(8,128)(2,1)}, bf16[256,2048]{1,0:T(8,128)(2,1)}, u32[]{:S(2)}, u32[]{:S(2)}) %collective-permute-start.36) | collective-permute-done | bytes 1048608 | tf_op jit(solution)/shard_map/ppermute | solution.py:48
  205.5 14.2 %add_convert_fusion.qkv_ref = bf16[2048,1536]{1,0:T(8,128)(2,1)S(1)} fusion(bf16[2048,2048]{1,0:T(8,128)(2,1)S(1)} %bitcast.326, bf16[2048,1536]{1,0:T(8,128)(2,1)S(1)} %constant_dynamic-update-slice_fusion.7, f32[1536]{0:T(1024)S(1)} %maximum_convert_fusion), kind=kOutput, calls=%fused_computation.2 | convolution fusion | flops 12891193344 | bytes 20977664 | tf_op jit(solution)/shard_map/dot_general | solution.py:18
  219.7 20.4 %attend_forward.1 = (bf16[2048,512]{1,0:T(8,128)(2,1)S(1)}, f32[4,8,2048]{2,1,0:T(8,128)S(1)}) custom-call(s32[1]{0:T(128)} %bitcast.1.here_ref, bf16[2048,1536]{1,0:T(8,128)(2,1)S(1)} %add_convert_fusion.qkv_ref), custom_call_target="tpu_custom_call" | custom-call | flops 10737418240 | bytes 12582912 | tf_op jit(solution)/shard_map/attend_forward/pallas_call | solution.py:201
  252.5 15.7 %collective-permute-done.20 = bf16[256,2048]{1,0:T(8,128)(2,1)} collective-permute-done((bf16[256,2048]{1,0:T(8,128)(2,1)}, bf16[256,2048]{1,0:T(8,128)(2,1)}, u32[]{:S(2)}, u32[]{:S(2)}) %collective-permute-start.20) | collective-permute-done | bytes 1048608 | tf_op jit(solution)/shard_map/ppermute | solution.py:48
  299.6 14.4 %collective-permute-done.22 = bf16[256,2048]{1,0:T(8,128)(2,1)} collective-permute-done((bf16[256,2048]{1,0:T(8,128)(2,1)}, bf16[256,2048]{1,0:T(8,128)(2,1)}, u32[]{:S(2)}, u32[]{:S(2)}) %collective-permute-start.22) | collective-permute-done | bytes 1048608 | tf_op jit(solution)/shard_map/ppermute | solution.py:48
  330.1 24.3 %fusion.167 = f32[2048,2048]{1,0:T(8,128)} fusion(bf16[2048,2048]{1,0:T(8,128)(2,1)} %constant_dynamic-update-slice_fusion.13, bf16[2048,2048]{1,0:T(8,128)(2,1)} %constant_dynamic-update-slice_fusion.20), kind=kOutput, calls=%fused_computation.372 | convolution fusion | flops 17179869184 | bytes 33554432 | tf_op jit(solution)/shard_map/dot_general | solution.py:18
  356.9 9.1 constant_dynamic-update-slice_fusion.43
  417.3 20.2 %collective-permute-done.33 = bf16[256,2048]{1,0:T(8,128)(2,1)S(1)} collective-permute-done((bf16[256,2048]{1,0:T(8,128)(2,1)}, bf16[256,2048]{1,0:T(8,128)(2,1)S(1)}, u32[]{:S(2)}, u32[]{:S(2)}) %collective-permute-start.33) | collective-permute-done | bytes 1048608 | tf_op jit(solution)/shard_map/ppermute | solution.py:48
  456.5 9.0 convolution_convert_fusion.15
  474.5 17.5 %collective-permute-done.49 = bf16[256,2048]{1,0:T(8,128)(2,1)} collective-permute-done((bf16[256,2048]{1,0:T(8,128)(2,1)}, bf16[256,2048]{1,0:T(8,128)(2,1)}, u32[]{:S(2)}, u32[]{:S(2)}) %collective-permute-start.49) | collective-permute-done | bytes 1048608 | tf_op jit(solution)/shard_map/ppermute | solution.py:48
  497.8 14.3 %fusion.30 = bf16[2048,1024]{1,0:T(8,128)(2,1)} fusion(bf16[2048,2048]{1,0:T(8,128)(2,1)} %constant_dynamic-update-slice_fusion.13, bf16[2048,2048]{1,0:T(8,128)(2,1)} %get-tuple-element.23), kind=kOutput, calls=%fused_computation.50 | convolution fusion | flops 8592031744 | bytes 16777216 | tf_op jit(solution)/shard_map/dot_general | solution.py:22
  542.3 10.8 collective-permute-done.51
  556.2 19.3 %collective-permute-done.52 = bf16[256,2048]{1,0:T(8,128)(2,1)} collective-permute-done((bf16[256,2048]{1,0:T(8,128)(2,1)}, bf16[256,2048]{1,0:T(8,128)(2,1)}, u32[]{:S(2)}, u32[]{:S(2)}) %collective-permute-start.52) | collective-permute-done | bytes 1048608 | tf_op jit(solution)/shard_map/ppermute | solution.py:48
  579.5 11.4 %collective-permute-done.55 = bf16[256,2048]{1,0:T(8,128)(2,1)S(1)} collective-permute-done((bf16[256,2048]{1,0:T(8,128)(2,1)}, bf16[256,2048]{1,0:T(8,128)(2,1)S(1)}, u32[]{:S(2)}, u32[]{:S(2)}) %collective-permute-start.55) | collective-permute-done | bytes 1048608 | tf_op jit(solution)/shard_map/ppermute | solution.py:48
  596.8 31.9 %attend_backward.1 = bf16[2048,1536]{1,0:T(8,128)(2,1)S(1)} custom-call(s32[1]{0:T(128)} %bitcast.1.here_ref, bf16[2048,1536]{1,0:T(8,128)(2,1)} %copy-done.1, bf16[2048,512]{1,0:T(8,128)(2,1)S(1)} %convolution_convert_fusion.1.grad_ref, bf16[2048,512]{1,0:T(8,128)(2,1)S(1)} %get-tuple-element.21.out_ref, f32[4,8,2048]{2,1,0:T(8,128)S(1)} %get-tuple-element.24.log_ref), custom_call_target="tpu_custom_call" | custom-call | flops 26843545600 | bytes 25165824 | tf_op jit(solution)/shard_map/attend_backward/pallas_call | solution.py:234
  644.9 16.6 %collective-permute-done.65 = bf16[256,2048]{1,0:T(8,128)(2,1)S(1)} collective-permute-done((bf16[256,2048]{1,0:T(8,128)(2,1)S(1)}, bf16[256,2048]{1,0:T(8,128)(2,1)S(1)}, u32[]{:S(2)}, u32[]{:S(2)}) %collective-permute-start.65) | collective-permute-done | bytes 1048608 | tf_op jit(solution)/shard_map/ppermute | solution.py:48
  665.2 23.8 %collective-permute-done.68 = bf16[256,2048]{1,0:T(8,128)(2,1)S(1)} collective-permute-done((bf16[256,2048]{1,0:T(8,128)(2,1)S(1)}, bf16[256,2048]{1,0:T(8,128)(2,1)S(1)}, u32[]{:S(2)}, u32[]{:S(2)}) %collective-permute-start.68) | collective-permute-done | bytes 1048608 | tf_op jit(solution)/shard_map/ppermute | solution.py:48
  694.4 11.9 %collective-permute-done.66 = bf16[256,2048]{1,0:T(8,128)(2,1)} collective-permute-done((bf16[256,2048]{1,0:T(8,128)(2,1)}, bf16[256,2048]{1,0:T(8,128)(2,1)}, u32[]{:S(2)}, u32[]{:S(2)}) %collective-permute-start.66) | collective-permute-done | bytes 1048608 | tf_op jit(solution)/shard_map/ppermute | solution.py:48
  728.7 15.3 %add_convert_fusion.1 = bf16[2048,1024]{1,0:T(8,128)(2,1)} fusion(bf16[2048,1024]{1,0:T(8,128)(2,1)} %collective-permute-done.83, bf16[2048,2048]{1,0:T(8,128)(2,1)} %constant_dynamic-update-slice_fusion.13, bf16[2048,2048]{1,0:T(8,128)(2,1)} %get-tuple-element.23), kind=kOutput, calls=%fused_computation.3 | convolution fusion | flops 8596226048 | bytes 20971520 | tf_op jit(solution)/shard_map/dot_general | solution.py:22
  744.3 12.7 %fusion.27 = bf16[2048,1024]{1,0:T(8,128)(2,1)S(1)} fusion(bf16[2048,2048]{1,0:T(8,128)(2,1)} %constant_dynamic-update-slice_fusion.29, bf16[2048,2048]{1,0:T(8,128)(2,1)} %copy-done.19), kind=kOutput, calls=%fused_computation.49 | convolution fusion | flops 8592031744 | bytes 16777216 | tf_op jit(solution)/shard_map/dot_general | solution.py:22
  764.3 14.0 %add_convert_fusion.2 = bf16[2048,1024]{1,0:T(8,128)(2,1)} fusion(bf16[2048,1024]{1,0:T(8,128)(2,1)S(1)} %collective-permute-done.79, bf16[2048,2048]{1,0:T(8,128)(2,1)} %constant_dynamic-update-slice_fusion.29, bf16[2048,2048]{1,0:T(8,128)(2,1)} %copy-done.19), kind=kOutput, calls=%fused_computation.4 | convolution fusion | flops 8596226048 | bytes 20971520 | tf_op jit(solution)/shard_map/dot_general | solution.py:22
  778.3 11.8 %convolution_convert_fusion = bf16[2048,768]{1,0:T(8,128)(2,1)} fusion(bf16[2048,2048]{1,0:T(8,128)(2,1)} %constant_dynamic-update-slice_fusion, bf16[2048,1536]{1,0:T(8,128)(2,1)} %copy-done), kind=kOutput, calls=%fused_computation.53 | convolution fusion | flops 6444023808 | bytes 14680064 | tf_op jit(solution)/shard_map/dot_general | solution.py:22
  808.5 14.1 %collective-permute-done.58 = bf16[256,2048]{1,0:T(8,128)(2,1)S(1)} collective-permute-done((bf16[256,2048]{1,0:T(8,128)(2,1)S(1)}, bf16[256,2048]{1,0:T(8,128)(2,1)S(1)}, u32[]{:S(2)}, u32[]{:S(2)}) %collective-permute-start.58) | collective-permute-done | bytes 1048608 | tf_op jit(solution)/shard_map/ppermute | solution.py:48
  845.6 11.3 %collective-permute-done.59 = bf16[256,2048]{1,0:T(8,128)(2,1)} collective-permute-done((bf16[256,2048]{1,0:T(8,128)(2,1)}, bf16[256,2048]{1,0:T(8,128)(2,1)}, u32[]{:S(2)}, u32[]{:S(2)}) %collective-permute-start.59) | collective-permute-done | bytes 1048608 | tf_op jit(solution)/shard_map/ppermute | solution.py:48
  863.6 14.1 %collective-permute-done.60 = bf16[256,2048]{1,0:T(8,128)(2,1)S(1)} collective-permute-done((bf16[256,2048]{1,0:T(8,128)(2,1)}, bf16[256,2048]{1,0:T(8,128)(2,1)S(1)}, u32[]{:S(2)}, u32[]{:S(2)}) %collective-permute-start.60) | collective-permute-done | bytes 1048608 | tf_op jit(solution)/shard_map/ppermute | solution.py:48
  886.8 10.0 add_convert_fusion.3
  931.8 24.3 %reduce-scatter.11.cloned.1.call-done = bf16[512,1024]{1,0:T(8,128)(2,1)} async-done(((bf16[2048,1024]{1,0:T(8,128)(2,1)}), bf16[512,1024]{1,0:T(8,128)(2,1)}) %reduce-scatter.11.cloned.1.call-update) | async-done | bytes 1048592 | tf_op jit(solution)/shard_map/reduce_scatter | solution.py:112
  964.0 71.7 %reduce-scatter.9.cloned.1.call-done = bf16[512,1024]{1,0:T(8,128)(2,1)} async-done(((bf16[2048,1024]{1,0:T(8,128)(2,1)}), bf16[512,1024]{1,0:T(8,128)(2,1)}) %reduce-scatter.9.cloned.1.call-update) | async-done | bytes 1048592 | tf_op jit(solution)/shard_map/reduce_scatter | solution.py:112
  1065.2 33.7 %reduce-scatter.5.cloned.1.call-done = bf16[512,768]{1,0:T(8,128)(2,1)} async-done(((bf16[2048,768]{1,0:T(8,128)(2,1)}), bf16[512,768]{1,0:T(8,128)(2,1)}) %reduce-scatter.5.cloned.1.call-update) | async-done | bytes 786448 | tf_op jit(solution)/shard_map/reduce_scatter | solution.py:112
  (568 shorter events, 525.5 us)
Async XLA Ops:
  7.2 132.5 %all-gather.7.cloned.1.call-start = ((), (), s32[]{:S(2)}) async-start(), calls=%async_computation.5 | async-start | bytes 1310720 | tf_op jit(solution)/shard_map/all_gather | solution.py:102
  19.5 123.5 %all-gather.5.cloned.1.call-start = ((), (), s32[]{:S(2)}) async-start(), calls=%async_computation.4 | async-start | bytes 3932160 | tf_op jit(solution)/shard_map/all_gather | solution.py:102
  33.3 214.1 %all-gather.11.cloned.1.call-start = ((), (), s32[]{:S(2)}) async-start(), calls=%async_computation.7 | async-start | bytes 5242880 | tf_op jit(solution)/shard_map/all_gather | solution.py:102
  47.6 233.7 %all-gather.9.cloned.1.call-start = ((), (), s32[]{:S(2)}) async-start(), calls=%async_computation.6 | async-start | bytes 5242880 | tf_op jit(solution)/shard_map/all_gather | solution.py:102
  78.5 48.6 %collective-permute-start.7 = (bf16[256,2048]{1,0:T(8,128)(2,1)}, bf16[256,2048]{1,0:T(8,128)(2,1)}, u32[]{:S(2)}, u32[]{:S(2)}) collective-permute-start(bf16[256,2048]{1,0:T(8,128)(2,1)} %get-tuple-element.105), channel_id=1, source_target_pairs={{0,4},{2,6},{4,0},{6,2},{1,5},{3,7},{5,1},{7,3},{8,12},{10,14},{12... | collective-permute-start | bytes 3145736 | tf_op jit(solution)/shard_map/ppermute | solution.py:48
  78.6 52.1 %collective-permute-start.5 = (bf16[256,2048]{1,0:T(8,128)(2,1)}, bf16[256,2048]{1,0:T(8,128)(2,1)}, u32[]{:S(2)}, u32[]{:S(2)}) collective-permute-start(bf16[256,2048]{1,0:T(8,128)(2,1)} %get-tuple-element.105), channel_id=1, source_target_pairs={{0,2},{2,0},{4,6},{6,4},{1,3},{3,1},{5,7},{7,5},{8,10},{10,8},{12,... | collective-permute-start | bytes 3145736 | tf_op jit(solution)/shard_map/ppermute | solution.py:48
  80.8 54.2 %collective-permute-start.6 = (bf16[256,2048]{1,0:T(8,128)(2,1)}, bf16[256,2048]{1,0:T(8,128)(2,1)}, u32[]{:S(2)}, u32[]{:S(2)}) collective-permute-start(bf16[256,2048]{1,0:T(8,128)(2,1)} %get-tuple-element.106), channel_id=1, source_target_pairs={{0,4},{2,6},{4,0},{6,2},{1,5},{3,7},{5,1},{7,3},{8,12},{10,14},{12... | collective-permute-start | bytes 3145736 | tf_op jit(solution)/shard_map/ppermute | solution.py:48
  143.0 60.0 %collective-permute-start.13 = (bf16[2048,768]{1,0:T(8,128)(2,1)}, bf16[2048,768]{1,0:T(8,128)(2,1)}, u32[]{:S(2)}, u32[]{:S(2)}) collective-permute-start(bf16[2048,768]{1,0:T(8,128)(2,1)} %all-gather.5.cloned.1.call-done), channel_id=1, source_target_pairs={{0,1},{1,0},{2,3},{3,2},{4,5},{5,4},{6,7},{7,6},{8,9},{9,8},{10,11... | collective-permute-start | bytes 9437192 | tf_op jit(solution)/shard_map/ppermute | solution.py:48
  152.1 44.6 %collective-permute-start.36 = (bf16[256,2048]{1,0:T(8,128)(2,1)}, bf16[256,2048]{1,0:T(8,128)(2,1)}, u32[]{:S(2)}, u32[]{:S(2)}) collective-permute-start(bf16[256,2048]{1,0:T(8,128)(2,1)} %get-tuple-element.101), channel_id=1, source_target_pairs={{0,2},{2,0},{4,6},{6,4},{1,3},{3,1},{5,7},{7,5},{8,10},{10,8},{12,... | collective-permute-start | bytes 3145736 | tf_op jit(solution)/shard_map/ppermute | solution.py:48
  155.2 749.4 %all-reduce.3.cloned.1.call-start = ((), (), s32[]{:S(2)}) async-start(), calls=%async_computation.12 | async-start | bytes 245760 | tf_op jit(solution)/shard_map/psum | solution.py:401
  173.0 73.3 %collective-permute-start.40 = (bf16[256,2048]{1,0:T(8,128)(2,1)}, bf16[256,2048]{1,0:T(8,128)(2,1)S(1)}, u32[]{:S(2)}, u32[]{:S(2)}) collective-permute-start(bf16[256,2048]{1,0:T(8,128)(2,1)} %collective-permute-done.38), channel_id=1, source_target_pairs={{0,2},{2,0},{4,6},{6,4},{1,3},{3,1},{5,7},{7,5},{8,10},{10,8},{12,... | collective-permute-start | bytes 3145736 | tf_op jit(solution)/shard_map/ppermute | solution.py:48
  174.2 68.4 %collective-permute-start.39 = (bf16[256,2048]{1,0:T(8,128)(2,1)}, bf16[256,2048]{1,0:T(8,128)(2,1)S(1)}, u32[]{:S(2)}, u32[]{:S(2)}) collective-permute-start(bf16[256,2048]{1,0:T(8,128)(2,1)} %collective-permute-done.35), channel_id=1, source_target_pairs={{0,4},{2,6},{4,0},{6,2},{1,5},{3,7},{5,1},{7,3},{8,12},{10,14},{12... | collective-permute-start | bytes 3145736 | tf_op jit(solution)/shard_map/ppermute | solution.py:48
  247.4 76.8 %collective-permute-start.44 = (bf16[2048,1024]{1,0:T(8,128)(2,1)}, bf16[2048,1024]{1,0:T(8,128)(2,1)}, u32[]{:S(2)}, u32[]{:S(2)}) collective-permute-start(bf16[2048,1024]{1,0:T(8,128)(2,1)} %all-gather.11.cloned.1.call-done), channel_id=1, source_target_pairs={{0,1},{1,0},{2,3},{3,2},{4,5},{5,4},{6,7},{7,6},{8,9},{9,8},{10,11... | collective-permute-start | bytes 12582920 | tf_op jit(solution)/shard_map/ppermute | solution.py:48
  290.6 63.8 %collective-permute-start.28 = (bf16[2048,1024]{1,0:T(8,128)(2,1)S(1)}, bf16[2048,1024]{1,0:T(8,128)(2,1)S(1)}, u32[]{:S(2)}, u32[]{:S(2)}) collective-permute-start(bf16[2048,1024]{1,0:T(8,128)(2,1)S(1)} %copy-done.22), channel_id=1, source_target_pairs={{0,1},{1,0},{2,3},{3,2},{4,5},{5,4},{6,7},{7,6},{8,9},{9,8},{10,11... | collective-permute-start | bytes 12582920 | tf_op jit(solution)/shard_map/ppermute | solution.py:48
  321.3 57.1 %collective-permute-start.30 = (bf16[256,2048]{1,0:T(8,128)(2,1)S(1)}, bf16[256,2048]{1,0:T(8,128)(2,1)S(1)}, u32[]{:S(2)}, u32[]{:S(2)}) collective-permute-start(bf16[256,2048]{1,0:T(8,128)(2,1)S(1)} %get-tuple-element.103), channel_id=1, source_target_pairs={{0,2},{2,0},{4,6},{6,4},{1,3},{3,1},{5,7},{7,5},{8,10},{10,8},{12,... | collective-permute-start | bytes 3145736 | tf_op jit(solution)/shard_map/ppermute | solution.py:48
  322.2 83.6 %collective-permute-start.32 = (bf16[256,2048]{1,0:T(8,128)(2,1)S(1)}, bf16[256,2048]{1,0:T(8,128)(2,1)S(1)}, u32[]{:S(2)}, u32[]{:S(2)}) collective-permute-start(bf16[256,2048]{1,0:T(8,128)(2,1)S(1)} %get-tuple-element.103), channel_id=1, source_target_pairs={{0,4},{2,6},{4,0},{6,2},{1,5},{3,7},{5,1},{7,3},{8,12},{10,14},{12... | collective-permute-start | bytes 3145736 | tf_op jit(solution)/shard_map/ppermute | solution.py:48
  322.9 49.3 %collective-permute-start.29 = (bf16[256,2048]{1,0:T(8,128)(2,1)S(1)}, bf16[256,2048]{1,0:T(8,128)(2,1)}, u32[]{:S(2)}, u32[]{:S(2)}) collective-permute-start(bf16[256,2048]{1,0:T(8,128)(2,1)S(1)} %get-tuple-element.104), channel_id=1, source_target_pairs={{0,2},{2,0},{4,6},{6,4},{1,3},{3,1},{5,7},{7,5},{8,10},{10,8},{12,... | collective-permute-start | bytes 3145736 | tf_op jit(solution)/shard_map/ppermute | solution.py:48
  324.2 60.4 %collective-permute-start.31 = (bf16[256,2048]{1,0:T(8,128)(2,1)S(1)}, bf16[256,2048]{1,0:T(8,128)(2,1)S(1)}, u32[]{:S(2)}, u32[]{:S(2)}) collective-permute-start(bf16[256,2048]{1,0:T(8,128)(2,1)S(1)} %get-tuple-element.104), channel_id=1, source_target_pairs={{0,4},{2,6},{4,0},{6,2},{1,5},{3,7},{5,1},{7,3},{8,12},{10,14},{12... | collective-permute-start | bytes 3145736 | tf_op jit(solution)/shard_map/ppermute | solution.py:48
  396.8 115.2 %collective-permute-start.45 = (bf16[256,2048]{1,0:T(8,128)(2,1)}, bf16[256,2048]{1,0:T(8,128)(2,1)}, u32[]{:S(2)}, u32[]{:S(2)}) collective-permute-start(bf16[256,2048]{1,0:T(8,128)(2,1)} %convolution_convert_fusion.18), channel_id=1, source_target_pairs={{0,4},{2,6},{4,0},{6,2},{1,5},{3,7},{5,1},{7,3},{8,12},{10,14},{12... | collective-permute-start | bytes 3145736 | tf_op jit(solution)/shard_map/ppermute | solution.py:48
  403.7 113.2 %collective-permute-start.48 = (bf16[256,2048]{1,0:T(8,128)(2,1)}, bf16[256,2048]{1,0:T(8,128)(2,1)}, u32[]{:S(2)}, u32[]{:S(2)}) collective-permute-start(bf16[256,2048]{1,0:T(8,128)(2,1)} %convolution_convert_fusion.16), channel_id=1, source_target_pairs={{0,2},{2,0},{4,6},{6,4},{1,3},{3,1},{5,7},{7,5},{8,10},{10,8},{12,... | collective-permute-start | bytes 3145736 | tf_op jit(solution)/shard_map/ppermute | solution.py:48
  405.8 44.9 %collective-permute-start.34 = (bf16[256,2048]{1,0:T(8,128)(2,1)S(1)}, bf16[256,2048]{1,0:T(8,128)(2,1)S(1)}, u32[]{:S(2)}, u32[]{:S(2)}) collective-permute-start(bf16[256,2048]{1,0:T(8,128)(2,1)S(1)} %collective-permute-done.32), channel_id=1, source_target_pairs={{0,2},{2,0},{4,6},{6,4},{1,3},{3,1},{5,7},{7,5},{8,10},{10,8},{12,... | collective-permute-start | bytes 3145736 | tf_op jit(solution)/shard_map/ppermute | solution.py:48
  537.5 191.2 %collective-permute-start.83 = (bf16[2048,1024]{1,0:T(8,128)(2,1)}, bf16[2048,1024]{1,0:T(8,128)(2,1)}, u32[]{:S(2)}, u32[]{:S(2)}) collective-permute-start(bf16[2048,1024]{1,0:T(8,128)(2,1)} %fusion.30), channel_id=1, source_target_pairs={{0,1},{1,0},{2,3},{3,2},{4,5},{5,4},{6,7},{7,6},{8,9},{9,8},{10,11... | collective-permute-start | bytes 12582920 | tf_op jit(solution)/shard_map/ppermute | solution.py:48
  639.3 55.0 %collective-permute-start.64 = (bf16[256,2048]{1,0:T(8,128)(2,1)}, bf16[256,2048]{1,0:T(8,128)(2,1)}, u32[]{:S(2)}, u32[]{:S(2)}) collective-permute-start(bf16[256,2048]{1,0:T(8,128)(2,1)} %convolution_convert_fusion.9), channel_id=1, source_target_pairs={{0,4},{2,6},{4,0},{6,2},{1,5},{3,7},{5,1},{7,3},{8,12},{10,14},{12... | collective-permute-start | bytes 3145736 | tf_op jit(solution)/shard_map/ppermute | solution.py:48
  640.3 71.7 %collective-permute-start.67 = (bf16[256,2048]{1,0:T(8,128)(2,1)}, bf16[256,2048]{1,0:T(8,128)(2,1)}, u32[]{:S(2)}, u32[]{:S(2)}) collective-permute-start(bf16[256,2048]{1,0:T(8,128)(2,1)} %convolution_convert_fusion.7), channel_id=1, source_target_pairs={{0,2},{2,0},{4,6},{6,4},{1,3},{3,1},{5,7},{7,5},{8,10},{10,8},{12,... | collective-permute-start | bytes 3145736 | tf_op jit(solution)/shard_map/ppermute | solution.py:48
  641.0 48.0 %collective-permute-start.68 = (bf16[256,2048]{1,0:T(8,128)(2,1)S(1)}, bf16[256,2048]{1,0:T(8,128)(2,1)S(1)}, u32[]{:S(2)}, u32[]{:S(2)}) collective-permute-start(bf16[256,2048]{1,0:T(8,128)(2,1)S(1)} %convolution_convert_fusion.6), channel_id=1, source_target_pairs={{0,2},{2,0},{4,6},{6,4},{1,3},{3,1},{5,7},{7,5},{8,10},{10,8},{12,... | collective-permute-start | bytes 3145736 | tf_op jit(solution)/shard_map/ppermute | solution.py:48
  721.3 185.3 %reduce-scatter.7.cloned.1.call-start = ((), (), s32[]{:S(2)}) async-start(), calls=%async_computation.9 | async-start | bytes 1310720 | tf_op jit(solution)/shard_map/reduce_scatter | solution.py:112
  728.7 227.5 %reduce-scatter.11.cloned.1.call-start = ((), (), s32[]{:S(2)}) async-start(), calls=%async_computation.11 | async-start | bytes 5242880 | tf_op jit(solution)/shard_map/reduce_scatter | solution.py:112
  744.1 291.7 %reduce-scatter.9.cloned.1.call-start = ((), (), s32[]{:S(2)}) async-start(), calls=%async_computation.10 | async-start | bytes 5242880 | tf_op jit(solution)/shard_map/reduce_scatter | solution.py:112
  778.3 320.6 %reduce-scatter.5.cloned.1.call-start = ((), (), s32[]{:S(2)}) async-start(), calls=%async_computation.8 | async-start | bytes 3932160 | tf_op jit(solution)/shard_map/reduce_scatter | solution.py:112
  830.0 47.7 %collective-permute-start.60 = (bf16[256,2048]{1,0:T(8,128)(2,1)}, bf16[256,2048]{1,0:T(8,128)(2,1)S(1)}, u32[]{:S(2)}, u32[]{:S(2)}) collective-permute-start(bf16[256,2048]{1,0:T(8,128)(2,1)} %convolution_convert_fusion.12), channel_id=1, source_target_pairs={{0,2},{2,0},{4,6},{6,4},{1,3},{3,1},{5,7},{7,5},{8,10},{10,8},{12,... | collective-permute-start | bytes 3145736 | tf_op jit(solution)/shard_map/ppermute | solution.py:48
  831.3 55.4 %collective-permute-start.71 = (bf16[2048,768]{1,0:T(8,128)(2,1)}, bf16[2048,768]{1,0:T(8,128)(2,1)}, u32[]{:S(2)}, u32[]{:S(2)}) collective-permute-start(bf16[2048,768]{1,0:T(8,128)(2,1)} %convolution_convert_fusion), channel_id=1, source_target_pairs={{0,1},{1,0},{2,3},{3,2},{4,5},{5,4},{6,7},{7,6},{8,9},{9,8},{10,11... | collective-permute-start | bytes 9437192 | tf_op jit(solution)/shard_map/ppermute | solution.py:48
  957.8 80.6 %collective-permute-start.84 = (bf16[128,1024]{1,0:T(8,128)(2,1)}, bf16[128,1024]{1,0:T(8,128)(2,1)S(1)}, u32[]{:S(2)}, u32[]{:S(2)}) collective-permute-start(bf16[128,1024]{1,0:T(8,128)(2,1)} %dynamic-slice_bitcast_fusion.3), channel_id=1, source_target_pairs={{0,2},{2,0},{4,6},{6,4},{1,3},{3,1},{5,7},{7,5},{8,10},{10,8},{12,... | collective-permute-start | bytes 786440 | tf_op jit(solution)/shard_map/ppermute | solution.py:48
  (146 other events, 2716.5 us)
Sparse Core Ops, SparseCore 0:
  19.6 28.1 all-gather.6
  50.0 64.3 all-gather.4
  116.5 79.4 all-gather.10
  197.5 79.2 all-gather.8
  721.5 127.1 all-reduce.2
  850.8 27.3 reduce-scatter.6
  880.7 75.4 reduce-scatter.10
  958.4 77.2 reduce-scatter.8
  1038.1 60.7 reduce-scatter.4

commit v2 on v1

--- a/solution.py
+++ b/solution.py
@@ -12,6 +12,7 @@
 NEGATIVE = -1e30
 F32 = jnp.float32
 BF16 = jnp.bfloat16
+MESH = pl.DeviceIdType.MESH
 
 
 def product(former, latter):
@@ -76,6 +77,15 @@
     return jnp.concatenate(sums, axis=0)
 
 
+def summed(values, axes):
+    for axis in axes:
+        mask = 1
+        while mask < lax.axis_size(axis):
+            values = values + swap(values, axis, mask)
+            mask *= 2
+    return values
+
+
 def joined(blocks):
     return jnp.concatenate([blocks[key] for key in sorted(blocks)], axis=0)
 
@@ -103,15 +113,23 @@
     return jnp.concatenate([half, swap(half, "tp", 1)], axis=1)
 
 
-def scatter_grad(former, latter):
+def weight_grad(former, latter):
     width = latter.shape[1] // 2
     theirs = inner(former, latter[:, width:]).astype(BF16)
-    came = swap(theirs, "tp", 1)
-    ours = inner(former, latter[:, :width])
-    summed = (ours + came.astype(F32)).astype(BF16)
-    rows = lax.psum_scatter(summed, "dp", scatter_dimension=0, tiled=True)
+    return (theirs, inner(former, latter[:, :width]))
+
+
+def over_cores(theirs, ours):
+    return (ours + swap(theirs, "tp", 1).astype(F32)).astype(BF16)
+
+
+def over_dp(both):
+    return lax.psum_scatter(both, "dp", scatter_dimension=0, tiled=True)
+
+
+def to_shards(rows):
     count = lax.axis_size("ctx")
-    return exchange(rows.reshape(count, rows.shape[0] // count, width))
+    return exchange(rows.reshape(count, rows.shape[0] // count, rows.shape[1]))
 
 
 def rows_of(here, block, size):
@@ -193,6 +211,289 @@
         )
 
 
+class Links:
+    def __init__(self, count, half):
+        self.count, self.half = count, half
+        self.bits = (count - 1).bit_length()
+        self.pairs = [(i, part) for i in range(1, count) for part in (0, 1)]
+        self.slot = {pair: n for n, pair in enumerate(self.pairs)}
+
+    def block(self, i, part):
+        if part == 0:
+            return i
+        return sum(((i >> b) & 1) << (self.bits - 1 - b) for b in range(self.bits))
+
+    def top(self, i):
+        return 1 << (i.bit_length() - 1)
+
+    def near(self, i):
+        return i ^ self.top(i)
+
+    def given(self, i):
+        return [j for j in range(self.count - 1, 0, -1) if self.near(j) == i]
+
+    def far(self, i, part):
+        mask = self.block(self.top(i), part)
+        return {"ctx": lax.bitwise_xor(lax.axis_index("ctx"), mask)}
+
+    def start_row(self, i, part):
+        return (2 * self.block(i, part) + part) * self.half
+
+    def rows(self, ref, i, part):
+        return ref.at[pl.ds(self.start_row(i, part), self.half)]
+
+    def greet(self, others=()):
+        barrier = pltpu.get_barrier_semaphore()
+        partners = [
+            {"ctx": lax.bitwise_xor(lax.axis_index("ctx"), 1 << bit)} for bit in range(self.bits)
+        ]
+        partners += list(others)
+        for partner in partners:
+            pl.semaphore_signal(barrier, 1, device_id=partner, device_id_type=MESH)
+        pl.semaphore_wait(barrier, len(partners))
+
+    def sharing(self, own_ref, full_ref, send_sem, recv_sem):
+        copies = {}
+        for i, part in self.pairs:
+            near = self.near(i)
+            source = (
+                own_ref.at[pl.ds(part * self.half, self.half)]
+                if near == 0
+                else self.rows(full_ref, near, part)
+            )
+            n = self.slot[(i, part)]
+            copies[(i, part)] = pltpu.make_async_remote_copy(
+                src_ref=source,
+                dst_ref=self.rows(full_ref, i, part),
+                send_sem=send_sem.at[n],
+                recv_sem=recv_sem.at[n],
+                device_id=self.far(i, part),
+                device_id_type=MESH,
+            )
+        return copies
+
+    def summing(self, send_ref, recv_ref, send_sem, recv_sem):
+        copies = {}
+        for i, part in self.pairs:
+            n = self.slot[(i, part)]
+            copies[(i, part)] = pltpu.make_async_remote_copy(
+                src_ref=send_ref.at[n],
+                dst_ref=recv_ref.at[n],
+                send_sem=send_sem.at[n],
+                recv_sem=recv_sem.at[n],
+                device_id=self.far(i, part),
+                device_id_type=MESH,
+            )
+        return copies
+
+    def pass_on(self, copies, arrived, own=False):
+        for i, part in self.pairs:
+            if self.near(i) == arrived:
+                copies[(i, part)].start()
+
+    def finish(self, copies, kept_ref, send_ref, recv_ref, result_ref):
+        middle = self.count // 2
+        for i in range(middle - 1, -1, -1):
+            for part in (0, 1):
+                for j in self.given(i):
+                    copies[(j, part)].wait_recv()
+                chunk = min(32, self.half)
+
+                def add(step, _, i=i, part=part):
+                    at = pl.ds(pl.multiple_of(step * chunk, chunk), chunk)
+                    value = kept_ref[2 * i + part, at, :]
+                    for j in self.given(i):
+                        value = value + recv_ref[self.slot[(j, part)], at, :].astype(F32)
+                    if i == 0:
+                        place = pl.ds(pl.multiple_of(part * self.half + step * chunk, chunk), chunk)
+                        result_ref[place, :] = value
+                    else:
+                        send_ref[self.slot[(i, part)], at, :] = value.astype(BF16)
+                    return 0
+
+                lax.fori_loop(0, self.half // chunk, add, 0)
+                if i:
+                    copies[(i, part)].start()
+        for pair in self.pairs:
+            copies[pair].wait_send()
+
+
+def feed_forward_kernel(
+    links,
+    own_ref,
+    grads_ref,
+    rise_ref,
+    shift_ref,
+    fall_ref,
+    full_ref,
+    hid_ref,
+    slope_ref,
+    result_ref,
+    bias_ref,
+    rise_v,
+    fall_v,
+    rows_v,
+    grads_v,
+    hid_v,
+    slope_v,
+    kept_v,
+    send_v,
+    recv_v,
+    load_sem,
+    store_sem,
+    share_send,
+    share_recv,
+    sum_send,
+    sum_recv,
+):
+    half, count = links.half, links.count
+    width, hidden = rise_v.shape
+    links.greet()
+    shares = links.sharing(own_ref, full_ref, share_send, share_recv)
+    sums = links.summing(send_v, recv_v, sum_send, sum_recv)
+    links.pass_on(shares, 0)
+    keep = pltpu.make_async_copy(own_ref, full_ref.at[pl.ds(0, 2 * half)], load_sem.at[0])
+    keep.start()
+    first = pltpu.make_async_copy(own_ref, rows_v, load_sem.at[1])
+    first.start()
+    rise = pltpu.make_async_copy(rise_ref, rise_v, load_sem.at[2])
+    rise.start()
+    fall = pltpu.make_async_copy(fall_ref, fall_v, load_sem.at[3])
+    fall.start()
+    bias_ref[...] = jnp.zeros_like(bias_ref)
+
+    def loads(ref, buffer, i, base):
+        return [
+            pltpu.make_async_copy(
+                links.rows(ref, i, part), buffer.at[pl.ds(part * half, half)], load_sem.at[base + part]
+            )
+            for part in (0, 1)
+        ]
+
+    grad_loads = loads(grads_ref, grads_v.at[0], 0, 4)
+    for copy in grad_loads:
+        copy.start()
+    stores = []
+    tile = min(256, hidden)
+    for i in range(count):
+        if i == 0:
+            first.wait()
+            rise.wait()
+            fall.wait()
+        else:
+            for part in (0, 1):
+                shares[(i, part)].wait_recv()
+            links.pass_on(shares, i)
+            row_loads = loads(full_ref, rows_v, i, 8)
+            for copy in row_loads:
+                copy.start()
+            for copy in row_loads:
+                copy.wait()
+        for copy in grad_loads:
+            copy.wait()
+        if i + 1 < count:
+            grad_loads = loads(grads_ref, grads_v.at[(i + 1) % 2], i + 1, 4 + 2 * ((i + 1) % 2))
+            for copy in grad_loads:
+                copy.start()
+        for copy in stores:
+            copy.wait()
+
+        def rise_step(step, _, i=i):
+            at = pl.ds(pl.multiple_of(step * tile, tile), tile)
+            pre = product(rows_v[...], rise_v[:, at]) + shift_ref[0:1, at]
+            back = product(grads_v[i % 2], fall_v[:, at])
+            cumulative = 0.5 * (1.0 + lax.erf(pre * 0.7071067811865476))
+            density = jnp.exp(-0.5 * pre * pre) * 0.3989422804014327
+            hid_v[:, at] = (pre * cumulative).astype(BF16)
+            slope = (back * (cumulative + pre * density)).astype(BF16)
+            slope_v[:, at] = slope
+            bias_ref[0:1, at] += jnp.sum(slope.astype(F32), axis=0, keepdims=True)
+            return 0
+
+        lax.fori_loop(0, hidden // tile, rise_step, 0)
+        stores = []
+        for n, (buffer, ref) in enumerate(((hid_v, hid_ref), (slope_v, slope_ref))):
+            for part in (0, 1):
+                copy = pltpu.make_async_copy(
+                    buffer.at[pl.ds(part * half, half)],
+                    links.rows(ref, i, part),
+                    store_sem.at[2 * n + part],
+                )
+                copy.start()
+                stores.append(copy)
+
+        def back_step(step, _, i=i):
+            at = pl.ds(pl.multiple_of(step * 256, 256), 256)
+            term = across(slope_v[...], rise_v[at, :])
+            for part in (0, 1):
+                piece = term[part * half : (part + 1) * half]
+                if i < count // 2:
+                    kept_v[2 * i + part, :, at] = piece
+                else:
+                    send_v[links.slot[(i, part)], :, at] = piece.astype(BF16)
+            return 0
+
+        lax.fori_loop(0, width // 256, back_step, 0)
+        if i >= count // 2:
+            for part in (0, 1):
+                sums[(i, part)].start()
+    links.finish(sums, kept_v, send_v, recv_v, result_ref)
+    for copy in stores:
+        copy.wait()
+    keep.wait()
+    for pair in links.pairs:
+        shares[pair].wait_send()
+
+
+def feed_forward(own, grads, rise_weight, shift, fall_weight, count):
+    rows, width = own.shape
+    hidden = rise_weight.shape[1]
+    length = rows * count
+    links = Links(count, rows // 2)
+    half, copies = links.half, len(links.pairs)
+    anywhere = pl.BlockSpec(memory_space=pl.ANY)
+    inside = pl.BlockSpec(memory_space=pltpu.VMEM)
+    dma = pltpu.SemaphoreType.DMA
+    return pl.pallas_call(
+        functools.partial(feed_forward_kernel, links),
+        out_shape=(
+            jax.ShapeDtypeStruct((length, width), BF16),
+            jax.ShapeDtypeStruct((length, hidden), BF16),
+            jax.ShapeDtypeStruct((length, hidden), BF16),
+            jax.ShapeDtypeStruct((rows, width), F32),
+            jax.ShapeDtypeStruct((1, hidden), F32),
+        ),
+        in_specs=[anywhere, anywhere, anywhere, inside, anywhere],
+        out_specs=(anywhere, anywhere, anywhere, inside, inside),
+        scratch_shapes=[
+            pltpu.VMEM((width, hidden), BF16),
+            pltpu.VMEM((width, hidden), BF16),
+            pltpu.VMEM((rows, width), BF16),
+            pltpu.VMEM((2, rows, width), BF16),
+            pltpu.VMEM((rows, hidden), BF16),
+            pltpu.VMEM((rows, hidden), BF16),
+            pltpu.VMEM((count, half, width), F32),
+            pltpu.VMEM((copies, half, width), BF16),
+            pltpu.VMEM((copies, half, width), BF16),
+            dma((10,)),
+            dma((4,)),
+            dma((copies,)),
+            dma((copies,)),
+            dma((copies,)),
+            dma((copies,)),
+        ],
+        compiler_params=pltpu.CompilerParams(
+            collective_id=3, has_side_effects=True, vmem_limit_bytes=58 * 1024 * 1024
+        ),
+        cost_estimate=pl.CostEstimate(
+            flops=6 * length * width * hidden,
+            bytes_accessed=length * width * 8 + width * hidden * 4 + length * hidden * 4,
+            transcendentals=length * hidden * 2,
+        ),
+        name="feed_forward",
+    )(own, grads, rise_weight, shift, fall_weight)
+
+
 def attend_forward(here, qkv, blocks):
     length, width = qkv.shape
     heads = width // (3 * HEAD_DIM)
@@ -287,30 +588,38 @@
     units = [(r, part) for r in range(ctx) for part in (0, 1)]
     place = {key: slice(n * half_rows, (n + 1) * half_rows) for n, key in enumerate(units)}
 
+    inputs = lax.dynamic_index_in_dim(tokens, core, 0, keepdims=False)
+    incoming = lax.dynamic_index_in_dim(cotangent, core, 0, keepdims=False)
+
+    packed = jnp.stack(
+        [w.reshape(thin, ctx, heads, HEAD_DIM) for w in (query_weight, key_weight, value_weight)],
+        axis=3,
+    ).reshape(thin, ctx, heads * 3 * HEAD_DIM)
+    qkv_pieces = packed.transpose(1, 0, 2)
+    qkv_weight = gather_weight(qkv_pieces)
+    token_blocks = share(halves(inputs))
+    first_arrivals = [token_blocks[(1, 0)], token_blocks[(ctx // 2, 1)]]
+    out_pieces, rise_pieces, fall_pieces = after(
+        (
+            output_weight.reshape(ctx, heads * HEAD_DIM, thin).transpose(0, 2, 1),
+            up_weight.reshape(thin, ctx, hidden).transpose(1, 0, 2),
+            down_weight.reshape(ctx, hidden, thin).transpose(0, 2, 1),
+        ),
+        *first_arrivals,
+    )
+    out_weight = gather_weight(out_pieces)
+    rise_weight = gather_weight(rise_pieces)
+    fall_weight = gather_weight(fall_pieces)
+
     small = jnp.stack(
         [attention_gain, attention_bias, feedforward_gain, feedforward_bias, output_bias, down_bias]
     ).astype(F32)
     table = jnp.zeros((6, model_width), F32)
     table = lax.dynamic_update_slice(table, small, (0, shard * thin))
-    flat = ("dp", "ctx")
-    mask = 1
-    while mask < dp * ctx:
-        table = table + lax.ppermute(table, flat, [(i, i ^ mask) for i in range(dp * ctx)])
-        mask *= 2
+    table = summed(table, ("dp", "ctx"))
     gain_one, shift_one, gain_two, shift_two, output_shift, down_shift = [
         table[n : n + 1] for n in range(6)
     ]
-
-    packed = jnp.stack(
-        [w.reshape(thin, ctx, heads, HEAD_DIM) for w in (query_weight, key_weight, value_weight)],
-        axis=3,
-    ).reshape(thin, ctx, heads * 3 * HEAD_DIM)
-    qkv_weight = gather_weight(packed.transpose(1, 0, 2))
-    out_weight = gather_weight(
-        output_weight.reshape(ctx, heads * HEAD_DIM, thin).transpose(0, 2, 1)
-    )
-    rise_weight = gather_weight(up_weight.reshape(thin, ctx, hidden).transpose(1, 0, 2))
-    fall_weight = gather_weight(down_weight.reshape(ctx, hidden, thin).transpose(0, 2, 1))
 
     def own_columns(vector):
         return lax.dynamic_index_in_dim(vector.reshape(ctx, -1), here, 0, keepdims=False)
@@ -324,54 +633,62 @@
     qkv_shift = jnp.concatenate([shifts[:wide], other_shifts[:wide]]).astype(F32)
     rise_shift = jnp.concatenate([shifts[wide:], other_shifts[wide:]]).astype(F32)
 
-    inputs = lax.dynamic_index_in_dim(tokens, core, 0, keepdims=False).astype(F32)
-    incoming = lax.dynamic_index_in_dim(cotangent, core, 0, keepdims=False)
-    normed_one, spread_one = normalize(inputs)
-    input_one = (normed_one * gain_one + shift_one).astype(BF16)
-    ones = joined(share(halves(input_one)))
+    def first_norm(rows):
+        normed, spread = normalize(rows.astype(F32))
+        return (normed * gain_one + shift_one).astype(BF16), normed, spread
+
+    ones = joined({key: first_norm(token_blocks[key])[0] for key in units})
+    wide_inputs = inputs.astype(F32)
+    _, normed_one, spread_one = first_norm(inputs)
     qkv = (product(ones, qkv_weight) + qkv_shift).astype(BF16)
-    later = after(incoming, ones)
+    later = after(incoming, *[token_blocks[key] for key in units])
     grads_in = joined(share(halves(later)))
     mixed, log_total = attend_forward(here_ref, qkv, ctx)
     branch = total({key: across(mixed[place[key]], out_weight) for key in units})
-    residual = inputs + (branch + output_shift)
+    residual = wide_inputs + (branch + output_shift)
 
     normed_two, spread_two = normalize(residual)
     input_two = (normed_two * gain_two + shift_two).astype(BF16)
-    hidden_back = product(grads_in, fall_weight)
-    twos = share(halves(input_two))
-    hid, hid_grad, second = {}, {}, {}
-    for key in units:
-        pre = product(twos[key], rise_weight) + rise_shift
-        cumulative = 0.5 * (1.0 + lax.erf(pre * 0.7071067811865476))
-        density = jnp.exp(-0.5 * pre * pre) * 0.3989422804014327
-        hid[key] = (pre * cumulative).astype(BF16)
-        hid_grad[key] = (hidden_back[place[key]] * (cumulative + pre * density)).astype(BF16)
-        second[key] = across(hid_grad[key], rise_weight)
-    second_grad = total(second)
+    all_twos, all_hid, all_hid_grad, second_grad, rise_bias = feed_forward(
+        input_two, grads_in, rise_weight, rise_shift[None], fall_weight, ctx
+    )
+    fall_parts = weight_grad(grads_in, all_hid)
+    rise_parts = weight_grad(all_twos, all_hid_grad)
+    second_grad = after(second_grad, fall_parts, rise_parts)
+    fall_both = over_cores(*fall_parts)
+    rise_both = over_cores(*rise_parts)
+    fall_rows = over_dp(fall_both)
+    rise_rows = over_dp(rise_both)
     gain_two_sum = jnp.sum(second_grad * normed_two, axis=0)
     bias_two_sum = jnp.sum(second_grad, axis=0)
     wide_incoming = incoming.astype(F32)
     residual_grad = wide_incoming + norm_back(second_grad * gain_two, normed_two, spread_two)
     branch_grad = residual_grad.astype(BF16)
-    branch_grads = joined(share(halves(branch_grad)))
-
-    all_hid, all_hid_grad, all_twos = joined(hid), joined(hid_grad), joined(twos)
-    fall_grad = scatter_grad(grads_in, all_hid)
-    rise_grad = scatter_grad(all_twos, all_hid_grad)
-    rise_bias = jnp.sum(all_hid_grad.astype(F32), axis=0)
+    branch_blocks = share(halves(branch_grad))
+    late_hid = after(all_hid, branch_grad)
+    lasts = {key: across(late_hid[place[key]], fall_weight) for key in units}
+    branch_blocks, lasts = lax.optimization_barrier((branch_blocks, lasts))
+    branch_grads = joined(branch_blocks)
+    block_out = residual + (total(lasts) + down_shift)
 
     mixed_grad = product(branch_grads, out_weight).astype(BF16)
-    out_grad = scatter_grad(branch_grads, mixed)
-    late_hid = after(all_hid, branch_grads)
-    block_out = residual + (
-        total({key: across(late_hid[place[key]], fall_weight) for key in units}) + down_shift
-    )
+    mixed_grad = after(mixed_grad, fall_rows)
     own_out = block_out.astype(BF16)
     qkv_grads = attend_backward(here_ref, qkv, mixed_grad, mixed, log_total, ctx)
-    first_grad = total({key: across(qkv_grads[place[key]], qkv_weight) for key in units})
-    qkv_grad = scatter_grad(ones, qkv_grads)
-    qkv_bias = jnp.sum(qkv_grads.astype(F32), axis=0)
+    qkv_grads = after(qkv_grads, rise_rows, own_out)
+    first_terms = {key: across(qkv_grads[place[key]], qkv_weight) for key in units}
+    first_grad = total(first_terms)
+    late_grads = after(qkv_grads, first_terms)
+    qkv_parts = weight_grad(ones, late_grads)
+    out_parts = weight_grad(branch_grads, after(mixed, first_terms))
+    qkv_bias = jnp.sum(late_grads.astype(F32), axis=0)
+    qkv_both = over_cores(*qkv_parts)
+    out_both = over_cores(*out_parts)
+    first_grad = after(first_grad, qkv_both, out_both, qkv_bias)
+    qkv_grad = to_shards(over_dp(qkv_both))
+    out_grad = to_shards(over_dp(out_both))
+    fall_grad = to_shards(fall_rows)
+    rise_grad = to_shards(rise_rows)
     gain_one_sum = jnp.sum(first_grad * normed_one, axis=0)
     bias_one_sum = jnp.sum(first_grad, axis=0)
     token_grad = residual_grad + norm_back(first_grad * gain_one, normed_one, spread_one)
@@ -388,19 +705,23 @@
         whole = lax.dynamic_update_slice(whole, own[None, None], (core, here, 0))
         return lax.dynamic_update_slice(whole, other[None, None], (1 - core, here, 0))
 
-    features = jnp.stack(
+    everywhere = ("tp", "ctx", "dp")
+    early = jnp.stack(
         [
-            gain_one_sum,
-            bias_one_sum,
             gain_two_sum,
             bias_two_sum,
             jnp.sum(branch_grad.astype(F32), axis=0),
             jnp.sum(wide_incoming, axis=0),
         ]
     )
-    features, qkv_bias, rise_bias = lax.psum(
-        (features, spread_columns(qkv_bias), spread_columns(rise_bias)), ("dp", "ctx", "tp")
-    )
+    features = jnp.concatenate(
+        [
+            summed(jnp.stack([gain_one_sum, bias_one_sum]), everywhere),
+            summed(early, everywhere),
+        ]
+    )
+    qkv_bias = summed(spread_columns(qkv_bias), everywhere)
+    rise_bias = summed(spread_columns(rise_bias[0]), everywhere)
     features = lax.dynamic_slice(features, (0, shard * thin), (6, thin))
     qkv_bias = lax.dynamic_index_in_dim(qkv_bias, core, 0, keepdims=False)
     qkv_bias = qkv_bias.reshape(ctx * heads, 3, HEAD_DIM)

time: 1130 us -> 1020 us (0.903)
  waiting for transfers between devices: 490 us -> 312 us
  Pallas kernels: 52.2 us -> 193 us
  matrix products: 315 us -> 189 us
  other arithmetic: 52.4 us -> 122 us
  local copies, waits for them, and re-layouts: 112 us -> 84.7 us
    pallas_call x0 -> x1, Pallas kernels: none -> 141 us  [feed_forward(): pl.pallas_call(functools.partial(feed_forward_kernel, links), out_shape=(...]
    reduce_scatter x4, waiting for transfers between devices: 130 us -> 16.4 us  [over_dp(): return lax.psum_scatter(both, 'dp', scatter_dimension=0, tiled=True)]
    dot_general x11 -> x2, matrix products: 95 us -> 19.5 us  [product(): return jnp.dot(former, latter, preferred_element_type=F32)]
    ppermute x83 -> x95, waiting for transfers between devices: 346 us -> 292 us  [swap(): return lax.ppermute(value, axis, [(i, i ^ mask) for i in range(size)])]
    dot_general x32 -> x24, matrix products: 132 us -> 85 us  [across(): lax.dot_general(former, latter, (((1,), (1,)), ((), ())), preferred_eleme...]
    convert_element_type x0 -> x7, other arithmetic: none -> 23 us  [the longest x2 11.6 us: over_cores(): return (ours + swap(theirs, 'tp', 1).astype(F32)).astype(BF16)]
    unnamed x201 -> x184, local copies, waits for them, and re-layouts: 56 us -> 40.3 us
    unnamed x10 -> x17, other arithmetic: 4.71 us -> 19.3 us
  transfers between devices with their start and end apart: 96 -> 103, of which waited for: 46 -> 37; matrix products, arithmetic and copies ran while one was open for 40% -> 32% of each run, Pallas kernels for 5% -> 5%
where the time goes in v2:
time: 1020 us; the launch traced here: 1010 us
  waiting for transfers between devices  312 us (31%)
  Pallas kernels  193 us (19%)
  matrix products  189 us (19%)
  other arithmetic  122 us (12%)
  starting transfers between devices  92.3 us (9%)
  local copies, waits for them, and re-layouts  84.7 us (8%)
  between operations  16.1 us (2%)
    ppermute x95, waiting for transfers between devices, swap(): return lax.ppermute(value, axis, [(i, i ^ mask) for i in range(size)])  292 us
    pallas_call x1, Pallas kernels, feed_forward(): pl.pallas_call(functools.partial(feed_forward_kernel, links), out_shape=(...  141 us
    ppermute x95, starting transfers between devices, swap(): return lax.ppermute(value, axis, [(i, i ^ mask) for i in range(size)])  91.3 us
    dot_general x24, matrix products, across(): lax.dot_general(former, latter, (((1,), (1,)), ((), ())), preferred_eleme...  85 us
    dot_general x8, matrix products, inner(): lax.dot_general(former, latter, (((0,), (0,)), ((), ())), preferred_eleme...  84.4 us
    unnamed x184, local copies, waits for them, and re-layouts  40.3 us
    pallas_call x1, Pallas kernels, attend_backward(): pl.pallas_call(functools.partial(attend_backward_kernel, size, blocks), o...  31.5 us
  transfers between devices with their start and end apart: 103, of which 37 were waited for; matrix products, arithmetic and copies ran while one was open for 32% of the time, Pallas kernels for 5%

profile of v2, /device:TPU:0, one launch (start us, length us, event | category | flops | bytes accessed | tf_op | source)
XLA Modules:
  0.0 1008.4 jit_solution(16024775739340968115)
XLA Ops:
  56.1 23.5 %collective-permute-done.2 = f32[6,2048]{1,0:T(8,128)S(1)} collective-permute-done((f32[6,2048]{1,0:T(8,128)S(1)}, f32[6,2048]{1,0:T(8,128)S(1)}, u32[]{:S(2)}, u32[]{:S(2)}) %collective-permute-start.2) | collective-permute-done | bytes 49184 | tf_op jit(solution)/shard_map/ppermute | solution.py:49
  140.7 8.5 collective-permute-done.36
  168.5 30.7 %collective-permute-done.25 = bf16[256,2048]{1,0:T(8,128)(2,1)} collective-permute-done((bf16[256,2048]{1,0:T(8,128)(2,1)}, bf16[256,2048]{1,0:T(8,128)(2,1)}, u32[]{:S(2)}, u32[]{:S(2)}) %collective-permute-start.25) | collective-permute-done | bytes 1048608 | tf_op jit(solution)/shard_map/ppermute | solution.py:49
  215.3 13.6 %add_convert_fusion.qkv_ref = bf16[2048,1536]{1,0:T(8,128)(2,1)S(1)} fusion(bf16[2048,2048]{1,0:T(8,128)(2,1)S(1)} %bitcast.337, bf16[2048,1536]{1,0:T(8,128)(2,1)S(1)} %constant_dynamic-update-slice_fusion, f32[1536]{0:T(1024)S(1)} %maximum_convert_fusion.1), kind=kOutput, calls=%fused_computation.1 | convolution fusion | flops 12891193344 | bytes 20977664 | tf_op jit(solution)/shard_map/dot_general | solution.py:19
  228.9 20.0 %attend_forward.1 = (bf16[2048,512]{1,0:T(8,128)(2,1)S(1)}, f32[4,8,2048]{2,1,0:T(8,128)S(1)}) custom-call(s32[1]{0:T(128)} %bitcast.1.here_ref, bf16[2048,1536]{1,0:T(8,128)(2,1)S(1)} %add_convert_fusion.qkv_ref), custom_call_target="tpu_custom_call" | custom-call | flops 10737418240 | bytes 12582912 | tf_op jit(solution)/shard_map/attend_forward/pallas_call | solution.py:502
  260.2 16.9 %collective-permute-done.20 = bf16[256,2048]{1,0:T(8,128)(2,1)} collective-permute-done((bf16[256,2048]{1,0:T(8,128)(2,1)}, bf16[256,2048]{1,0:T(8,128)(2,1)}, u32[]{:S(2)}, u32[]{:S(2)}) %collective-permute-start.20) | collective-permute-done | bytes 1048608 | tf_op jit(solution)/shard_map/ppermute | solution.py:49
  287.9 10.4 %collective-permute-done.19 = bf16[256,2048]{1,0:T(8,128)(2,1)S(1)} collective-permute-done((bf16[256,2048]{1,0:T(8,128)(2,1)}, bf16[256,2048]{1,0:T(8,128)(2,1)S(1)}, u32[]{:S(2)}, u32[]{:S(2)}) %collective-permute-start.19) | collective-permute-done | bytes 1048608 | tf_op jit(solution)/shard_map/ppermute | solution.py:49
  310.1 18.7 %collective-permute-done.22 = bf16[256,2048]{1,0:T(8,128)(2,1)S(1)} collective-permute-done((bf16[256,2048]{1,0:T(8,128)(2,1)}, bf16[256,2048]{1,0:T(8,128)(2,1)S(1)}, u32[]{:S(2)}, u32[]{:S(2)}) %collective-permute-start.22) | collective-permute-done | bytes 1048608 | tf_op jit(solution)/shard_map/ppermute | solution.py:49
  334.3 8.1 pad_maximum_fusion.rise_ref
  347.0 141.4 %feed_forward.1 = (bf16[2048,2048]{1,0:T(8,128)(2,1)}, bf16[2048,2048]{1,0:T(8,128)(2,1)}, bf16[2048,2048]{1,0:T(8,128)(2,1)}, f32[512,2048]{1,0:T(8,128)}, f32[1,2048]{1,0:T(1,128)}) custom-call(bf16[512,2048]{1,0:T(8,128)(2,1)} %add_convert_fusion.4.own_ref, bf16[2048,2048]{1,0:T(8,128)(2,1)} %constant_dynamic-update-slice_fusion.4.grads_ref, ...), custom_call_target="tpu_custom_call" | custom-call | flops 51539607552 | bytes 67108864 | tf_op jit(solution)/shard_map/feed_forward/pallas_call | solution.py:457
  488.4 14.1 %fusion.24 = bf16[2048,1024]{1,0:T(8,128)(2,1)} fusion(bf16[2048,2048]{1,0:T(8,128)(2,1)} %constant_dynamic-update-slice_fusion.4.grads_ref, bf16[2048,2048]{1,0:T(8,128)(2,1)} %get-tuple-element.61), kind=kOutput, calls=%fused_computation.45 | convolution fusion | flops 8592031744 | bytes 16777216 | tf_op jit(solution)/shard_map/dot_general | solution.py:23
  502.6 11.4 %fusion.27 = bf16[2048,1024]{1,0:T(8,128)(2,1)} fusion(bf16[2048,2048]{1,0:T(8,128)(2,1)S(1)} %copy-done.62, bf16[2048,2048]{1,0:T(8,128)(2,1)S(1)} %copy-done.63), kind=kOutput, calls=%fused_computation.46 | convolution fusion | flops 8592031744 | bytes 16777216 | tf_op jit(solution)/shard_map/dot_general | solution.py:23
  514.0 11.7 %fusion.16 = f32[2048,1024]{1,0:T(8,128)} fusion(bf16[2048,2048]{1,0:T(8,128)(2,1)S(1)} %copy-done.62, bf16[2048,2048]{1,0:T(8,128)(2,1)S(1)} %copy-done.63), kind=kOutput, calls=%fused_computation.34 | convolution fusion | flops 8589934592 | bytes 20971520 | tf_op jit(solution)/shard_map/dot_general | solution.py:23
  526.4 13.1 %fusion.20 = f32[2048,1024]{1,0:T(8,128)S(1)} fusion(bf16[2048,2048]{1,0:T(8,128)(2,1)} %constant_dynamic-update-slice_fusion.4.grads_ref, bf16[2048,2048]{1,0:T(8,128)(2,1)} %get-tuple-element.61), kind=kOutput, calls=%fused_computation.38 | convolution fusion | flops 8589934592 | bytes 20971520 | tf_op jit(solution)/shard_map/dot_general | solution.py:23
  551.8 7.2 fusion.98
  559.0 7.2 fusion.100
  616.7 11.3 %collective-permute-done.40 = bf16[256,2048]{1,0:T(8,128)(2,1)} collective-permute-done((bf16[256,2048]{1,0:T(8,128)(2,1)S(1)}, bf16[256,2048]{1,0:T(8,128)(2,1)}, u32[]{:S(2)}, u32[]{:S(2)}) %collective-permute-start.40) | collective-permute-done | bytes 1048608 | tf_op jit(solution)/shard_map/ppermute | solution.py:49
  627.9 21.0 %collective-permute-done.44 = bf16[256,2048]{1,0:T(8,128)(2,1)S(1)} collective-permute-done((bf16[256,2048]{1,0:T(8,128)(2,1)S(1)}, bf16[256,2048]{1,0:T(8,128)(2,1)S(1)}, u32[]{:S(2)}, u32[]{:S(2)}) %collective-permute-start.44) | collective-permute-done | bytes 1048608 | tf_op jit(solution)/shard_map/ppermute | solution.py:49
  661.1 34.6 %collective-permute-done.46 = bf16[256,2048]{1,0:T(8,128)(2,1)} collective-permute-done((bf16[256,2048]{1,0:T(8,128)(2,1)}, bf16[256,2048]{1,0:T(8,128)(2,1)}, u32[]{:S(2)}, u32[]{:S(2)}) %collective-permute-start.46) | collective-permute-done | bytes 1048608 | tf_op jit(solution)/shard_map/ppermute | solution.py:49
  705.2 15.8 %collective-permute-done.47 = bf16[256,2048]{1,0:T(8,128)(2,1)S(1)} collective-permute-done((bf16[256,2048]{1,0:T(8,128)(2,1)S(1)}, bf16[256,2048]{1,0:T(8,128)(2,1)S(1)}, u32[]{:S(2)}, u32[]{:S(2)}) %collective-permute-start.47) | collective-permute-done | bytes 1048608 | tf_op jit(solution)/shard_map/ppermute | solution.py:49
  728.8 5.8 convolution_convert_fusion.1.grad_ref
  738.5 31.5 %attend_backward.1 = bf16[2048,1536]{1,0:T(8,128)(2,1)S(1)} custom-call(s32[1]{0:T(128)} %bitcast.1.here_ref, bf16[2048,1536]{1,0:T(8,128)(2,1)} %copy-done.5, bf16[2048,512]{1,0:T(8,128)(2,1)S(1)} %copy-done.6, bf16[2048,512]{1,0:T(8,128)(2,1)S(1)} %get-tuple-element.82.out_ref, f32[4,8,2048]{2,1,0:T(8,128)S(1)} %get-tuple-element.79.log_ref), custom_call_target="tpu_custom_call" | custom-call | flops 26843545600 | bytes 25165824 | tf_op jit(solution)/shard_map/attend_backward/pallas_call | solution.py:535
  772.8 5.9 fusion.114
  811.7 11.5 %convolution_convert_fusion = bf16[2048,768]{1,0:T(8,128)(2,1)} fusion(bf16[2048,2048]{1,0:T(8,128)(2,1)} %fusion.95, bf16[2048,1536]{1,0:T(8,128)(2,1)S(1)} %bitcast.262), kind=kOutput, calls=%fused_computation.49 | convolution fusion | flops 6444023808 | bytes 14680064 | tf_op jit(solution)/shard_map/dot_general | solution.py:23
  823.2 12.4 %collective-permute-done.77 = f32[2,4,768]{2,1,0:T(4,128)S(1)} collective-permute-done((f32[2,4,768]{2,1,0:T(4,128)S(1)}, f32[2,4,768]{2,1,0:T(4,128)S(1)}, u32[]{:S(2)}, u32[]{:S(2)}) %collective-permute-start.77) | collective-permute-done | bytes 24608 | tf_op jit(solution)/shard_map/ppermute | solution.py:49
  853.2 9.7 collective-permute-done.85
  865.5 9.4 collective-permute-done.93
  882.2 6.9 fusion.37
  889.2 12.1 %collective-permute-done.55 = bf16[256,2048]{1,0:T(8,128)(2,1)} collective-permute-done((bf16[256,2048]{1,0:T(8,128)(2,1)}, bf16[256,2048]{1,0:T(8,128)(2,1)}, u32[]{:S(2)}, u32[]{:S(2)}) %collective-permute-start.55) | collective-permute-done | bytes 1048608 | tf_op jit(solution)/shard_map/ppermute | solution.py:49
  905.3 12.0 %add_convert_fusion.3 = bf16[2048,768]{1,0:T(8,128)(2,1)} fusion(bf16[2048,768]{1,0:T(8,128)(2,1)} %collective-permute-done.60, bf16[2048,2048]{1,0:T(8,128)(2,1)} %fusion.95, bf16[2048,1536]{1,0:T(8,128)(2,1)} %copy-done), kind=kOutput, calls=%fused_computation.5 | convolution fusion | flops 6447169536 | bytes 17825792 | tf_op jit(solution)/shard_map/dot_general | solution.py:23
  962.9 16.4 %reduce-scatter.9.cloned.1.call-done = bf16[512,768]{1,0:T(8,128)(2,1)} async-done(((bf16[2048,768]{1,0:T(8,128)(2,1)}), bf16[512,768]{1,0:T(8,128)(2,1)}) %reduce-scatter.9.cloned.1.call-update) | async-done | bytes 786448 | tf_op jit(solution)/shard_map/reduce_scatter | solution.py:127
  989.6 8.4 collective-permute-done.74
  (604 shorter events, 410.9 us)
Async XLA Ops:
  7.2 154.1 %all-gather.5.cloned.1.call-start = ((), (), s32[]{:S(2)}) async-start(), calls=%async_computation.4 | async-start | bytes 3932160 | tf_op jit(solution)/shard_map/all_gather | solution.py:112
  27.4 141.0 %all-gather.7.cloned.1.call-start = ((), (), s32[]{:S(2)}) async-start(), calls=%async_computation.5 | async-start | bytes 1310720 | tf_op jit(solution)/shard_map/all_gather | solution.py:112
  30.5 49.4 %collective-permute-start.7 = (bf16[256,2048]{1,0:T(8,128)(2,1)}, bf16[256,2048]{1,0:T(8,128)(2,1)S(1)}, u32[]{:S(2)}, u32[]{:S(2)}) collective-permute-start(bf16[256,2048]{1,0:T(8,128)(2,1)} %get-tuple-element.137), channel_id=1, source_target_pairs={{0,4},{2,6},{4,0},{6,2},{1,5},{3,7},{5,1},{7,3},{8,12},{10,14},{12... | collective-permute-start | bytes 3145736 | tf_op jit(solution)/shard_map/ppermute | solution.py:49
  32.0 87.2 %collective-permute-start.5 = (bf16[256,2048]{1,0:T(8,128)(2,1)}, bf16[256,2048]{1,0:T(8,128)(2,1)}, u32[]{:S(2)}, u32[]{:S(2)}) collective-permute-start(bf16[256,2048]{1,0:T(8,128)(2,1)} %get-tuple-element.137), channel_id=1, source_target_pairs={{0,2},{2,0},{4,6},{6,4},{1,3},{3,1},{5,7},{7,5},{8,10},{10,8},{12,... | collective-permute-start | bytes 3145736 | tf_op jit(solution)/shard_map/ppermute | solution.py:49
  35.1 44.7 %collective-permute-start.4 = (bf16[256,2048]{1,0:T(8,128)(2,1)}, bf16[256,2048]{1,0:T(8,128)(2,1)}, u32[]{:S(2)}, u32[]{:S(2)}) collective-permute-start(bf16[256,2048]{1,0:T(8,128)(2,1)} %get-tuple-element.146), channel_id=1, source_target_pairs={{0,2},{2,0},{4,6},{6,4},{1,3},{3,1},{5,7},{7,5},{8,10},{10,8},{12,... | collective-permute-start | bytes 3145736 | tf_op jit(solution)/shard_map/ppermute | solution.py:49
  51.3 69.3 %collective-permute-start.6 = (bf16[256,2048]{1,0:T(8,128)(2,1)}, bf16[256,2048]{1,0:T(8,128)(2,1)}, u32[]{:S(2)}, u32[]{:S(2)}) collective-permute-start(bf16[256,2048]{1,0:T(8,128)(2,1)} %get-tuple-element.146), channel_id=1, source_target_pairs={{0,4},{2,6},{4,0},{6,2},{1,5},{3,7},{5,1},{7,3},{8,12},{10,14},{12... | collective-permute-start | bytes 3145736 | tf_op jit(solution)/shard_map/ppermute | solution.py:49
  95.7 164.5 %all-gather.9.cloned.1.call-start = ((), (), s32[]{:S(2)}) async-start(), calls=%async_computation.6 | async-start | bytes 5242880 | tf_op jit(solution)/shard_map/all_gather | solution.py:112
  109.9 176.5 %all-gather.11.cloned.1.call-start = ((), (), s32[]{:S(2)}) async-start(), calls=%async_computation.7 | async-start | bytes 5242880 | tf_op jit(solution)/shard_map/all_gather | solution.py:112
  150.7 586.2 %reduce-scatter.5.cloned.1.call-start = ((), (), s32[]{:S(2)}) async-start(), calls=%async_computation.8 | async-start | bytes 5242880 | tf_op jit(solution)/shard_map/reduce_scatter | solution.py:127
  152.6 50.6 %collective-permute-start.28 = (bf16[256,2048]{1,0:T(8,128)(2,1)}, bf16[256,2048]{1,0:T(8,128)(2,1)}, u32[]{:S(2)}, u32[]{:S(2)}) collective-permute-start(bf16[256,2048]{1,0:T(8,128)(2,1)} %get-tuple-element.149), channel_id=1, source_target_pairs={{0,4},{2,6},{4,0},{6,2},{1,5},{3,7},{5,1},{7,3},{8,12},{10,14},{12... | collective-permute-start | bytes 3145736 | tf_op jit(solution)/shard_map/ppermute | solution.py:49
  154.1 50.9 %collective-permute-start.26 = (bf16[256,2048]{1,0:T(8,128)(2,1)}, bf16[256,2048]{1,0:T(8,128)(2,1)}, u32[]{:S(2)}, u32[]{:S(2)}) collective-permute-start(bf16[256,2048]{1,0:T(8,128)(2,1)} %get-tuple-element.149), channel_id=1, source_target_pairs={{0,2},{2,0},{4,6},{6,4},{1,3},{3,1},{5,7},{7,5},{8,10},{10,8},{12,... | collective-permute-start | bytes 3145736 | tf_op jit(solution)/shard_map/ppermute | solution.py:49
  154.9 54.1 %collective-permute-start.27 = (bf16[256,2048]{1,0:T(8,128)(2,1)}, bf16[256,2048]{1,0:T(8,128)(2,1)S(1)}, u32[]{:S(2)}, u32[]{:S(2)}) collective-permute-start(bf16[256,2048]{1,0:T(8,128)(2,1)} %get-tuple-element.150), channel_id=1, source_target_pairs={{0,4},{2,6},{4,0},{6,2},{1,5},{3,7},{5,1},{7,3},{8,12},{10,14},{12... | collective-permute-start | bytes 3145736 | tf_op jit(solution)/shard_map/ppermute | solution.py:49
  161.3 49.2 %collective-permute-start.13 = (bf16[2048,768]{1,0:T(8,128)(2,1)}, bf16[2048,768]{1,0:T(8,128)(2,1)}, u32[]{:S(2)}, u32[]{:S(2)}) collective-permute-start(bf16[2048,768]{1,0:T(8,128)(2,1)} %all-gather.5.cloned.1.call-done), channel_id=1, source_target_pairs={{0,1},{1,0},{2,3},{3,2},{4,5},{5,4},{6,7},{7,6},{8,9},{9,8},{10,11... | collective-permute-start | bytes 9437192 | tf_op jit(solution)/shard_map/ppermute | solution.py:49
  203.2 83.2 %collective-permute-start.29 = (bf16[256,2048]{1,0:T(8,128)(2,1)}, bf16[256,2048]{1,0:T(8,128)(2,1)}, u32[]{:S(2)}, u32[]{:S(2)}) collective-permute-start(bf16[256,2048]{1,0:T(8,128)(2,1)} %collective-permute-done.25), channel_id=1, source_target_pairs={{0,4},{2,6},{4,0},{6,2},{1,5},{3,7},{5,1},{7,3},{8,12},{10,14},{12... | collective-permute-start | bytes 3145736 | tf_op jit(solution)/shard_map/ppermute | solution.py:49
  205.0 78.6 %collective-permute-start.30 = (bf16[256,2048]{1,0:T(8,128)(2,1)}, bf16[256,2048]{1,0:T(8,128)(2,1)}, u32[]{:S(2)}, u32[]{:S(2)}) collective-permute-start(bf16[256,2048]{1,0:T(8,128)(2,1)} %collective-permute-done.28), channel_id=1, source_target_pairs={{0,2},{2,0},{4,6},{6,4},{1,3},{3,1},{5,7},{7,5},{8,10},{10,8},{12,... | collective-permute-start | bytes 3145736 | tf_op jit(solution)/shard_map/ppermute | solution.py:49
  254.1 44.2 %collective-permute-start.19 = (bf16[256,2048]{1,0:T(8,128)(2,1)}, bf16[256,2048]{1,0:T(8,128)(2,1)S(1)}, u32[]{:S(2)}, u32[]{:S(2)}) collective-permute-start(bf16[256,2048]{1,0:T(8,128)(2,1)} %convolution_convert_fusion.5), channel_id=1, source_target_pairs={{0,4},{2,6},{4,0},{6,2},{1,5},{3,7},{5,1},{7,3},{8,12},{10,14},{12... | collective-permute-start | bytes 3145736 | tf_op jit(solution)/shard_map/ppermute | solution.py:49
  277.0 57.2 %collective-permute-start.34 = (bf16[2048,1024]{1,0:T(8,128)(2,1)}, bf16[2048,1024]{1,0:T(8,128)(2,1)}, u32[]{:S(2)}, u32[]{:S(2)}) collective-permute-start(bf16[2048,1024]{1,0:T(8,128)(2,1)} %all-gather.9.cloned.1.call-done), channel_id=1, source_target_pairs={{0,1},{1,0},{2,3},{3,2},{4,5},{5,4},{6,7},{7,6},{8,9},{9,8},{10,11... | collective-permute-start | bytes 12582920 | tf_op jit(solution)/shard_map/ppermute | solution.py:49
  286.4 56.0 %collective-permute-start.38 = (bf16[2048,1024]{1,0:T(8,128)(2,1)}, bf16[2048,1024]{1,0:T(8,128)(2,1)}, u32[]{:S(2)}, u32[]{:S(2)}) collective-permute-start(bf16[2048,1024]{1,0:T(8,128)(2,1)} %all-gather.11.cloned.1.call-done), channel_id=1, source_target_pairs={{0,1},{1,0},{2,3},{3,2},{4,5},{5,4},{6,7},{7,6},{8,9},{9,8},{10,11... | collective-permute-start | bytes 12582920 | tf_op jit(solution)/shard_map/ppermute | solution.py:49
  525.9 43.8 %collective-permute-start.87 = (f32[2,4,1024]{2,1,0:T(4,128)S(1)}, f32[2,4,1024]{2,1,0:T(4,128)S(1)}, u32[]{:S(2)}, u32[]{:S(2)}) collective-permute-start(f32[2,4,1024]{2,1,0:T(4,128)S(1)} %dynamic_update_slice.118), channel_id=1, source_target_pairs={{0,1},{1,0},{2,3},{3,2},{4,5},{5,4},{6,7},{7,6},{8,9},{9,8},{10,11... | collective-permute-start | bytes 98312 | tf_op jit(solution)/shard_map/ppermute | solution.py:49
  551.6 221.2 %reduce-scatter.7.cloned.1.call-start = ((), (), s32[]{:S(2)}) async-start(), calls=%async_computation.9 | async-start | bytes 5242880 | tf_op jit(solution)/shard_map/reduce_scatter | solution.py:127
  575.2 80.0 %collective-permute-start.53 = (bf16[2048,1024]{1,0:T(8,128)(2,1)}, bf16[2048,1024]{1,0:T(8,128)(2,1)}, u32[]{:S(2)}, u32[]{:S(2)}) collective-permute-start(bf16[2048,1024]{1,0:T(8,128)(2,1)} %fusion.27), channel_id=1, source_target_pairs={{0,1},{1,0},{2,3},{3,2},{4,5},{5,4},{6,7},{7,6},{8,9},{9,8},{10,11... | collective-permute-start | bytes 12582920 | tf_op jit(solution)/shard_map/ppermute | solution.py:49
  603.7 45.3 %collective-permute-start.44 = (bf16[256,2048]{1,0:T(8,128)(2,1)S(1)}, bf16[256,2048]{1,0:T(8,128)(2,1)S(1)}, u32[]{:S(2)}, u32[]{:S(2)}) collective-permute-start(bf16[256,2048]{1,0:T(8,128)(2,1)S(1)} %collective-permute-done.42), channel_id=1, source_target_pairs={{0,2},{2,0},{4,6},{6,4},{1,3},{3,1},{5,7},{7,5},{8,10},{10,8},{12,... | collective-permute-start | bytes 3145736 | tf_op jit(solution)/shard_map/ppermute | solution.py:49
  605.4 43.6 %collective-permute-start.43 = (bf16[256,2048]{1,0:T(8,128)(2,1)S(1)}, bf16[256,2048]{1,0:T(8,128)(2,1)}, u32[]{:S(2)}, u32[]{:S(2)}) collective-permute-start(bf16[256,2048]{1,0:T(8,128)(2,1)S(1)} %collective-permute-done.39), channel_id=1, source_target_pairs={{0,4},{2,6},{4,0},{6,2},{1,5},{3,7},{5,1},{7,3},{8,12},{10,14},{12... | collective-permute-start | bytes 3145736 | tf_op jit(solution)/shard_map/ppermute | solution.py:49
  649.0 56.2 %collective-permute-start.45 = (bf16[256,2048]{1,0:T(8,128)(2,1)}, bf16[256,2048]{1,0:T(8,128)(2,1)}, u32[]{:S(2)}, u32[]{:S(2)}) collective-permute-start(bf16[256,2048]{1,0:T(8,128)(2,1)} %fusion.104), channel_id=1, source_target_pairs={{0,4},{2,6},{4,0},{6,2},{1,5},{3,7},{5,1},{7,3},{8,12},{10,14},{12... | collective-permute-start | bytes 3145736 | tf_op jit(solution)/shard_map/ppermute | solution.py:49
  649.4 46.3 %collective-permute-start.46 = (bf16[256,2048]{1,0:T(8,128)(2,1)}, bf16[256,2048]{1,0:T(8,128)(2,1)}, u32[]{:S(2)}, u32[]{:S(2)}) collective-permute-start(bf16[256,2048]{1,0:T(8,128)(2,1)} %fusion.100), channel_id=1, source_target_pairs={{0,4},{2,6},{4,0},{6,2},{1,5},{3,7},{5,1},{7,3},{8,12},{10,14},{12... | collective-permute-start | bytes 3145736 | tf_op jit(solution)/shard_map/ppermute | solution.py:49
  651.0 71.9 %collective-permute-start.48 = (bf16[256,2048]{1,0:T(8,128)(2,1)}, bf16[256,2048]{1,0:T(8,128)(2,1)}, u32[]{:S(2)}, u32[]{:S(2)}) collective-permute-start(bf16[256,2048]{1,0:T(8,128)(2,1)} %fusion.106), channel_id=1, source_target_pairs={{0,2},{2,0},{4,6},{6,4},{1,3},{3,1},{5,7},{7,5},{8,10},{10,8},{12,... | collective-permute-start | bytes 3145736 | tf_op jit(solution)/shard_map/ppermute | solution.py:49
  651.5 47.1 %collective-permute-start.49 = (bf16[256,2048]{1,0:T(8,128)(2,1)}, bf16[256,2048]{1,0:T(8,128)(2,1)}, u32[]{:S(2)}, u32[]{:S(2)}) collective-permute-start(bf16[256,2048]{1,0:T(8,128)(2,1)} %fusion.98), channel_id=1, source_target_pairs={{0,2},{2,0},{4,6},{6,4},{1,3},{3,1},{5,7},{7,5},{8,10},{10,8},{12,... | collective-permute-start | bytes 3145736 | tf_op jit(solution)/shard_map/ppermute | solution.py:49
  661.0 277.7 %reduce-scatter.11.cloned.1.call-start = ((), (), s32[]{:S(2)}) async-start(), calls=%async_computation.11 | async-start | bytes 1310720 | tf_op jit(solution)/shard_map/reduce_scatter | solution.py:127
  808.6 115.1 %collective-permute-start.54 = (bf16[256,2048]{1,0:T(8,128)(2,1)}, bf16[256,2048]{1,0:T(8,128)(2,1)}, u32[]{:S(2)}, u32[]{:S(2)}) collective-permute-start(bf16[256,2048]{1,0:T(8,128)(2,1)} %fusion.126), channel_id=1, source_target_pairs={{0,4},{2,6},{4,0},{6,2},{1,5},{3,7},{5,1},{7,3},{8,12},{10,14},{12... | collective-permute-start | bytes 3145736 | tf_op jit(solution)/shard_map/ppermute | solution.py:49
  809.6 68.5 %collective-permute-start.58 = (bf16[256,2048]{1,0:T(8,128)(2,1)}, bf16[256,2048]{1,0:T(8,128)(2,1)}, u32[]{:S(2)}, u32[]{:S(2)}) collective-permute-start(bf16[256,2048]{1,0:T(8,128)(2,1)} %fusion.114), channel_id=1, source_target_pairs={{0,2},{2,0},{4,6},{6,4},{1,3},{3,1},{5,7},{7,5},{8,10},{10,8},{12,... | collective-permute-start | bytes 3145736 | tf_op jit(solution)/shard_map/ppermute | solution.py:49
  848.3 57.0 %collective-permute-start.60 = (bf16[2048,768]{1,0:T(8,128)(2,1)}, bf16[2048,768]{1,0:T(8,128)(2,1)}, u32[]{:S(2)}, u32[]{:S(2)}) collective-permute-start(bf16[2048,768]{1,0:T(8,128)(2,1)} %convolution_convert_fusion), channel_id=1, source_target_pairs={{0,1},{1,0},{2,3},{3,2},{4,5},{5,4},{6,7},{7,6},{8,9},{9,8},{10,11... | collective-permute-start | bytes 9437192 | tf_op jit(solution)/shard_map/ppermute | solution.py:49
  889.1 90.1 %reduce-scatter.9.cloned.1.call-start = ((), (), s32[]{:S(2)}) async-start(), calls=%async_computation.10 | async-start | bytes 3932160 | tf_op jit(solution)/shard_map/reduce_scatter | solution.py:127
  (151 other events, 3113.1 us)
Sparse Core Ops, SparseCore 0:
  27.5 66.5 all-gather.4
  96.3 27.4 all-gather.6
  125.4 80.2 all-gather.8
  207.1 79.2 all-gather.10
  551.7 79.2 reduce-scatter.4
  661.2 75.5 reduce-scatter.6
  889.3 27.4 reduce-scatter.10
  919.7 59.5 reduce-scatter.8

commit v3 on v2

v3 whole, which is shorter than its diff:
```python
import functools

import jax
import jax.numpy as jnp
from jax import lax
from jax.experimental import pallas as pl
from jax.experimental.pallas import tpu as pltpu
from jax.sharding import PartitionSpec as P

HEAD_DIM = 128
EPSILON = 1e-05
NEGATIVE = -1e30
F32 = jnp.float32
BF16 = jnp.bfloat16
MESH = pl.DeviceIdType.MESH


def product(former, latter):
    return jnp.dot(former, latter, preferred_element_type=F32)


def inner(former, latter):
    return lax.dot_general(former, latter, (((0,), (0,)), ((), ())), preferred_element_type=F32)


def across(former, latter):
    return lax.dot_general(former, latter, (((1,), (1,)), ((), ())), preferred_element_type=F32)


def normalize(values):
    average = jnp.mean(values, axis=-1, keepdims=True)
    centred = values - average
    spread = lax.rsqrt(jnp.mean(centred * centred, axis=-1, keepdims=True) + EPSILON)
    return (centred * spread, spread)


def norm_back(gradient, normed, spread):
    first_mean = jnp.mean(gradient, axis=-1, keepdims=True)
    second_mean = jnp.mean(gradient * normed, axis=-1, keepdims=True)
    return spread * (gradient - first_mean - normed * second_mean)


def after(values, *earlier):
    return lax.optimization_barrier((values, earlier))[0]


def swap(value, axis, mask):
    size = lax.axis_size(axis)
    return lax.ppermute(value, axis, [(i, i ^ mask) for i in range(size)])


def bit_order(part):
    bits = list(range((lax.axis_size("ctx") - 1).bit_length()))
    return bits if part == 0 else bits[::-1]


def share(parts):
    found = {}
    for part in (0, 1):
        have = {0: parts[part]}
        for bit in bit_order(part):
            mask = 1 << bit
            have.update({r ^ mask: swap(have[r], "ctx", mask) for r in list(have)})
        found.update({(r, part): have[r] for r in have})
    return found


def total(partial):
    sums = []
    for part in (0, 1):
        have = {r: partial[(r, part)] for r in range(lax.axis_size("ctx"))}
        for bit in bit_order(part)[::-1]:
            mask = 1 << bit
            came = {r ^ mask: swap(have[r].astype(BF16), "ctx", mask) for r in have if r & mask}
            have = {r: have[r].astype(F32) + came[r].astype(F32) for r in came}
        sums.append(have[0])
    return jnp.concatenate(sums, axis=0)


def summed(values, axes):
    for axis in axes:
        mask = 1
        while mask < lax.axis_size(axis):
            values = values + swap(values, axis, mask)
            mask *= 2
    return values


def joined(blocks):
    return jnp.concatenate([blocks[key] for key in sorted(blocks)], axis=0)


def halves(rows):
    middle = rows.shape[0] // 2
    return (rows[:middle], rows[middle:])


def exchange(pieces):
    count = pieces.shape[0]
    here = lax.axis_index("ctx")
    result = pieces
    for mask in range(1, count):
        other = here ^ mask
        came = swap(lax.dynamic_index_in_dim(pieces, other, 0, keepdims=False), "ctx", mask)
        result = lax.dynamic_update_index_in_dim(result, came, other, 0)
    return result


def gather_weight(pieces):
    count, rows, columns = pieces.shape
    block = exchange(pieces).reshape(count * rows, columns)
    half = lax.all_gather(block, "dp", axis=0, tiled=True)
    return jnp.concatenate([half, swap(half, "tp", 1)], axis=1)


def weight_grad(former, latter):
    width = latter.shape[1] // 2
    theirs = inner(former, latter[:, width:]).astype(BF16)
    return (theirs, inner(former, latter[:, :width]))


def over_cores(theirs, ours):
    return (ours + swap(theirs, "tp", 1).astype(F32)).astype(BF16)


def over_dp(both):
    return lax.psum_scatter(both, "dp", scatter_dimension=0, tiled=True)


def to_shards(rows):
    count = lax.axis_size("ctx")
    return exchange(rows.reshape(count, rows.shape[0] // count, rows.shape[1]))


def rows_of(here, block, size):
    return pl.multiple_of(lax.bitwise_xor(here, block) * size, size)


class Links:
    def __init__(self, count, half):
        self.count, self.half = count, half
        self.bits = (count - 1).bit_length()
        self.pairs = [(i, part) for i in range(1, count) for part in (0, 1)]
        self.slot = {pair: n for n, pair in enumerate(self.pairs)}

    def block(self, i, part):
        if part == 0:
            return i
        return sum(((i >> b) & 1) << (self.bits - 1 - b) for b in range(self.bits))

    def top(self, i):
        return 1 << (i.bit_length() - 1)

    def near(self, i):
        return i ^ self.top(i)

    def given(self, i):
        return [j for j in range(self.count - 1, 0, -1) if self.near(j) == i]

    def far(self, i, part):
        mask = self.block(self.top(i), part)
        return {"ctx": lax.bitwise_xor(lax.axis_index("ctx"), mask)}

    def start_row(self, i, part):
        return (2 * self.block(i, part) + part) * self.half

    def rows(self, ref, i, part):
        return ref.at[pl.ds(self.start_row(i, part), self.half)]

    def greet(self, others=(), masks=None):
        barrier = pltpu.get_barrier_semaphore()
        masks = [1 << bit for bit in range(self.bits)] if masks is None else masks
        partners = [{"ctx": lax.bitwise_xor(lax.axis_index("ctx"), mask)} for mask in masks]
        partners += list(others)
        for partner in partners:
            pl.semaphore_signal(barrier, 1, device_id=partner, device_id_type=MESH)
        pl.semaphore_wait(barrier, len(partners))

    def sharing(self, own_ref, full_ref, send_sem, recv_sem):
        copies = {}
        for i, part in self.pairs:
            near = self.near(i)
            source = (
                own_ref.at[pl.ds(part * self.half, self.half)]
                if near == 0
                else self.rows(full_ref, near, part)
            )
            n = self.slot[(i, part)]
            copies[(i, part)] = pltpu.make_async_remote_copy(
                src_ref=source,
                dst_ref=self.rows(full_ref, i, part),
                send_sem=send_sem.at[n],
                recv_sem=recv_sem.at[n],
                device_id=self.far(i, part),
                device_id_type=MESH,
            )
        return copies

    def summing(self, send_ref, recv_ref, send_sem, recv_sem):
        copies = {}
        for i, part in self.pairs:
            n = self.slot[(i, part)]
            copies[(i, part)] = pltpu.make_async_remote_copy(
                src_ref=send_ref.at[n],
                dst_ref=recv_ref.at[n],
                send_sem=send_sem.at[n],
                recv_sem=recv_sem.at[n],
                device_id=self.far(i, part),
                device_id_type=MESH,
            )
        return copies

    def pass_on(self, copies, arrived, own=False):
        for i, part in self.pairs:
            if self.near(i) == arrived:
                copies[(i, part)].start()

    def loads(self, ref, buffer, i, sem, base):
        return [
            pltpu.make_async_copy(
                self.rows(ref, i, part),
                buffer.at[pl.ds(part * self.half, self.half)],
                sem.at[base + part],
            )
            for part in (0, 1)
        ]

    def terms(self, i, columns, width, kept_v, send_v):
        tile = min(256, width)

        def step(n, _):
            at = pl.ds(pl.multiple_of(n * tile, tile), tile)
            term = columns(at)
            for part in (0, 1):
                piece = term[part * self.half : (part + 1) * self.half]
                if i < self.count // 2:
                    kept_v[2 * i + part, :, at] = piece
                else:
                    send_v[self.slot[(i, part)], :, at] = piece.astype(BF16)
            return 0

        lax.fori_loop(0, width // tile, step, 0)

    def combine(self, copies, kept_ref, send_ref, recv_ref, result_ref, first, last):
        for i in range(first, last - 1, -1):
            for part in (0, 1):
                for j in self.given(i):
                    copies[(j, part)].wait_recv()
                chunk = min(32, self.half)

                def add(step, _, i=i, part=part):
                    at = pl.ds(pl.multiple_of(step * chunk, chunk), chunk)
                    value = kept_ref[2 * i + part, at, :]
                    for j in self.given(i):
                        value = value + recv_ref[self.slot[(j, part)], at, :].astype(F32)
                    if i == 0:
                        place = pl.ds(pl.multiple_of(part * self.half + step * chunk, chunk), chunk)
                        result_ref[place, :] = value
                    else:
                        send_ref[self.slot[(i, part)], at, :] = value.astype(BF16)
                    return 0

                lax.fori_loop(0, self.half // chunk, add, 0)
                if i:
                    copies[(i, part)].start()


def weight_grads(partner, rows_v, columns_v, theirs_v, came_v, result_ref, send_sem, recv_sem, store_sem):
    tile = 256
    width = rows_v.shape[1]
    own = columns_v.shape[1] // 2

    def place(m):
        return pl.ds(pl.multiple_of(m * tile, tile), tile)

    def swap_tile(m):
        return pltpu.make_async_remote_copy(
            src_ref=theirs_v.at[place(m)],
            dst_ref=came_v.at[place(m)],
            send_sem=send_sem.at[m],
            recv_sem=recv_sem.at[m],
            device_id=partner,
            device_id_type=MESH,
        )

    def store_tile(m):
        return pltpu.make_async_copy(came_v.at[place(m)], result_ref.at[place(m)], store_sem.at[m])

    def first(m, _):
        term = inner(rows_v[:, place(m)], columns_v[:, own : 2 * own])
        theirs_v[place(m), :] = term.astype(BF16)
        swap_tile(m).start()
        return 0

    def second(m, _):
        swap_tile(m).wait_recv()
        term = inner(rows_v[:, place(m)], columns_v[:, 0:own])
        came_v[place(m), :] = (term + came_v[place(m), :].astype(F32)).astype(BF16)
        store_tile(m).start()
        return 0

    def end(m, _):
        store_tile(m).wait()
        swap_tile(m).wait_send()
        return 0

    lax.fori_loop(0, width // tile, first, 0)
    lax.fori_loop(0, width // tile, second, 0)
    return lambda: lax.fori_loop(0, width // tile, end, 0)


def feed_forward_kernel(
    links,
    own_ref,
    grads_ref,
    both_ref,
    shift_ref,
    residual_ref,
    table_ref,
    full_ref,
    hid_ref,
    slope_ref,
    both_grad_ref,
    back_ref,
    branch_ref,
    vector_ref,
    bias_ref,
    fall_ref,
    rise_big,
    fall_big,
    rows_v,
    grads_v,
    hid_v,
    slope_v,
    kept_v,
    send_v,
    recv_v,
    theirs_v,
    came_v,
    load_sem,
    store_sem,
    pair_send,
    pair_recv,
    grad_send,
    grad_recv,
    grad_store,
    share_send,
    share_recv,
    sum_send,
    sum_recv,
):
    half, count = links.half, links.count
    width, hidden = own_ref.shape[1], hid_v.shape[1]
    length = 2 * half * count
    rise_v = rise_big.at[pl.ds(0, width), pl.ds(0, hidden)]
    fall_v = fall_big.at[pl.ds(0, width), pl.ds(0, hidden)]
    own_half = pl.ds(0, hidden // 2)
    other_half = pl.ds(hidden // 2, hidden // 2)
    partner = {"tp": 1 - lax.axis_index("tp")}
    links.greet([partner])
    swaps = [
        pltpu.make_async_remote_copy(
            src_ref=both_ref.at[:, pl.ds(n * (hidden // 2), hidden // 2)],
            dst_ref=target.at[:, other_half],
            send_sem=pair_send.at[n],
            recv_sem=pair_recv.at[n],
            device_id=partner,
            device_id_type=MESH,
        )
        for n, target in enumerate((fall_v, rise_v))
    ]
    for copy in swaps:
        copy.start()
    shares = links.sharing(own_ref, full_ref, share_send, share_recv)
    sums = links.summing(send_v, recv_v, sum_send, sum_recv)
    links.pass_on(shares, 0)
    keep = pltpu.make_async_copy(own_ref, full_ref.at[pl.ds(0, 2 * half)], load_sem.at[0])
    keep.start()
    first = pltpu.make_async_copy(own_ref, rows_v, load_sem.at[1])
    first.start()
    rise = pltpu.make_async_copy(both_ref.at[:, other_half], rise_v.at[:, own_half], load_sem.at[2])
    rise.start()
    fall = pltpu.make_async_copy(both_ref.at[:, own_half], fall_v.at[:, own_half], load_sem.at[3])
    fall.start()
    bias_ref[...] = jnp.zeros_like(bias_ref)

    grad_loads = links.loads(grads_ref, grads_v, 0, load_sem, 4)
    for copy in grad_loads:
        copy.start()
    stores = []
    tile = min(256, hidden)
    for i in range(count):
        if i == 0:
            first.wait()
            rise.wait()
            fall.wait()
            for copy in swaps:
                copy.wait_recv()
            keep_fall = pltpu.make_async_copy(fall_v, fall_ref, store_sem.at[4])
            keep_fall.start()
        else:
            for part in (0, 1):
                shares[(i, part)].wait_recv()
            links.pass_on(shares, i)
            row_loads = links.loads(full_ref, rows_v, i, load_sem, 8)
            for copy in row_loads:
                copy.start()
            for copy in row_loads:
                copy.wait()
        for copy in grad_loads + stores:
            copy.wait()

        def rise_step(step, _, i=i):
            at = pl.ds(pl.multiple_of(step * tile, tile), tile)
            pre = product(rows_v[...], rise_v[:, at]) + shift_ref[0:1, at]
            back = product(grads_v[...], fall_v[:, at])
            cumulative = 0.5 * (1.0 + lax.erf(pre * 0.7071067811865476))
            density = jnp.exp(-0.5 * pre * pre) * 0.3989422804014327
            hid_v[:, at] = (pre * cumulative).astype(BF16)
            slope = (back * (cumulative + pre * density)).astype(BF16)
            slope_v[:, at] = slope
            bias_ref[0:1, at] += jnp.sum(slope.astype(F32), axis=0, keepdims=True)
            return 0

        lax.fori_loop(0, hidden // tile, rise_step, 0)
        if i + 1 < count:
            grad_loads = links.loads(grads_ref, grads_v, i + 1, load_sem, 4)
            for copy in grad_loads:
                copy.start()
        stores = []
        for n, (buffer, ref) in enumerate(((hid_v, hid_ref), (slope_v, slope_ref))):
            for part in (0, 1):
                copy = pltpu.make_async_copy(
                    buffer.at[pl.ds(part * half, half)],
                    links.rows(ref, i, part),
                    store_sem.at[2 * n + part],
                )
                copy.start()
                stores.append(copy)

        links.terms(i, lambda at: across(slope_v[...], rise_v[at, :]), width, kept_v, send_v)
        if i >= count // 2:
            for part in (0, 1):
                sums[(i, part)].start()
    for copy in stores:
        copy.wait()
    keep.wait()
    keep_fall.wait()
    rows_big = rise_big.at[pl.ds(0, length), pl.ds(0, width)]
    columns_big = fall_big.at[pl.ds(0, length), pl.ds(0, hidden)]
    ends = []
    for n, (left, right) in enumerate(((full_ref, slope_ref), (grads_ref, hid_ref))):
        lefts = pltpu.make_async_copy(left, rows_big, load_sem.at[0])
        rights = pltpu.make_async_copy(right, columns_big, load_sem.at[1])
        lefts.start()
        rights.start()
        for end in ends:
            end()
        lefts.wait()
        rights.wait()
        ends = [
            weight_grads(
                partner,
                rows_big,
                columns_big,
                theirs_v,
                came_v.at[n],
                both_grad_ref.at[:, pl.ds((1 - n) * (hidden // 2), hidden // 2)],
                grad_send.at[n],
                grad_recv.at[n],
                grad_store.at[n],
            )
        ]
        if n == 0:
            links.combine(sums, kept_v, send_v, recv_v, None, count // 2 - 1, 1)
            finals = [
                pltpu.make_async_copy(
                    residual_ref.at[pl.ds(part * half, half)], kept_v.at[2 + part], load_sem.at[2 + part]
                )
                for part in (0, 1)
            ]
            finals.append(
                pltpu.make_async_copy(grads_ref.at[pl.ds(0, 2 * half)], rows_v, load_sem.at[4])
            )
            for copy in finals:
                copy.start()
    for copy in finals:
        copy.wait()
    vector_ref[...] = jnp.zeros_like(vector_ref)
    chunk = min(32, half)
    results = []
    for part in (0, 1):
        for j in links.given(0):
            sums[(j, part)].wait_recv()

        def last(step, _, part=part):
            at = pl.ds(pl.multiple_of(step * chunk, chunk), chunk)
            to = pl.ds(pl.multiple_of(part * half + step * chunk, chunk), chunk)
            second = kept_v[part, at, :]
            for j in links.given(0):
                second = second + recv_v[links.slot[(j, part)], at, :].astype(F32)
            normed, spread = normalize(kept_v[2 + part, at, :])
            incoming = rows_v[to, :].astype(F32)
            back = incoming + norm_back(second * table_ref[2:3, :], normed, spread)
            branch = back.astype(BF16)
            kept_v[part, at, :] = back
            rows_v[to, :] = branch
            for n, value in enumerate((second * normed, second, branch.astype(F32), incoming)):
                vector_ref[n : n + 1, :] += jnp.sum(value, axis=0, keepdims=True)
            return 0

        lax.fori_loop(0, half // chunk, last, 0)
        rows = pl.ds(part * half, half)
        for n, (source, target) in enumerate(
            ((kept_v.at[part], back_ref.at[rows]), (rows_v.at[rows], branch_ref.at[rows]))
        ):
            copy = pltpu.make_async_copy(source, target, load_sem.at[2 * part + n])
            copy.start()
            results.append(copy)
    for end in ends:
        end()
    for copy in results:
        copy.wait()
    for copy in swaps:
        copy.wait_send()
    for pair in links.pairs:
        shares[pair].wait_send()
        sums[pair].wait_send()


def feed_forward(own, grads, both_weights, shift, residual, table, count):
    rows, width = own.shape
    hidden = both_weights.shape[1]
    length = rows * count
    links = Links(count, rows // 2)
    half, copies = links.half, len(links.pairs)
    anywhere = pl.BlockSpec(memory_space=pl.ANY)
    inside = pl.BlockSpec(memory_space=pltpu.VMEM)
    dma = pltpu.SemaphoreType.DMA
    return pl.pallas_call(
        functools.partial(feed_forward_kernel, links),
        out_shape=(
            jax.ShapeDtypeStruct((length, width), BF16),
            jax.ShapeDtypeStruct((length, hidden), BF16),
            jax.ShapeDtypeStruct((length, hidden), BF16),
            jax.ShapeDtypeStruct((width, hidden), BF16),
            jax.ShapeDtypeStruct((rows, width), F32),
            jax.ShapeDtypeStruct((rows, width), BF16),
            jax.ShapeDtypeStruct((8, width), F32),
            jax.ShapeDtypeStruct((1, hidden), F32),
            jax.ShapeDtypeStruct((width, hidden), BF16),
        ),
        in_specs=[anywhere, anywhere, anywhere, inside, anywhere, inside],
        out_specs=(anywhere,) * 6 + (inside, inside, anywhere),
        scratch_shapes=[
            pltpu.VMEM((max(width, length), max(width, hidden)), BF16),
            pltpu.VMEM((max(width, length), hidden), BF16),
            pltpu.VMEM((rows, width), BF16),
            pltpu.VMEM((rows, width), BF16),
            pltpu.VMEM((rows, hidden), BF16),
            pltpu.VMEM((rows, hidden), BF16),
            pltpu.VMEM((count, half, width), F32),
            pltpu.VMEM((copies, half, width), BF16),
            pltpu.VMEM((copies, half, width), BF16),
            pltpu.VMEM((width, hidden // 2), BF16),
            pltpu.VMEM((2, width, hidden // 2), BF16),
            dma((10,)),
            dma((5,)),
            dma((2,)),
            dma((2,)),
            dma((2, width // 256)),
            dma((2, width // 256)),
            dma((2, width // 256)),
            dma((copies,)),
            dma((copies,)),
            dma((copies,)),
            dma((copies,)),
        ],
        compiler_params=pltpu.CompilerParams(
            collective_id=3, has_side_effects=True, vmem_limit_bytes=63 * 1024 * 1024
        ),
        cost_estimate=pl.CostEstimate(
            flops=10 * length * width * hidden,
            bytes_accessed=length * width * 8 + width * hidden * 4 + length * hidden * 4,
            transcendentals=length * hidden * 2,
        ),
        name="feed_forward",
    )(own, grads, both_weights, shift, residual, table)


def front_kernel(
    links,
    own_ref,
    pieces_ref,
    table_ref,
    normed_ref,
    block_ref,
    rows_v,
    normed_v,
    load_sem,
    store_sem,
    share_send,
    share_recv,
    piece_send,
    piece_recv,
):
    count, half = links.count, links.half
    size = 2 * half
    here = lax.axis_index("ctx")
    links.greet(masks=range(1, count))
    shares = links.sharing(own_ref, rows_v, share_send, share_recv)
    links.pass_on(shares, 0)
    pieces = [
        pltpu.make_async_remote_copy(
            src_ref=pieces_ref.at[lax.bitwise_xor(here, mask)],
            dst_ref=block_ref.at[here],
            send_sem=piece_send.at[mask - 1],
            recv_sem=piece_recv.at[mask - 1],
            device_id={"ctx": lax.bitwise_xor(here, mask)},
            device_id_type=MESH,
        )
        for mask in range(1, count)
    ]
    for copy in pieces:
        copy.start()
    kept = pltpu.make_async_copy(pieces_ref.at[here], block_ref.at[here], load_sem.at[0])
    kept.start()
    first = pltpu.make_async_copy(own_ref, rows_v.at[pl.ds(0, size)], load_sem.at[1])
    first.start()
    chunk = min(32, half)
    stores = []
    for i in range(count):
        if i == 0:
            first.wait()
        else:
            for part in (0, 1):
                shares[(i, part)].wait_recv()
            links.pass_on(shares, i)
        for part in (0, 1):
            base = links.start_row(i, part)

            def norm(step, _, base=base):
                at = pl.ds(pl.multiple_of(base + step * chunk, chunk), chunk)
                normed = normalize(rows_v[at, :].astype(F32))[0]
                normed_v[at, :] = (normed * table_ref[0:1, :] + table_ref[1:2, :]).astype(BF16)
                return 0

            lax.fori_loop(0, half // chunk, norm, 0)
            store = pltpu.make_async_copy(
                links.rows(normed_v, i, part), links.rows(normed_ref, i, part), store_sem.at[2 * i + part]
            )
            store.start()
            stores.append(store)
    kept.wait()
    for copy in stores:
        copy.wait()
    for copy in pieces:
        copy.wait()
    for pair in links.pairs:
        shares[pair].wait_send()


def front(own, pieces, table, count):
    rows, width = own.shape
    length = rows * count
    links = Links(count, rows // 2)
    copies = len(links.pairs)
    anywhere = pl.BlockSpec(memory_space=pl.ANY)
    dma = pltpu.SemaphoreType.DMA
    return pl.pallas_call(
        functools.partial(front_kernel, links),
        out_shape=(
            jax.ShapeDtypeStruct((length, width), BF16),
            jax.ShapeDtypeStruct(pieces.shape, BF16),
        ),
        in_specs=[anywhere, anywhere, pl.BlockSpec(memory_space=pltpu.VMEM)],
        out_specs=(anywhere, anywhere),
        scratch_shapes=[
            pltpu.VMEM((length, width), BF16),
            pltpu.VMEM((length, width), BF16),
            dma((2,)),
            dma((2 * count,)),
            dma((copies,)),
            dma((copies,)),
            dma((count - 1,)),
            dma((count - 1,)),
        ],
        compiler_params=pltpu.CompilerParams(
            collective_id=1, has_side_effects=True, vmem_limit_bytes=40 * 1024 * 1024
        ),
        cost_estimate=pl.CostEstimate(
            flops=20 * length * width, bytes_accessed=120000000, transcendentals=0
        ),
        name="front",
    )(own, pieces, table)


def attend_kernel(
    links,
    heads,
    rows_ref,
    weight_ref,
    shift_ref,
    grads_ref,
    own_ref,
    table_ref,
    qkv_ref,
    mixed_ref,
    log_ref,
    grads_full_ref,
    residual_ref,
    second_ref,
    whole_ref,
    rows_v,
    weight_v,
    qkv_v,
    mixed_v,
    scores_v,
    kept_v,
    send_v,
    recv_v,
    load_sem,
    store_sem,
    pair_send,
    pair_recv,
    share_send,
    share_recv,
    sum_send,
    sum_recv,
):
    count, half = links.count, links.half
    size = 2 * half
    here = lax.axis_index("ctx")
    partner = {"tp": 1 - lax.axis_index("tp")}
    narrow = weight_ref.shape[1]
    wide = heads * 3 * HEAD_DIM // 2
    links.greet([partner])
    theirs = pltpu.make_async_remote_copy(
        src_ref=weight_ref,
        dst_ref=weight_v.at[1],
        send_sem=pair_send.at[0],
        recv_sem=pair_recv.at[0],
        device_id=partner,
        device_id_type=MESH,
    )
    theirs.start()
    shares = links.sharing(grads_ref, grads_full_ref, share_send, share_recv)
    sums = links.summing(send_v, recv_v, sum_send, sum_recv)
    links.pass_on(shares, 0)
    ours = pltpu.make_async_copy(weight_ref, weight_v.at[0], load_sem.at[0])
    ours.start()
    keep = pltpu.make_async_copy(grads_ref, grads_full_ref.at[pl.ds(0, size)], load_sem.at[1])
    keep.start()

    def load(n):
        return pltpu.make_async_copy(
            rows_ref.at[pl.ds(n * size, size)], rows_v.at[n % 2], load_sem.at[2 + n % 2]
        )

    coming = load(0)
    coming.start()
    ours.wait()
    theirs.wait_recv()
    wholes = []
    for core in (0, 1):
        copy = pltpu.make_async_copy(weight_v.at[core], whole_ref.at[core], store_sem.at[core])
        copy.start()
        wholes.append(copy)
    tile = 256 if wide % 256 == 0 else HEAD_DIM
    for n in range(count):
        coming.wait()
        if n + 1 < count:
            coming = load(n + 1)
            coming.start()
        for core in (0, 1):

            def step(m, _, n=n, core=core):
                at = pl.ds(pl.multiple_of(m * tile, tile), tile)
                to = pl.ds(pl.multiple_of(core * wide + m * tile, tile), tile)
                value = product(rows_v[n % 2], weight_v[core, :, at]) + shift_ref[0:1, to]
                qkv_v[n * size : (n + 1) * size, to] = value.astype(BF16)
                return 0

            lax.fori_loop(0, wide // tile, step, 0)
    keep_qkv = pltpu.make_async_copy(qkv_v, qkv_ref, store_sem.at[2])
    keep_qkv.start()

    def one_head(head, _):
        @pl.when(head == heads // 2)
        def _():
            for i in range(1, (count + 1) // 2):
                for part in (0, 1):
                    shares[(i, part)].wait_recv()
                links.pass_on(shares, i)

        attend_forward_head(here, head, size, count, qkv_v, mixed_v, log_ref, scores_v)
        return 0

    lax.fori_loop(0, heads, one_head, 0)
    keep_mixed = pltpu.make_async_copy(mixed_v, mixed_ref, store_sem.at[3])
    keep_mixed.start()
    chip = heads * HEAD_DIM // 2
    for i in range(count - 1, -1, -1):

        def out_rows(core, i=i):
            at = slice(core * chip, (core + 1) * chip)
            first = [links.start_row(i, part) for part in (0, 1)]
            return jnp.concatenate([mixed_v[row : row + half, at] for row in first], axis=0)

        links.terms(
            i,
            lambda at: across(out_rows(0), weight_v[0, at, wide:narrow])
            + across(out_rows(1), weight_v[1, at, wide:narrow]),
            residual_ref.shape[1],
            kept_v,
            send_v,
        )
        if i >= count // 2:
            for part in (0, 1):
                sums[(i, part)].start()
    links.combine(sums, kept_v, send_v, recv_v, residual_ref, count // 2 - 1, 0)
    chunk = min(32, half)

    def norm(step, _):
        at = pl.ds(pl.multiple_of(step * chunk, chunk), chunk)
        residual = own_ref[at, :].astype(F32) + (residual_ref[at, :] + table_ref[4:5, :])
        residual_ref[at, :] = residual
        normed = normalize(residual)[0]
        second_ref[at, :] = (normed * table_ref[2:3, :] + table_ref[3:4, :]).astype(BF16)
        return 0

    lax.fori_loop(0, size // chunk, norm, 0)
    for i in range(1, count):
        for part in (0, 1):
            if i >= (count + 1) // 2:
                shares[(i, part)].wait_recv()
    for copy in wholes + [keep_qkv, keep_mixed, keep]:
        copy.wait()
    theirs.wait_send()
    for pair in links.pairs:
        sums[pair].wait_send()
        shares[pair].wait_send()


def attend_forward_head(here, head, size, blocks, qkv_v, mixed_v, log_ref, scores_v):
    scaling = HEAD_DIM ** (-0.5)
    behind = lax.broadcasted_iota(jnp.int32, (size, size), 1) <= lax.broadcasted_iota(
        jnp.int32, (size, size), 0
    )
    column = pl.multiple_of(head * (3 * HEAD_DIM), HEAD_DIM)
    query_at = pl.ds(column, HEAD_DIM)
    key_at = pl.ds(pl.multiple_of(column + HEAD_DIM, HEAD_DIM), HEAD_DIM)
    value_at = pl.ds(pl.multiple_of(column + 2 * HEAD_DIM, HEAD_DIM), HEAD_DIM)
    head_at = pl.ds(pl.multiple_of(head * HEAD_DIM, HEAD_DIM), HEAD_DIM)
    for i in range(blocks):
        at = pl.ds(rows_of(here, i, size), size)
        queries = qkv_v[at, query_at]
        highest = jnp.full((size, 1), NEGATIVE, F32)
        for j in range(i + 1):
            keys = qkv_v[pl.ds(rows_of(here, j, size), size), key_at]
            scores = across(queries, keys) * scaling
            if j == i:
                scores = jnp.where(behind, scores, NEGATIVE)
            scores_v[:, j * size : (j + 1) * size] = scores
            highest = jnp.maximum(highest, jnp.max(scores, axis=1, keepdims=True))
        row_total = jnp.zeros((size, 1), F32)
        mixed = jnp.zeros((size, HEAD_DIM), F32)
        for j in range(i + 1):
            exponent = jnp.exp(scores_v[:, j * size : (j + 1) * size] - highest)
            row_total = row_total + jnp.sum(exponent, axis=1, keepdims=True)
            values = qkv_v[pl.ds(rows_of(here, j, size), size), value_at]
            mixed = mixed + product(exponent.astype(BF16), values)
        mixed_v[at, head_at] = (mixed / row_total).astype(BF16)
        log_total = jnp.broadcast_to(highest + jnp.log(row_total), (size, HEAD_DIM))
        log_ref[head, :, at] = log_total.T[0:8, :]


def attend(rows, weight, shift, grads, own, table, heads, count):
    length, width = rows.shape
    size = length // count
    narrow = weight.shape[1]
    columns = heads * 3 * HEAD_DIM
    links = Links(count, size // 2)
    half, copies = links.half, len(links.pairs)
    pairs = heads * length * (length + size) // 2
    anywhere = pl.BlockSpec(memory_space=pl.ANY)
    inside = pl.BlockSpec(memory_space=pltpu.VMEM)
    dma = pltpu.SemaphoreType.DMA
    return pl.pallas_call(
        functools.partial(attend_kernel, links, heads),
        out_shape=(
            jax.ShapeDtypeStruct((length, columns), BF16),
            jax.ShapeDtypeStruct((length, heads * HEAD_DIM), BF16),
            jax.ShapeDtypeStruct((heads, 8, length), F32),
            jax.ShapeDtypeStruct((length, width), BF16),
            jax.ShapeDtypeStruct((size, width), F32),
            jax.ShapeDtypeStruct((size, width), BF16),
            jax.ShapeDtypeStruct((2, width, narrow), BF16),
        ),
        in_specs=[anywhere, anywhere, inside, anywhere, inside, inside],
        out_specs=(anywhere, anywhere, inside, anywhere, inside, inside, anywhere),
        scratch_shapes=[
            pltpu.VMEM((2, size, width), BF16),
            pltpu.VMEM((2, width, narrow), BF16),
            pltpu.VMEM((length, columns), BF16),
            pltpu.VMEM((length, heads * HEAD_DIM), BF16),
            pltpu.VMEM((size, length), F32),
            pltpu.VMEM((count, half, width), F32),
            pltpu.VMEM((copies, half, width), BF16),
            pltpu.VMEM((copies, half, width), BF16),
            dma((4,)),
            dma((4,)),
            dma((1,)),
            dma((1,)),
            dma((copies,)),
            dma((copies,)),
            dma((copies,)),
            dma((copies,)),
        ],
        compiler_params=pltpu.CompilerParams(
            collective_id=2, has_side_effects=True, vmem_limit_bytes=60 * 1024 * 1024
        ),
        cost_estimate=pl.CostEstimate(
            flops=pairs * HEAD_DIM * 8 + 2 * length * width * heads * HEAD_DIM * 4,
            bytes_accessed=length * width * 8,
            transcendentals=pairs,
        ),
        name="attend",
    )(rows, weight, shift, grads, own, table)


def attend_back_kernel(
    links,
    heads,
    own_ref,
    weight_ref,
    qkv_ref,
    mixed_ref,
    log_ref,
    hid_ref,
    fall_ref,
    first_ref,
    full_ref,
    result_ref,
    sum_ref,
    head_grad_ref,
    weight_v,
    qkv_v,
    mixed_v,
    big_v,
    theirs_v,
    came_v,
    grad_v,
    rows_v,
    hid_v,
    fall_v,
    key_v,
    value_v,
    kept_v,
    send_v,
    recv_v,
    load_sem,
    grad_send,
    grad_recv,
    grad_store,
    share_send,
    share_recv,
    sum_send,
    sum_recv,
):
    half, count = links.half, links.count
    size = 2 * half
    here = lax.axis_index("ctx")
    chip = weight_v.shape[2]
    wide = heads * 3 * HEAD_DIM // 2
    partner = {"tp": 1 - lax.axis_index("tp")}
    links.greet([partner])
    shares = links.sharing(own_ref, full_ref, share_send, share_recv)
    sums = links.summing(send_v, recv_v, sum_send, sum_recv)
    links.pass_on(shares, 0)
    narrow = fall_v.shape[0]
    loads = [
        pltpu.make_async_copy(source, target, load_sem.at[n])
        for n, (source, target) in enumerate(
            (
                (fall_ref.at[pl.ds(0, narrow)], fall_v),
                (own_ref, rows_v),
                (weight_ref.at[:, :, pl.ds(weight_ref.shape[2] - chip, chip)], weight_v),
                (qkv_ref, qkv_v),
                (mixed_ref, mixed_v),
                (own_ref, full_ref.at[pl.ds(0, size)]),
                (first_ref, big_v),
            )
        )
    ]
    for copy in loads:
        copy.start()
    loads[0].wait()
    out_terms(links, hid_ref, hid_v, fall_v, kept_v, send_v, load_sem, 7)
    for i in range(count):
        if i == 0:
            loads[1].wait()
            loads[2].wait()
        else:
            for part in (0, 1):
                shares[(i, part)].wait_recv()
            links.pass_on(shares, i)
            unit_loads = links.loads(full_ref, rows_v, i, load_sem, 7)
            for copy in unit_loads:
                copy.start()
            for copy in unit_loads:
                copy.wait()
        for core in (0, 1):
            term = product(rows_v[...], weight_v[core]).astype(BF16)
            for part in (0, 1):
                first = links.start_row(i, part)
                grad_v[first : first + half, core * chip : (core + 1) * chip] = term[
                    part * half : (part + 1) * half
                ]
    for i in range(count - 1, count // 2 - 1, -1):
        for part in (0, 1):
            sums[(i, part)].start()
    loads[3].wait()
    loads[4].wait()

    def one_head(head, _):
        @pl.when(head == heads // 2)
        def _():
            links.combine(sums, kept_v, send_v, recv_v, None, count // 2 - 1, 1)

        attend_backward_head(
            here, head, size, count, qkv_v, grad_v, mixed_v, log_ref, result_ref, key_v, value_v
        )
        return 0

    lax.fori_loop(0, heads, one_head, 0)
    loads[5].wait()
    loads[6].wait()
    end_first = weight_grads(
        partner,
        big_v,
        result_ref,
        theirs_v.at[:, pl.ds(0, wide)],
        came_v.at[:, pl.ds(0, wide)],
        head_grad_ref.at[:, pl.ds(0, wide)],
        grad_send.at[0],
        grad_recv.at[0],
        grad_store.at[0],
    )
    again = pltpu.make_async_copy(full_ref, big_v, load_sem.at[6])
    again.start()
    links.combine(sums, kept_v, send_v, recv_v, sum_ref, 0, 0)
    again.wait()
    end_second = weight_grads(
        partner,
        big_v,
        mixed_v,
        theirs_v.at[:, pl.ds(wide, chip)],
        came_v.at[:, pl.ds(wide, chip)],
        head_grad_ref.at[:, pl.ds(wide, chip)],
        grad_send.at[1],
        grad_recv.at[1],
        grad_store.at[1],
    )
    end_first()
    end_second()
    for pair in links.pairs:
        sums[pair].wait_send()
        shares[pair].wait_send()


def out_terms(links, hid_ref, hid_v, fall_v, kept_v, send_v, load_sem, base):
    count, half = links.count, links.half
    order = list(range(count - 1, -1, -1))
    unit_loads = links.loads(hid_ref, hid_v.at[0], order[0], load_sem, base)
    for copy in unit_loads:
        copy.start()
    for n, i in enumerate(order):
        for copy in unit_loads:
            copy.wait()
        if n + 1 < count:
            unit_loads = links.loads(
                hid_ref, hid_v.at[(n + 1) % 2], order[n + 1], load_sem, base + 2 * ((n + 1) % 2)
            )
            for copy in unit_loads:
                copy.start()
        links.terms(
            i, lambda at, n=n: across(hid_v[n % 2], fall_v[at, :]), fall_v.shape[0], kept_v, send_v
        )


def attend_backward_head(
    here, head, size, blocks, qkv_v, grad_v, mixed_v, log_ref, result_ref, key_v, value_v
):
    scaling = HEAD_DIM ** (-0.5)
    behind = lax.broadcasted_iota(jnp.int32, (size, size), 0) <= lax.broadcasted_iota(
        jnp.int32, (size, size), 1
    )
    column = pl.multiple_of(head * (3 * HEAD_DIM), HEAD_DIM)
    query_at = pl.ds(column, HEAD_DIM)
    key_at = pl.ds(pl.multiple_of(column + HEAD_DIM, HEAD_DIM), HEAD_DIM)
    value_at = pl.ds(pl.multiple_of(column + 2 * HEAD_DIM, HEAD_DIM), HEAD_DIM)
    head_at = pl.ds(pl.multiple_of(head * HEAD_DIM, HEAD_DIM), HEAD_DIM)
    for i in range(blocks):
        at = pl.ds(rows_of(here, i, size), size)
        queries = qkv_v[at, query_at]
        grads = grad_v[at, head_at]
        both = grads.astype(F32) * mixed_v[at, head_at].astype(F32)
        centre = jnp.sum(both.T, axis=0, keepdims=True)
        log_total = log_ref[head, 0:1, at]
        query_grad = jnp.zeros((size, HEAD_DIM), F32)
        for j in range(i + 1):
            there = pl.ds(rows_of(here, j, size), size)
            keys = qkv_v[there, key_at]
            values = qkv_v[there, value_at]
            weights = jnp.exp(across(keys, queries) * scaling - log_total)
            if j == i:
                weights = jnp.where(behind, weights, 0.0)
            slopes = (weights * (across(values, grads) - centre)).astype(BF16)
            value_term = product(weights.astype(BF16), grads)
            key_term = product(slopes, queries)
            query_grad = query_grad + inner(slopes, keys)
            place = slice(j * size, (j + 1) * size)
            if i == j:
                value_v[place, :] = value_term
                key_v[place, :] = key_term
            else:
                value_v[place, :] += value_term
                key_v[place, :] += key_term
        result_ref[at, query_at] = (query_grad * scaling).astype(BF16)
    for j in range(blocks):
        there = pl.ds(rows_of(here, j, size), size)
        place = slice(j * size, (j + 1) * size)
        result_ref[there, key_at] = (key_v[place, :] * scaling).astype(BF16)
        result_ref[there, value_at] = value_v[place, :].astype(BF16)


def attend_back(own, weight, qkv, mixed, log_total, hid, fall_weight, first, count):
    rows, width = own.shape
    length, columns = qkv.shape
    heads = columns // (3 * HEAD_DIM)
    hidden = hid.shape[1]
    links = Links(count, rows // 2)
    half, copies = links.half, len(links.pairs)
    narrow = width // 2
    pairs = heads * length * (length + rows) // 2
    anywhere = pl.BlockSpec(memory_space=pl.ANY)
    inside = pl.BlockSpec(memory_space=pltpu.VMEM)
    dma = pltpu.SemaphoreType.DMA
    return pl.pallas_call(
        functools.partial(attend_back_kernel, links, heads),
        out_shape=(
            jax.ShapeDtypeStruct((length, width), BF16),
            jax.ShapeDtypeStruct((length, columns), BF16),
            jax.ShapeDtypeStruct((rows, narrow), F32),
            jax.ShapeDtypeStruct((width, 2 * heads * HEAD_DIM), BF16),
        ),
        in_specs=[anywhere] * 4 + [inside, anywhere, anywhere, anywhere],
        out_specs=(anywhere, inside, inside, anywhere),
        scratch_shapes=[
            pltpu.VMEM((2, width, heads * HEAD_DIM // 2), BF16),
            pltpu.VMEM(qkv.shape, BF16),
            pltpu.VMEM(mixed.shape, BF16),
            pltpu.VMEM((length, width), BF16),
            pltpu.VMEM((width, 2 * heads * HEAD_DIM), BF16),
            pltpu.VMEM((width, 2 * heads * HEAD_DIM), BF16),
            pltpu.VMEM(mixed.shape, BF16),
            pltpu.VMEM((rows, width), BF16),
            pltpu.VMEM((2, rows, hidden), BF16),
            pltpu.VMEM((narrow, hidden), BF16),
            pltpu.VMEM((length, HEAD_DIM), F32),
            pltpu.VMEM((length, HEAD_DIM), F32),
            pltpu.VMEM((count, half, narrow), F32),
            pltpu.VMEM((copies, half, narrow), BF16),
            pltpu.VMEM((copies, half, narrow), BF16),
            dma((11,)),
            dma((2, width // 256)),
            dma((2, width // 256)),
            dma((2, width // 256)),
            dma((copies,)),
            dma((copies,)),
            dma((copies,)),
            dma((copies,)),
        ],
        compiler_params=pltpu.CompilerParams(
            collective_id=4, has_side_effects=True, vmem_limit_bytes=63 * 1024 * 1024
        ),
        cost_estimate=pl.CostEstimate(
            flops=pairs * HEAD_DIM * 20 + 2 * length * width * (heads * HEAD_DIM + hidden // 2),
            bytes_accessed=length * width * 6 + length * columns * 4 + length * hidden * 2,
            transcendentals=pairs,
        ),
        name="attend_back",
    )(own, weight, qkv, mixed, log_total, hid, fall_weight, first)


def first_back_kernel(
    links,
    grads_ref,
    weight_ref,
    hid_ref,
    fall_ref,
    first_ref,
    sum_ref,
    grads_v,
    weight_v,
    hid_v,
    fall_v,
    kept_v,
    send_v,
    recv_v,
    kept_w,
    send_w,
    recv_w,
    load_sem,
    sum_send,
    sum_recv,
    late_send,
    late_recv,
):
    count, half = links.count, links.half
    wide = weight_v.shape[2]
    links.greet()
    sums = links.summing(send_v, recv_v, sum_send, sum_recv)
    lates = links.summing(send_w, recv_w, late_send, late_recv)
    narrow = fall_v.shape[0]
    loads = [
        pltpu.make_async_copy(source, target, load_sem.at[n])
        for n, (source, target) in enumerate(
            (
                (weight_ref.at[:, :, pl.ds(0, wide)], weight_v),
                (fall_ref.at[pl.ds(fall_ref.shape[0] - narrow, narrow)], fall_v),
            )
        )
    ]
    for copy in loads:
        copy.start()
    order = list(range(count - 1, -1, -1))
    unit_loads = links.loads(grads_ref, grads_v.at[0], order[0], load_sem, 2)
    for copy in unit_loads:
        copy.start()
    loads[0].wait()
    for n, i in enumerate(order):
        for copy in unit_loads:
            copy.wait()
        if n + 1 < count:
            unit_loads = links.loads(
                grads_ref, grads_v.at[(n + 1) % 2], order[n + 1], load_sem, 2 + 2 * ((n + 1) % 2)
            )
            for copy in unit_loads:
                copy.start()
        links.terms(
            i,
            lambda at, n=n: across(grads_v[n % 2, :, :wide], weight_v[0, at, :])
            + across(grads_v[n % 2, :, wide:], weight_v[1, at, :]),
            weight_v.shape[1],
            kept_v,
            send_v,
        )
        if i >= count // 2:
            for part in (0, 1):
                sums[(i, part)].start()
    loads[1].wait()
    out_terms(links, hid_ref, hid_v, fall_v, kept_w, send_w, load_sem, 6)
    links.combine(sums, kept_v, send_v, recv_v, None, count // 2 - 1, 1)
    for i in range(count - 1, count // 2 - 1, -1):
        for part in (0, 1):
            lates[(i, part)].start()
    links.combine(sums, kept_v, send_v, recv_v, first_ref, 0, 0)
    links.combine(lates, kept_w, send_w, recv_w, sum_ref, count // 2 - 1, 0)
    for pair in links.pairs:
        sums[pair].wait_send()
        lates[pair].wait_send()


def first_back(grads, weight, hid, fall_weight, count):
    length, columns = grads.shape
    width, hidden = fall_weight.shape
    rows = length // count
    links = Links(count, rows // 2)
    half, copies = links.half, len(links.pairs)
    narrow = width // 2
    anywhere = pl.BlockSpec(memory_space=pl.ANY)
    inside = pl.BlockSpec(memory_space=pltpu.VMEM)
    dma = pltpu.SemaphoreType.DMA
    return pl.pallas_call(
        functools.partial(first_back_kernel, links),
        out_shape=(
            jax.ShapeDtypeStruct((rows, width), F32),
            jax.ShapeDtypeStruct((rows, narrow), F32),
        ),
        in_specs=[anywhere] * 4,
        out_specs=(inside, inside),
        scratch_shapes=[
            pltpu.VMEM((2, rows, columns), BF16),
            pltpu.VMEM((2, width, columns // 2), BF16),
            pltpu.VMEM((2, rows, hidden), BF16),
            pltpu.VMEM((narrow, hidden), BF16),
            pltpu.VMEM((count, half, width), F32),
            pltpu.VMEM((copies, half, width), BF16),
            pltpu.VMEM((copies, half, width), BF16),
            pltpu.VMEM((count, half, narrow), F32),
            pltpu.VMEM((copies, half, narrow), BF16),
            pltpu.VMEM((copies, half, narrow), BF16),
            dma((10,)),
            dma((copies,)),
            dma((copies,)),
            dma((copies,)),
            dma((copies,)),
        ],
        compiler_params=pltpu.CompilerParams(
            collective_id=5, has_side_effects=True, vmem_limit_bytes=58 * 1024 * 1024
        ),
        cost_estimate=pl.CostEstimate(
            flops=2 * length * width * (columns + hidden // 2),
            bytes_accessed=length * columns * 2 + length * hidden * 2 + width * (columns + hidden) * 2,
            transcendentals=0,
        ),
        name="first_back",
    )(grads, weight, hid, fall_weight)


def body(
    tokens,
    cotangent,
    attention_gain,
    attention_bias,
    feedforward_gain,
    feedforward_bias,
    query_weight,
    query_bias,
    key_weight,
    value_weight,
    value_bias,
    output_weight,
    output_bias,
    up_weight,
    up_bias,
    down_weight,
    down_bias,
):
    _, local_rows, model_width = tokens.shape
    ctx, dp = lax.axis_size("ctx"), lax.axis_size("dp")
    here, core = lax.axis_index("ctx"), lax.axis_index("tp")
    shard = lax.axis_index("dp") * ctx + here
    thin = query_weight.shape[0]
    heads = query_weight.shape[1] // (HEAD_DIM * ctx)
    hidden = up_weight.shape[1] // ctx
    inputs = lax.dynamic_index_in_dim(tokens, core, 0, keepdims=False)
    incoming = lax.dynamic_index_in_dim(cotangent, core, 0, keepdims=False)

    packed = jnp.stack(
        [w.reshape(thin, ctx, heads, HEAD_DIM) for w in (query_weight, key_weight, value_weight)],
        axis=3,
    ).reshape(thin, ctx, heads * 3 * HEAD_DIM)
    head_pieces = jnp.concatenate(
        [
            packed.transpose(1, 0, 2),
            output_weight.reshape(ctx, heads * HEAD_DIM, thin).transpose(0, 2, 1),
        ],
        axis=2,
    )
    hidden_pieces = jnp.concatenate(
        [
            down_weight.reshape(ctx, hidden, thin).transpose(0, 2, 1),
            up_weight.reshape(thin, ctx, hidden).transpose(1, 0, 2),
        ],
        axis=2,
    )
    head_block = exchange(head_pieces).reshape(ctx * thin, -1)
    head_weights = lax.all_gather(head_block, "dp", axis=0, tiled=True)

    small = jnp.stack(
        [attention_gain, attention_bias, feedforward_gain, feedforward_bias, output_bias, down_bias]
    ).astype(F32)
    small = jnp.concatenate([small, jnp.zeros((2, thin), F32)])
    table = jnp.zeros((8, model_width), F32)
    table = lax.dynamic_update_slice(table, small, (0, shard * thin))
    table = summed(table, ("dp", "ctx"))
    gain_one, shift_one, gain_two, shift_two, output_shift, down_shift = [
        table[n : n + 1] for n in range(6)
    ]

    def own_columns(vector):
        return lax.dynamic_index_in_dim(vector.reshape(ctx, -1), here, 0, keepdims=False)

    query_shift = own_columns(query_bias).reshape(heads, HEAD_DIM)
    value_shift = own_columns(value_bias).reshape(heads, HEAD_DIM)
    qkv_shift = jnp.stack([query_shift, jnp.zeros_like(query_shift), value_shift], axis=1)
    shifts = jnp.concatenate([qkv_shift.reshape(-1), own_columns(up_bias)])
    other_shifts = swap(shifts, "tp", 1)
    wide = heads * 3 * HEAD_DIM
    qkv_shift = jnp.concatenate([shifts[:wide], other_shifts[:wide]]).astype(F32)
    rise_shift = jnp.concatenate([shifts[wide:], other_shifts[wide:]]).astype(F32)

    wide_inputs = inputs.astype(F32)
    normed_one, spread_one = normalize(wide_inputs)
    ones, hidden_block = front(after(inputs, head_block), hidden_pieces, table, ctx)
    hidden_weights = lax.all_gather(
        hidden_block.reshape(ctx * thin, -1), "dp", axis=0, tiled=True
    )
    qkv, mixed, log_total, grads_in, residual, input_two, head_whole = attend(
        ones, head_weights, qkv_shift[None], incoming, inputs, table, 2 * heads, ctx
    )
    _, all_hid, _, hidden_both, residual_grad, branch_grad, vectors, rise_bias, fall_weight = (
        feed_forward(input_two, grads_in, hidden_weights, rise_shift[None], residual, table, ctx)
    )
    hidden_rows = over_dp(hidden_both)

    _, qkv_grads, low_columns, head_both = attend_back(
        branch_grad, head_whole, qkv, mixed, log_total, all_hid, fall_weight, ones, ctx
    )
    qkv_bias = jnp.sum(qkv_grads.astype(F32), axis=0)
    head_both = after(head_both, hidden_rows)
    late_grads = after(qkv_grads, head_both)
    first_grad, high_columns = first_back(late_grads, head_whole, all_hid, fall_weight, ctx)
    block_out = residual + (jnp.concatenate([low_columns, high_columns], axis=1) + down_shift)
    own_out = block_out.astype(BF16)
    late_both = head_both
    width = hidden
    hidden_grad = to_shards(hidden_rows)
    fall_grad, rise_grad = hidden_grad[:, :, :width], hidden_grad[:, :, width:]
    late_grad = to_shards(over_dp(late_both))
    qkv_grad, out_grad = late_grad[:, :, :wide], late_grad[:, :, wide:]
    gain_one_sum = jnp.sum(first_grad * normed_one, axis=0)
    bias_one_sum = jnp.sum(first_grad, axis=0)
    token_grad = residual_grad + norm_back(first_grad * gain_one, normed_one, spread_one)
    own_grad = token_grad.astype(BF16)

    def both_sequences(own):
        other = swap(own, "tp", 1)
        first = core == 0
        return jnp.stack([jnp.where(first, own, other), jnp.where(first, other, own)])

    def spread_columns(vector):
        own, other = jnp.split(vector, 2)
        whole = jnp.zeros((2, ctx, own.shape[0]), F32)
        whole = lax.dynamic_update_slice(whole, own[None, None], (core, here, 0))
        return lax.dynamic_update_slice(whole, other[None, None], (1 - core, here, 0))

    everywhere = ("tp", "ctx", "dp")
    early = vectors[:4]
    features = jnp.concatenate(
        [
            summed(jnp.stack([gain_one_sum, bias_one_sum]), everywhere),
            summed(early, everywhere),
        ]
    )
    qkv_bias = summed(spread_columns(qkv_bias), everywhere)
    rise_bias = summed(spread_columns(rise_bias[0]), everywhere)
    features = lax.dynamic_slice(features, (0, shard * thin), (6, thin))
    qkv_bias = lax.dynamic_index_in_dim(qkv_bias, core, 0, keepdims=False)
    qkv_bias = qkv_bias.reshape(ctx * heads, 3, HEAD_DIM)
    rise_bias = lax.dynamic_index_in_dim(rise_bias, core, 0, keepdims=False).reshape(-1)

    qkv_grad = qkv_grad.reshape(ctx, thin, heads, 3, HEAD_DIM).transpose(3, 1, 0, 2, 4)
    qkv_grad = qkv_grad.reshape(3, thin, ctx * heads * HEAD_DIM).astype(F32)
    return (
        both_sequences(own_out),
        both_sequences(own_grad),
        features[0],
        features[1],
        features[2],
        features[3],
        qkv_grad[0],
        qkv_bias[:, 0].reshape(-1),
        qkv_grad[1],
        qkv_grad[2],
        qkv_bias[:, 2].reshape(-1),
        out_grad.transpose(0, 2, 1).reshape(-1, thin).astype(F32),
        features[4],
        rise_grad.transpose(1, 0, 2).reshape(thin, -1).astype(F32),
        rise_bias,
        fall_grad.transpose(0, 2, 1).reshape(-1, thin).astype(F32),
        features[5],
    )


def solution(mesh):
    placed = (
        P("dp", "ctx", None),
        P("dp", "ctx", None),
        P(("dp", "ctx")),
        P(("dp", "ctx")),
        P(("dp", "ctx")),
        P(("dp", "ctx")),
        P(("dp", "ctx"), "tp"),
        P("tp"),
        P(("dp", "ctx"), "tp"),
        P(("dp", "ctx"), "tp"),
        P("tp"),
        P("tp", ("dp", "ctx")),
        P(("dp", "ctx")),
        P(("dp", "ctx"), "tp"),
        P("tp"),
        P("tp", ("dp", "ctx")),
        P(("dp", "ctx")),
    )
    return jax.shard_map(
        body,
        mesh=mesh,
        in_specs=placed,
        out_specs=(
            P("dp", "ctx", None),
            P("dp", "ctx", None),
            P(("dp", "ctx")),
            P(("dp", "ctx")),
            P(("dp", "ctx")),
            P(("dp", "ctx")),
            P(("dp", "ctx"), "tp"),
            P("tp"),
            P(("dp", "ctx"), "tp"),
            P(("dp", "ctx"), "tp"),
            P("tp"),
            P("tp", ("dp", "ctx")),
            P(("dp", "ctx")),
            P(("dp", "ctx"), "tp"),
            P("tp"),
            P("tp", ("dp", "ctx")),
            P(("dp", "ctx")),
        ),
        check_vma=False,
    )
```

time: 1020 us -> 839 us (0.82)
  Pallas kernels: 193 us -> 646 us
  waiting for transfers between devices: 312 us -> 65.7 us
  matrix products: 189 us -> 0 us
  other arithmetic: 122 us -> 37.1 us
  local copies, waits for them, and re-layouts: 84.7 us -> 27.9 us
  starting transfers between devices: 92.3 us -> 42.1 us
    pallas_call x2 -> x4, Pallas kernels: 51.5 us -> 489 us  [the longest x1 148 us: attend(): pl.pallas_call(functools.partial(attend_kernel, links, heads), out_shape=...]
    ppermute x95 -> x36, waiting for transfers between devices: 292 us -> 65.6 us  [swap(): return lax.ppermute(value, axis, [(i, i ^ mask) for i in range(size)])]
    dot_general x34 -> x0, matrix products: 189 us -> none  [the longest x24 85 us: across(): lax.dot_general(former, latter, (((1,), (1,)), ((), ())), preferred_eleme...]
    ppermute x95 -> x36, starting transfers between devices: 91.3 us -> 42 us  [swap(): return lax.ppermute(value, axis, [(i, i ^ mask) for i in range(size)])]
    unnamed x184 -> x58, local copies, waits for them, and re-layouts: 40.3 us -> 9.08 us
    convert_element_type x7 -> x0, other arithmetic: 23 us -> none  [the longest x2 11.6 us: over_cores(): return (ours + swap(theirs, 'tp', 1).astype(F32)).astype(BF16)]
    unnamed x17 -> x1, other arithmetic: 19.3 us -> 0.01 us
    reduce_scatter x4 -> x2, waiting for transfers between devices: 16.4 us -> 0.02 us  [over_dp(): return lax.psum_scatter(both, 'dp', scatter_dimension=0, tiled=True)]
  transfers between devices with their start and end apart: 103 -> 40, of which waited for: 37 -> 19; matrix products, arithmetic and copies ran while one was open for 32% -> 6% of each run, Pallas kernels for 5% -> 59%
where the time goes in v3:
time: 839 us; the launch traced here: 834 us
  Pallas kernels  646 us (77%)
  waiting for transfers between devices  65.7 us (8%)
  starting transfers between devices  42.1 us (5%)
  other arithmetic  37.1 us (4%)
  local copies, waits for them, and re-layouts  27.9 us (3%)
  between operations  14.9 us (2%)
    pallas_call x1, Pallas kernels, feed_forward(): pl.pallas_call(functools.partial(feed_forward_kernel, links), out_shape=(...  157 us
    pallas_call x1, Pallas kernels, attend(): pl.pallas_call(functools.partial(attend_kernel, links, heads), out_shape=...  148 us
    pallas_call x1, Pallas kernels, attend_back(): pl.pallas_call(functools.partial(attend_back_kernel, links, heads), out_s...  137 us
    pallas_call x1, Pallas kernels, first_back(): pl.pallas_call(functools.partial(first_back_kernel, links), out_shape=(ja...  111 us
    pallas_call x1, Pallas kernels, front(): pl.pallas_call(functools.partial(front_kernel, links), out_shape=(jax.Sha...  93.2 us
    ppermute x36, waiting for transfers between devices, swap(): return lax.ppermute(value, axis, [(i, i ^ mask) for i in range(size)])  65.6 us
    ppermute x36, starting transfers between devices, swap(): return lax.ppermute(value, axis, [(i, i ^ mask) for i in range(size)])  42 us
  transfers between devices with their start and end apart: 40, of which 19 were waited for; matrix products, arithmetic and copies ran while one was open for 6% of the time, Pallas kernels for 59%

profile of v3, /device:TPU:0, one launch (start us, length us, event | category | flops | bytes accessed | tf_op | source)
XLA Modules:
  0.0 833.9 jit_solution(7147714414742676)
XLA Ops:
  11.9 3.0 collective-permute-start
  16.5 5.5 collective-permute-done
  22.1 6.2 collective-permute-done.1
  31.6 2.7 collective-permute-done.3
  34.3 2.6 collective-permute-start.4
  45.5 2.0 convert_reduce_fusion.1
  48.9 93.2 %front.1 = (bf16[2048,2048]{1,0:T(8,128)(2,1)}, bf16[4,128,2048]{2,1,0:T(8,128)(2,1)S(1)}) custom-call(bf16[512,2048]{1,0:T(8,128)(2,1)S(1)} %get-tuple-element.41.own_ref, bf16[4,128,2048]{2,1,0:T(8,128)(2,1)S(1)} %copy-done.2, f32[8,2048]{1,0:T(8,128)S(1)} %add.177.table_ref), custom_call_target="tpu_custom_call" | custom-call | flops 83886080 | bytes 120000000 | tf_op jit(solution)/shard_map/front/pallas_call | solution.py:670
  143.8 3.2 dynamic-slice_bitcast_fusion.grads_ref
  148.2 147.7 %attend.1 = (bf16[2048,1536]{1,0:T(8,128)(2,1)}, bf16[2048,512]{1,0:T(8,128)(2,1)}, f32[4,8,2048]{2,1,0:T(8,128)}, bf16[2048,2048]{1,0:T(8,128)(2,1)}, f32[512,2...) custom-call(bf16[2048,2048]{1,0:T(8,128)(2,1)} %get-tuple-element.42.rows_ref.first_ref, ...), custom_call_target="tpu_custom_call" | custom-call | flops 27917287424 | bytes 33554432 | tf_op jit(solution)/shard_map/attend/pallas_call | solution.py:889
  295.9 157.2 %feed_forward.1 = (bf16[2048,2048]{1,0:T(8,128)(2,1)}, bf16[2048,2048]{1,0:T(8,128)(2,1)}, bf16[2048,2048]{1,0:T(8,128)(2,1)}, bf16[2048,2048]{1,0:T(8,128)(2,1)...) custom-call(bf16[512,2048]{1,0:T(8,128)(2,1)} %get-tuple-element.44., ...), custom_call_target="tpu_custom_call" | custom-call | flops 85899345920 | bytes 67108864 | tf_op jit(solution)/shard_map/feed_forward/pallas_call | solution.py:540
  453.2 137.3 %attend_back.1 = (bf16[2048,2048]{1,0:T(8,128)(2,1)}, bf16[2048,1536]{1,0:T(8,128)(2,1)}, f32[512,1024]{1,0:T(8,128)}, bf16[2048,1024]{1,0:T(8,128)(2,1)}) custom-call(bf16[512,2048]{1,0:T(8,128)(2,1)} %get-tuple-element.47.own_ref, bf16[2,2048,1024]{2,1,0:T(8,128)(2,1)} %get-tuple-element.48.weight_ref, bf16[2048,1536]{1,0:T(8,128)(2,1)} %get-tuple-element.49.qkv_ref, ...), custom_call_target="tpu_custom_call" | custom-call | flops 39728447488 | bytes 46137344 | tf_op jit(solution)/shard_map/attend_back/pallas_call | solution.py:1150
  590.5 3.9 convert_reduce_fusion
  601.9 1.8 collective-permute-done.25
  607.6 3.6 collective-permute-start.27
  612.1 1.7 collective-permute-start.34
  614.3 1.8 collective-permute-done.34
  617.8 2.0 collective-permute-start.19
  622.7 111.0 %first_back.1 = (f32[512,2048]{1,0:T(8,128)}, f32[512,1024]{1,0:T(8,128)}) custom-call(bf16[2048,1536]{1,0:T(8,128)(2,1)} %get-tuple-element.59.grads_ref, bf16[2,2048,1024]{2,1,0:T(8,128)(2,1)} %get-tuple-element.48.weight_ref, bf16[2048,2048]{1,0:T(8,128)(2,1)} %get-tuple-element.52.hid_ref, bf16[2048,2048]{1,0:T(8,128)(2,1)} %get-tuple-element.53.fall_ref), custom_call_target="tpu_custom_call" | custom-call | flops 21474836480 | bytes 29360128 | tf_op jit(solution)/shard_map/first_back/pallas_call | solution.py:1286
  733.7 3.8 fusion.10
  739.9 12.5 %collective-permute-done.11 = f32[2,2048]{1,0:T(2,128)S(1)} collective-permute-done((f32[2,2048]{1,0:T(2,128)S(1)}, f32[2,2048]{1,0:T(2,128)S(1)}, u32[]{:S(2)}, u32[]{:S(2)}) %collective-permute-start.11) | collective-permute-done | bytes 16416 | tf_op jit(solution)/shard_map/ppermute | solution.py:49
  753.4 2.9 collective-permute-done.12
  757.5 4.5 fusion.9
  762.0 2.7 collective-permute-start.14
  765.9 2.3 fusion.13
  770.3 19.9 %collective-permute-done.29 = bf16[128,2048]{1,0:T(8,128)(2,1)S(1)} collective-permute-done((bf16[128,2048]{1,0:T(8,128)(2,1)S(1)}, bf16[128,2048]{1,0:T(8,128)(2,1)S(1)}, u32[]{:S(2)}, u32[]{:S(2)}) %collective-permute-start.29) | collective-permute-done | bytes 524320 | tf_op jit(solution)/shard_map/ppermute | solution.py:49
  790.3 1.7 convert_bitcast_fusion
  792.1 2.9 copy.52
  796.4 2.5 select_bitcast_fusion.1
  798.9 2.4 pad_maximum_fusion.1
  801.3 3.8 select_bitcast_fusion.3
  810.0 4.1 pad_maximum_fusion
  818.4 4.5 collective-permute-done.22
  (219 shorter events, 62.6 us)
Async XLA Ops:
  7.2 141.0 %all-gather.3.cloned.1.call-start = ((), (), s32[]{:S(2)}) async-start(), calls=%async_computation.2 | async-start | bytes 5242880 | tf_op jit(solution)/shard_map/all_gather | solution.py:1371
  11.9 10.1 %collective-permute-start = (bf16[128,1024]{0,1:T(8,128)(2,1)S(1)}, bf16[128,1024]{0,1:T(8,128)(2,1)S(1)}, u32[]{:S(2)}, u32[]{:S(2)}) collective-permute-start(bf16[128,1024]{0,1:T(8,128)(2,1)S(1)} %get-tuple-element.106), channel_id=1, source_target_pairs={{0,2},{2,0},{4,6},{6,4},{1,3},{3,1},{5,7},{7,5},{8,10},{10,8},{12,... | collective-permute-start | bytes 786440 | tf_op jit(solution)/shard_map/ppermute | solution.py:49
  14.9 13.4 %collective-permute-start.1 = (bf16[128,1024]{0,1:T(8,128)(2,1)S(1)}, bf16[128,1024]{0,1:T(8,128)(2,1)S(1)}, u32[]{:S(2)}, u32[]{:S(2)}) collective-permute-start(bf16[128,1024]{0,1:T(8,128)(2,1)S(1)} %get-tuple-element.107), channel_id=1, source_target_pairs={{0,4},{2,6},{4,0},{6,2},{1,5},{3,7},{5,1},{7,3},{8,12},{10,14},{12... | collective-permute-start | bytes 786440 | tf_op jit(solution)/shard_map/ppermute | solution.py:49
  16.5 11.9 %collective-permute-start.2 = (bf16[128,1024]{0,1:T(8,128)(2,1)S(1)}, bf16[128,1024]{0,1:T(8,128)(2,1)S(1)}, u32[]{:S(2)}, u32[]{:S(2)}) collective-permute-start(bf16[128,1024]{0,1:T(8,128)(2,1)S(1)} %get-tuple-element.105), channel_id=1, source_target_pairs={{0,6},{2,4},{4,2},{6,0},{1,7},{3,5},{5,3},{7,1},{8,14},{10,12},{12... | collective-permute-start | bytes 786440 | tf_op jit(solution)/shard_map/ppermute | solution.py:49
  29.8 266.2 %all-gather.5.cloned.1.call-start = ((), (), s32[]{:S(2)}) async-start(), calls=%async_computation.3 | async-start | bytes 10485760 | tf_op jit(solution)/shard_map/all_gather | solution.py:1399
  29.9 4.3 collective-permute-start.3
  34.3 5.2 collective-permute-start.4
  39.4 4.3 collective-permute-start.5
  43.8 5.0 collective-permute-start.6
  143.4 479.3 %reduce-scatter.3.cloned.1.call-start = ((), (), s32[]{:S(2)}) async-start(), calls=%async_computation.4 | async-start | bytes 10485760 | tf_op jit(solution)/shard_map/reduce_scatter | solution.py:127
  453.2 352.0 %reduce-scatter.5.cloned.1.call-start = ((), (), s32[]{:S(2)}) async-start(), calls=%async_computation.5 | async-start | bytes 5242880 | tf_op jit(solution)/shard_map/reduce_scatter | solution.py:127
  595.4 5.6 collective-permute-start.15
  597.9 7.5 collective-permute-start.32
  601.1 5.5 collective-permute-start.16
  605.3 6.7 collective-permute-start.33
  606.6 7.2 collective-permute-start.17
  607.6 6.7 collective-permute-start.27
  612.1 4.0 collective-permute-start.34
  613.8 4.0 collective-permute-start.18
  616.1 4.9 collective-permute-start.35
  617.8 4.9 collective-permute-start.19
  737.7 26.9 %collective-permute-start.28 = (bf16[128,2048]{1,0:T(8,128)(2,1)S(1)}, bf16[128,2048]{1,0:T(8,128)(2,1)S(1)}, u32[]{:S(2)}, u32[]{:S(2)}) collective-permute-start(bf16[128,2048]{1,0:T(8,128)(2,1)S(1)} %dynamic-slice_bitcast_fusion.4), channel_id=1, source_target_pairs={{0,2},{2,0},{4,6},{6,4},{1,3},{3,1},{5,7},{7,5},{8,10},{10,8},{12,... | collective-permute-start | bytes 1572872 | tf_op jit(solution)/shard_map/ppermute | solution.py:49
  738.8 13.6 %collective-permute-start.11 = (f32[2,2048]{1,0:T(2,128)S(1)}, f32[2,2048]{1,0:T(2,128)S(1)}, u32[]{:S(2)}, u32[]{:S(2)}) collective-permute-start(f32[2,2048]{1,0:T(2,128)S(1)} %fusion.24), channel_id=1, source_target_pairs={{0,2},{2,0},{4,6},{6,4},{1,3},{3,1},{5,7},{7,5},{8,10},{10,8},{12,... | collective-permute-start | bytes 49160 | tf_op jit(solution)/shard_map/ppermute | solution.py:49
  756.3 5.7 collective-permute-start.13
  762.0 34.4 %collective-permute-start.9 = (bf16[512,2048]{1,0:T(8,128)(2,1)}, bf16[512,2048]{1,0:T(8,128)(2,1)}, u32[]{:S(2)}, u32[]{:S(2)}) collective-permute-start(bf16[512,2048]{1,0:T(8,128)(2,1)} %fusion.9), channel_id=1, source_target_pairs={{0,1},{1,0},{2,3},{3,2},{4,5},{5,4},{6,7},{7,6},{8,9},{9,8},{10,11... | collective-permute-start | bytes 6291464 | tf_op jit(solution)/shard_map/ppermute | solution.py:49
  762.0 6.2 collective-permute-start.14
  764.8 25.3 %collective-permute-start.29 = (bf16[128,2048]{1,0:T(8,128)(2,1)S(1)}, bf16[128,2048]{1,0:T(8,128)(2,1)S(1)}, u32[]{:S(2)}, u32[]{:S(2)}) collective-permute-start(bf16[128,2048]{1,0:T(8,128)(2,1)S(1)} %get-tuple-element.97), channel_id=1, source_target_pairs={{0,4},{2,6},{4,0},{6,2},{1,5},{3,7},{5,1},{7,3},{8,12},{10,14},{12... | collective-permute-start | bytes 1572872 | tf_op jit(solution)/shard_map/ppermute | solution.py:49
  768.2 33.1 %collective-permute-start.8 = (bf16[512,2048]{1,0:T(8,128)(2,1)}, bf16[512,2048]{1,0:T(8,128)(2,1)}, u32[]{:S(2)}, u32[]{:S(2)}) collective-permute-start(bf16[512,2048]{1,0:T(8,128)(2,1)} %fusion.13), channel_id=1, source_target_pairs={{0,1},{1,0},{2,3},{3,2},{4,5},{5,4},{6,7},{7,6},{8,9},{9,8},{10,11... | collective-permute-start | bytes 6291464 | tf_op jit(solution)/shard_map/ppermute | solution.py:49
  768.3 21.9 %collective-permute-start.30 = (bf16[128,2048]{1,0:T(8,128)(2,1)S(1)}, bf16[128,2048]{1,0:T(8,128)(2,1)S(1)}, u32[]{:S(2)}, u32[]{:S(2)}) collective-permute-start(bf16[128,2048]{1,0:T(8,128)(2,1)S(1)} %get-tuple-element.96), channel_id=1, source_target_pairs={{0,6},{2,4},{4,2},{6,0},{1,7},{3,5},{5,3},{7,1},{8,14},{10,12},{12... | collective-permute-start | bytes 1572872 | tf_op jit(solution)/shard_map/ppermute | solution.py:49
  807.1 9.3 %collective-permute-start.20 = (bf16[128,1024]{0,1:T(8,128)(2,1)}, bf16[128,1024]{0,1:T(8,128)(2,1)}, u32[]{:S(2)}, u32[]{:S(2)}) collective-permute-start(bf16[128,1024]{0,1:T(8,128)(2,1)} %bitcast.42), channel_id=1, source_target_pairs={{0,2},{2,0},{4,6},{6,4},{1,3},{3,1},{5,7},{7,5},{8,10},{10,8},{12,... | collective-permute-start | bytes 786440 | tf_op jit(solution)/shard_map/ppermute | solution.py:49
  808.9 8.5 %collective-permute-start.21 = (bf16[128,1024]{0,1:T(8,128)(2,1)}, bf16[128,1024]{0,1:T(8,128)(2,1)}, u32[]{:S(2)}, u32[]{:S(2)}) collective-permute-start(bf16[128,1024]{0,1:T(8,128)(2,1)} %bitcast.44), channel_id=1, source_target_pairs={{0,4},{2,6},{4,0},{6,2},{1,5},{3,7},{5,1},{7,3},{8,12},{10,14},{12... | collective-permute-start | bytes 786440 | tf_op jit(solution)/shard_map/ppermute | solution.py:49
  814.9 8.0 collective-permute-start.22
  (33 other events, 751.5 us)
Sparse Core Ops, SparseCore 0:
  29.9 81.0 all-gather.2
  143.5 149.9 all-gather.4
  453.3 145.7 reduce-scatter.2
  622.9 76.8 reduce-scatter.4

commit v4 on v3

--- a/solution.py
+++ b/solution.py
@@ -40,96 +40,13 @@
     return spread * (gradient - first_mean - normed * second_mean)
 
 
-def after(values, *earlier):
-    return lax.optimization_barrier((values, earlier))[0]
-
-
 def swap(value, axis, mask):
     size = lax.axis_size(axis)
     return lax.ppermute(value, axis, [(i, i ^ mask) for i in range(size)])
 
 
-def bit_order(part):
-    bits = list(range((lax.axis_size("ctx") - 1).bit_length()))
-    return bits if part == 0 else bits[::-1]
-
-
-def share(parts):
-    found = {}
-    for part in (0, 1):
-        have = {0: parts[part]}
-        for bit in bit_order(part):
-            mask = 1 << bit
-            have.update({r ^ mask: swap(have[r], "ctx", mask) for r in list(have)})
-        found.update({(r, part): have[r] for r in have})
-    return found
-
-
-def total(partial):
-    sums = []
-    for part in (0, 1):
-        have = {r: partial[(r, part)] for r in range(lax.axis_size("ctx"))}
-        for bit in bit_order(part)[::-1]:
-            mask = 1 << bit
-            came = {r ^ mask: swap(have[r].astype(BF16), "ctx", mask) for r in have if r & mask}
-            have = {r: have[r].astype(F32) + came[r].astype(F32) for r in came}
-        sums.append(have[0])
-    return jnp.concatenate(sums, axis=0)
-
-
-def summed(values, axes):
-    for axis in axes:
-        mask = 1
-        while mask < lax.axis_size(axis):
-            values = values + swap(values, axis, mask)
-            mask *= 2
-    return values
-
-
-def joined(blocks):
-    return jnp.concatenate([blocks[key] for key in sorted(blocks)], axis=0)
-
-
-def halves(rows):
-    middle = rows.shape[0] // 2
-    return (rows[:middle], rows[middle:])
-
-
-def exchange(pieces):
-    count = pieces.shape[0]
-    here = lax.axis_index("ctx")
-    result = pieces
-    for mask in range(1, count):
-        other = here ^ mask
-        came = swap(lax.dynamic_index_in_dim(pieces, other, 0, keepdims=False), "ctx", mask)
-        result = lax.dynamic_update_index_in_dim(result, came, other, 0)
-    return result
-
-
-def gather_weight(pieces):
-    count, rows, columns = pieces.shape
-    block = exchange(pieces).reshape(count * rows, columns)
-    half = lax.all_gather(block, "dp", axis=0, tiled=True)
-    return jnp.concatenate([half, swap(half, "tp", 1)], axis=1)
-
-
-def weight_grad(former, latter):
-    width = latter.shape[1] // 2
-    theirs = inner(former, latter[:, width:]).astype(BF16)
-    return (theirs, inner(former, latter[:, :width]))
-
-
-def over_cores(theirs, ours):
-    return (ours + swap(theirs, "tp", 1).astype(F32)).astype(BF16)
-
-
 def over_dp(both):
     return lax.psum_scatter(both, "dp", scatter_dimension=0, tiled=True)
-
-
-def to_shards(rows):
-    count = lax.axis_size("ctx")
-    return exchange(rows.reshape(count, rows.shape[0] // count, rows.shape[1]))
 
 
 def rows_of(here, block, size):
@@ -241,7 +158,7 @@
 
         lax.fori_loop(0, width // tile, step, 0)
 
-    def combine(self, copies, kept_ref, send_ref, recv_ref, result_ref, first, last):
+    def combine(self, copies, kept_ref, send_ref, recv_ref, first, last, final=None, then=None):
         for i in range(first, last - 1, -1):
             for part in (0, 1):
                 for j in self.given(i):
@@ -254,8 +171,8 @@
                     for j in self.given(i):
                         value = value + recv_ref[self.slot[(j, part)], at, :].astype(F32)
                     if i == 0:
-                        place = pl.ds(pl.multiple_of(part * self.half + step * chunk, chunk), chunk)
-                        result_ref[place, :] = value
+                        to = pl.ds(pl.multiple_of(part * self.half + step * chunk, chunk), chunk)
+                        final(part, at, to, value)
                     else:
                         send_ref[self.slot[(i, part)], at, :] = value.astype(BF16)
                     return 0
@@ -263,6 +180,8 @@
                 lax.fori_loop(0, self.half // chunk, add, 0)
                 if i:
                     copies[(i, part)].start()
+                elif then:
+                    then(part)
 
 
 def weight_grads(partner, rows_v, columns_v, theirs_v, came_v, result_ref, send_sem, recv_sem, store_sem):
@@ -472,7 +391,7 @@
             )
         ]
         if n == 0:
-            links.combine(sums, kept_v, send_v, recv_v, None, count // 2 - 1, 1)
+            links.combine(sums, kept_v, send_v, recv_v, count // 2 - 1, 1)
             finals = [
                 pltpu.make_async_copy(
                     residual_ref.at[pl.ds(part * half, half)], kept_v.at[2 + part], load_sem.at[2 + part]
@@ -487,29 +406,19 @@
     for copy in finals:
         copy.wait()
     vector_ref[...] = jnp.zeros_like(vector_ref)
-    chunk = min(32, half)
     results = []
-    for part in (0, 1):
-        for j in links.given(0):
-            sums[(j, part)].wait_recv()
-
-        def last(step, _, part=part):
-            at = pl.ds(pl.multiple_of(step * chunk, chunk), chunk)
-            to = pl.ds(pl.multiple_of(part * half + step * chunk, chunk), chunk)
-            second = kept_v[part, at, :]
-            for j in links.given(0):
-                second = second + recv_v[links.slot[(j, part)], at, :].astype(F32)
-            normed, spread = normalize(kept_v[2 + part, at, :])
-            incoming = rows_v[to, :].astype(F32)
-            back = incoming + norm_back(second * table_ref[2:3, :], normed, spread)
-            branch = back.astype(BF16)
-            kept_v[part, at, :] = back
-            rows_v[to, :] = branch
-            for n, value in enumerate((second * normed, second, branch.astype(F32), incoming)):
-                vector_ref[n : n + 1, :] += jnp.sum(value, axis=0, keepdims=True)
-            return 0
-
-        lax.fori_loop(0, half // chunk, last, 0)
+
+    def last(part, at, to, second):
+        normed, spread = normalize(kept_v[2 + part, at, :])
+        incoming = rows_v[to, :].astype(F32)
+        back = incoming + norm_back(second * table_ref[2:3, :], normed, spread)
+        branch = back.astype(BF16)
+        kept_v[part, at, :] = back
+        rows_v[to, :] = branch
+        for n, value in enumerate((second * normed, second, branch.astype(F32), incoming)):
+            vector_ref[n : n + 1, :] += jnp.sum(value, axis=0, keepdims=True)
+
+    def store_part(part):
         rows = pl.ds(part * half, half)
         for n, (source, target) in enumerate(
             ((kept_v.at[part], back_ref.at[rows]), (rows_v.at[rows], branch_ref.at[rows]))
@@ -517,6 +426,8 @@
             copy = pltpu.make_async_copy(source, target, load_sem.at[2 * part + n])
             copy.start()
             results.append(copy)
+
+    links.combine(sums, kept_v, send_v, recv_v, 0, 0, last, store_part)
     for end in ends:
         end()
     for copy in results:
@@ -588,48 +499,171 @@
     )(own, grads, both_weights, shift, residual, table)
 
 
-def front_kernel(
-    links,
-    own_ref,
-    pieces_ref,
-    table_ref,
-    normed_ref,
-    block_ref,
-    rows_v,
-    normed_v,
-    load_sem,
-    store_sem,
-    share_send,
-    share_recv,
-    piece_send,
-    piece_recv,
-):
-    count, half = links.count, links.half
-    size = 2 * half
+def greet_all(partners):
+    barrier = pltpu.get_barrier_semaphore()
+    for partner in partners:
+        pl.semaphore_signal(barrier, 1, device_id=partner, device_id_type=MESH)
+    pl.semaphore_wait(barrier, len(partners))
+
+
+def others(axis, count):
+    return [{axis: lax.bitwise_xor(lax.axis_index(axis), mask)} for mask in range(1, count)]
+
+
+def axis_bits(axis, size):
+    return [
+        {axis: lax.bitwise_xor(lax.axis_index(axis), 1 << bit)}
+        for bit in range((size - 1).bit_length())
+    ]
+
+
+def piece_copies(count, source, target_ref, send_sem, recv_sem, local_sem):
     here = lax.axis_index("ctx")
-    links.greet(masks=range(1, count))
-    shares = links.sharing(own_ref, rows_v, share_send, share_recv)
-    links.pass_on(shares, 0)
-    pieces = [
+    copies = [
         pltpu.make_async_remote_copy(
-            src_ref=pieces_ref.at[lax.bitwise_xor(here, mask)],
-            dst_ref=block_ref.at[here],
-            send_sem=piece_send.at[mask - 1],
-            recv_sem=piece_recv.at[mask - 1],
+            src_ref=source(lax.bitwise_xor(here, mask)),
+            dst_ref=target_ref.at[here],
+            send_sem=send_sem.at[mask - 1],
+            recv_sem=recv_sem.at[mask - 1],
             device_id={"ctx": lax.bitwise_xor(here, mask)},
             device_id_type=MESH,
         )
         for mask in range(1, count)
     ]
+    return copies + [pltpu.make_async_copy(source(here), target_ref.at[here], local_sem)]
+
+
+class Line:
+    def __init__(self, whole_ref, depth, send_sem, recv_sem):
+        self.whole, self.depth = whole_ref, depth
+        self.send_sem, self.recv_sem = send_sem, recv_sem
+        self.me = lax.axis_index("dp")
+
+    def copy(self, way, step, block):
+        block = jnp.clip(block, 0, self.depth - 1)
+        target = jnp.clip(self.me + way, 0, self.depth - 1)
+        n = 0 if way > 0 else 1
+        return pltpu.make_async_remote_copy(
+            src_ref=self.whole.at[block],
+            dst_ref=self.whole.at[block],
+            send_sem=self.send_sem.at[n, step - 1],
+            recv_sem=self.recv_sem.at[n, step - 1],
+            device_id={"dp": target},
+            device_id_type=MESH,
+        )
+
+    def sends(self, step, act):
+        me, depth = self.me, self.depth
+
+        @pl.when((me + 1 < depth) & (me - step + 1 >= 0))
+        def _():
+            act(self.copy(1, step, me - step + 1))
+
+        @pl.when((me >= 1) & (me + step - 1 < depth))
+        def _():
+            act(self.copy(-1, step, me + step - 1))
+
+    def start(self, step):
+        self.sends(step, lambda copy: copy.start())
+
+    def arrive(self, step):
+        @pl.when(self.me - step >= 0)
+        def _():
+            self.copy(1, step, self.me - step).wait_recv()
+
+        @pl.when(self.me + step < self.depth)
+        def _():
+            self.copy(-1, step, self.me + step).wait_recv()
+
+    def finish(self):
+        for step in range(1, self.depth):
+            self.sends(step, lambda copy: copy.wait_send())
+
+
+def front_kernel(
+    links,
+    depth,
+    tokens_ref,
+    head_pieces_ref,
+    pieces_ref,
+    small_ref,
+    normed_ref,
+    head_ref,
+    block_ref,
+    table_ref,
+    rows_v,
+    normed_v,
+    shards_v,
+    load_sem,
+    store_sem,
+    share_send,
+    share_recv,
+    head_send,
+    head_recv,
+    piece_send,
+    piece_recv,
+    line_send,
+    line_recv,
+    shard_send,
+    shard_recv,
+):
+    count, half = links.count, links.half
+    size = 2 * half
+    here, layer = lax.axis_index("ctx"), lax.axis_index("dp")
+    shard = here * depth + layer
+    thin = small_ref.shape[1]
+    own_ref = tokens_ref.at[lax.axis_index("tp")]
+    greet_all(others("ctx", count) + others("dp", depth))
+    heads = piece_copies(
+        count, lambda i: head_pieces_ref.at[i], head_ref.at[layer], head_send, head_recv, load_sem.at[2]
+    )
+    for copy in heads:
+        copy.start()
+    first = pltpu.make_async_copy(own_ref, rows_v.at[pl.ds(0, size)], load_sem.at[1])
+    first.start()
+    shards_v[shard] = small_ref[...]
+    for bit, device in enumerate(axis_bits("dp", depth) + axis_bits("ctx", count)):
+        reach = 1 << bit
+        mine = pl.ds(shard // reach * reach, reach)
+        theirs = pl.ds((shard // reach ^ 1) * reach, reach)
+        copies = [
+            pltpu.make_async_remote_copy(
+                src_ref=shards_v.at[mine],
+                dst_ref=shards_v.at[place],
+                send_sem=shard_send.at[bit],
+                recv_sem=shard_recv.at[bit],
+                device_id=device,
+                device_id_type=MESH,
+            )
+            for place in (mine, theirs)
+        ]
+        copies[0].start()
+        copies[0].wait_send()
+        copies[1].wait_recv()
+    shares = links.sharing(own_ref, rows_v, share_send, share_recv)
+    links.pass_on(shares, 0)
+    line = Line(head_ref, depth, line_send, line_recv)
+    for copy in heads:
+        copy.wait()
+    line.start(1)
+    pieces = piece_copies(
+        count, lambda i: pieces_ref.at[i], block_ref, piece_send, piece_recv, load_sem.at[0]
+    )
     for copy in pieces:
         copy.start()
-    kept = pltpu.make_async_copy(pieces_ref.at[here], block_ref.at[here], load_sem.at[0])
-    kept.start()
-    first = pltpu.make_async_copy(own_ref, rows_v.at[pl.ds(0, size)], load_sem.at[1])
-    first.start()
+    for c in range(count):
+        for d in range(depth):
+            n = d * count + c
+            table_ref[:, n * thin : (n + 1) * thin] = shards_v[c * depth + d]
     chunk = min(32, half)
     stores = []
-    for i in range(count):
+    for i in range(max(count, depth)):
+        if 0 < i < depth:
+            line.arrive(i)
+            if i + 1 < depth:
+                line.start(i + 1)
+        if i >= count:
+            continue
         if i == 0:
             first.wait()
         else:
@@ -651,39 +685,48 @@
             )
             store.start()
             stores.append(store)
-    kept.wait()
-    for copy in stores:
+    for copy in stores + pieces:
         copy.wait()
-    for copy in pieces:
-        copy.wait()
+    line.finish()
     for pair in links.pairs:
         shares[pair].wait_send()
 
 
-def front(own, pieces, table, count):
-    rows, width = own.shape
+def front(tokens, head_pieces, pieces, small, count, depth):
+    _, rows, width = tokens.shape
     length = rows * count
     links = Links(count, rows // 2)
     copies = len(links.pairs)
+    bits = (count - 1).bit_length() + (depth - 1).bit_length()
     anywhere = pl.BlockSpec(memory_space=pl.ANY)
+    inside = pl.BlockSpec(memory_space=pltpu.VMEM)
     dma = pltpu.SemaphoreType.DMA
     return pl.pallas_call(
-        functools.partial(front_kernel, links),
+        functools.partial(front_kernel, links, depth),
         out_shape=(
             jax.ShapeDtypeStruct((length, width), BF16),
+            jax.ShapeDtypeStruct((depth, *head_pieces.shape), BF16),
             jax.ShapeDtypeStruct(pieces.shape, BF16),
+            jax.ShapeDtypeStruct((8, width), F32),
         ),
-        in_specs=[anywhere, anywhere, pl.BlockSpec(memory_space=pltpu.VMEM)],
-        out_specs=(anywhere, anywhere),
+        in_specs=[anywhere, anywhere, anywhere, inside],
+        out_specs=(anywhere, anywhere, anywhere, inside),
         scratch_shapes=[
             pltpu.VMEM((length, width), BF16),
             pltpu.VMEM((length, width), BF16),
-            dma((2,)),
+            pltpu.VMEM((count * depth, *small.shape), F32),
+            dma((3,)),
             dma((2 * count,)),
             dma((copies,)),
             dma((copies,)),
             dma((count - 1,)),
             dma((count - 1,)),
+            dma((count - 1,)),
+            dma((count - 1,)),
+            dma((2, depth - 1)),
+            dma((2, depth - 1)),
+            dma((bits,)),
+            dma((bits,)),
         ],
         compiler_params=pltpu.CompilerParams(
             collective_id=1, has_side_effects=True, vmem_limit_bytes=40 * 1024 * 1024
@@ -692,7 +735,170 @@
             flops=20 * length * width, bytes_accessed=120000000, transcendentals=0
         ),
         name="front",
-    )(own, pieces, table)
+    )(tokens, head_pieces, pieces, small)
+
+
+def end_kernel(
+    count,
+    depth,
+    heads,
+    rows_ref,
+    vectors_ref,
+    firsts_ref,
+    biases_ref,
+    query_ref,
+    key_ref,
+    value_ref,
+    out_ref,
+    features_ref,
+    totals_ref,
+    block_v,
+    shards_v,
+    pair_v,
+    landing_v,
+    bias_v,
+    load_sem,
+    piece_send,
+    piece_recv,
+    shard_send,
+    shard_recv,
+    bias_send,
+    bias_recv,
+    total_send,
+    total_recv,
+):
+    here, layer = lax.axis_index("ctx"), lax.axis_index("dp")
+    shard = layer * count + here
+    partner = {"tp": 1 - lax.axis_index("tp")}
+    thin = query_ref.shape[0]
+    wide = heads * 3 * HEAD_DIM
+    low, high = (count - 1).bit_length(), (depth - 1).bit_length()
+    greet_all([partner] + others("ctx", count) + others("dp", depth))
+    pieces = piece_copies(
+        count,
+        lambda i: rows_ref.at[pl.ds(pl.multiple_of(i * thin, thin), thin)],
+        block_v,
+        piece_send,
+        piece_recv,
+        load_sem.at[0],
+    )
+    for copy in pieces:
+        copy.start()
+    for n in range(count * depth):
+        at = slice(n * thin, (n + 1) * thin)
+        shards_v[n, 0:4, :] = vectors_ref[0:4, at]
+        shards_v[n, 4:8, :] = firsts_ref[0:4, at]
+
+    def exchange(source, target, device, send, recv):
+        copy = pltpu.make_async_remote_copy(
+            src_ref=source,
+            dst_ref=target,
+            send_sem=send,
+            recv_sem=recv,
+            device_id=device,
+            device_id_type=MESH,
+        )
+        copy.start()
+        return copy
+
+    bias_v[0] = biases_ref[0]
+    bias_v[1] = biases_ref[1]
+    stage = [
+        exchange(shards_v, pair_v, partner, shard_send.at[low + high], shard_recv.at[low + high]),
+        exchange(bias_v.at[1], bias_v.at[2], partner, bias_send.at[high], bias_recv.at[high]),
+    ]
+    for copy in stage:
+        copy.wait()
+    shards_v[...] += pair_v[...]
+    bias_v[0] += bias_v[2]
+    totals = []
+    devices = axis_bits("ctx", count) + axis_bits("dp", depth)
+    for bit in range(low + high - 1, -1, -1):
+        reach = 1 << bit
+        mine = shard // reach * reach
+        theirs = (shard // reach ^ 1) * reach
+        stage = [
+            exchange(
+                shards_v.at[pl.ds(theirs, reach)],
+                landing_v.at[pl.ds(reach, reach)],
+                devices[bit],
+                shard_send.at[bit],
+                shard_recv.at[bit],
+            )
+        ]
+        if bit >= low:
+            n = bit - low
+            stage.append(
+                exchange(bias_v.at[0], bias_v.at[3 + n], devices[bit], bias_send.at[n], bias_recv.at[n])
+            )
+        for copy in stage:
+            copy.wait()
+        shards_v[pl.ds(mine, reach)] += landing_v[reach : 2 * reach]
+        if bit >= low:
+            bias_v[0] += bias_v[3 + bit - low]
+        if bit == low:
+            totals_ref[here] = bias_v[0]
+            totals = [
+                exchange(
+                    bias_v.at[0], totals_ref.at[here], device, total_send.at[n], total_recv.at[n]
+                )
+                for n, device in enumerate(others("ctx", count))
+            ]
+    features_ref[...] = shards_v[shard]
+    for copy in pieces + totals:
+        copy.wait()
+    for c in range(count):
+        for j in range(heads):
+            to = slice((c * heads + j) * HEAD_DIM, (c * heads + j + 1) * HEAD_DIM)
+            for n, ref in enumerate((query_ref, key_ref, value_ref)):
+                column = (3 * j + n) * HEAD_DIM
+                ref[:, to] = block_v[c, :, column : column + HEAD_DIM].astype(F32)
+        rows = slice(c * heads * HEAD_DIM, (c + 1) * heads * HEAD_DIM)
+        out_ref[rows, :] = block_v[c, :, wide:].astype(F32).T
+
+
+def end(rows, vectors, firsts, biases, heads, count, depth):
+    low, high = (count - 1).bit_length(), (depth - 1).bit_length()
+    thin = rows.shape[0] // count
+    columns = rows.shape[1]
+    local = count * heads * HEAD_DIM
+    inside = pl.BlockSpec(memory_space=pltpu.VMEM)
+    dma = pltpu.SemaphoreType.DMA
+    shards = (count * depth, 8, thin)
+    return pl.pallas_call(
+        functools.partial(end_kernel, count, depth, heads),
+        out_shape=(
+            jax.ShapeDtypeStruct((thin, local), F32),
+            jax.ShapeDtypeStruct((thin, local), F32),
+            jax.ShapeDtypeStruct((thin, local), F32),
+            jax.ShapeDtypeStruct((local, thin), F32),
+            jax.ShapeDtypeStruct((8, thin), F32),
+            jax.ShapeDtypeStruct((count, 1, biases.shape[2]), F32),
+        ),
+        in_specs=[pl.BlockSpec(memory_space=pl.ANY), inside, inside, inside],
+        out_specs=(inside,) * 6,
+        scratch_shapes=[
+            pltpu.VMEM((count, thin, columns), BF16),
+            pltpu.VMEM(shards, F32),
+            pltpu.VMEM(shards, F32),
+            pltpu.VMEM(shards, F32),
+            pltpu.VMEM((3 + high, 1, biases.shape[2]), F32),
+            dma((1,)),
+            dma((count - 1,)),
+            dma((count - 1,)),
+            dma((low + high + 1,)),
+            dma((low + high + 1,)),
+            dma((high + 1,)),
+            dma((high + 1,)),
+            dma((count - 1,)),
+            dma((count - 1,)),
+        ],
+        compiler_params=pltpu.CompilerParams(
+            collective_id=7, has_side_effects=True, vmem_limit_bytes=24 * 1024 * 1024
+        ),
+        cost_estimate=pl.CostEstimate(flops=0, bytes_accessed=40000000, transcendentals=0),
+        name="end",
+    )(rows, vectors, firsts, biases)
 
 
 def attend_kernel(
@@ -701,8 +907,8 @@
     rows_ref,
     weight_ref,
     shift_ref,
-    grads_ref,
-    own_ref,
+    cotangent_ref,
+    tokens_ref,
     table_ref,
     qkv_ref,
     mixed_ref,
@@ -711,6 +917,7 @@
     residual_ref,
     second_ref,
     whole_ref,
+    own_v,
     rows_v,
     weight_v,
     qkv_v,
@@ -731,7 +938,9 @@
     count, half = links.count, links.half
     size = 2 * half
     here = lax.axis_index("ctx")
-    partner = {"tp": 1 - lax.axis_index("tp")}
+    core = lax.axis_index("tp")
+    partner = {"tp": 1 - core}
+    grads_ref = cotangent_ref.at[core]
     narrow = weight_ref.shape[1]
     wide = heads * 3 * HEAD_DIM // 2
     links.greet([partner])
@@ -751,6 +960,8 @@
     ours.start()
     keep = pltpu.make_async_copy(grads_ref, grads_full_ref.at[pl.ds(0, size)], load_sem.at[1])
     keep.start()
+    own = pltpu.make_async_copy(tokens_ref.at[core], own_v, load_sem.at[4])
+    own.start()
 
     def load(n):
         return pltpu.make_async_copy(
@@ -818,18 +1029,15 @@
         if i >= count // 2:
             for part in (0, 1):
                 sums[(i, part)].start()
-    links.combine(sums, kept_v, send_v, recv_v, residual_ref, count // 2 - 1, 0)
-    chunk = min(32, half)
-
-    def norm(step, _):
-        at = pl.ds(pl.multiple_of(step * chunk, chunk), chunk)
-        residual = own_ref[at, :].astype(F32) + (residual_ref[at, :] + table_ref[4:5, :])
-        residual_ref[at, :] = residual
+
+    def norm(part, at, to, value):
+        residual = own_v[to, :].astype(F32) + (value + table_ref[4:5, :])
+        residual_ref[to, :] = residual
         normed = normalize(residual)[0]
-        second_ref[at, :] = (normed * table_ref[2:3, :] + table_ref[3:4, :]).astype(BF16)
-        return 0
-
-    lax.fori_loop(0, size // chunk, norm, 0)
+        second_ref[to, :] = (normed * table_ref[2:3, :] + table_ref[3:4, :]).astype(BF16)
+
+    own.wait()
+    links.combine(sums, kept_v, send_v, recv_v, count // 2 - 1, 0, norm)
     for i in range(1, count):
         for part in (0, 1):
             if i >= (count + 1) // 2:
@@ -875,7 +1083,7 @@
         log_ref[head, :, at] = log_total.T[0:8, :]
 
 
-def attend(rows, weight, shift, grads, own, table, heads, count):
+def attend(rows, weight, shift, cotangent, tokens, table, heads, count):
     length, width = rows.shape
     size = length // count
     narrow = weight.shape[1]
@@ -897,9 +1105,10 @@
             jax.ShapeDtypeStruct((size, width), BF16),
             jax.ShapeDtypeStruct((2, width, narrow), BF16),
         ),
-        in_specs=[anywhere, anywhere, inside, anywhere, inside, inside],
+        in_specs=[anywhere, anywhere, inside, anywhere, anywhere, inside],
         out_specs=(anywhere, anywhere, inside, anywhere, inside, inside, anywhere),
         scratch_shapes=[
+            pltpu.VMEM((size, width), BF16),
             pltpu.VMEM((2, size, width), BF16),
             pltpu.VMEM((2, width, narrow), BF16),
             pltpu.VMEM((length, columns), BF16),
@@ -908,7 +1117,7 @@
             pltpu.VMEM((count, half, width), F32),
             pltpu.VMEM((copies, half, width), BF16),
             pltpu.VMEM((copies, half, width), BF16),
-            dma((4,)),
+            dma((5,)),
             dma((4,)),
             dma((1,)),
             dma((1,)),
@@ -926,7 +1135,7 @@
             transcendentals=pairs,
         ),
         name="attend",
-    )(rows, weight, shift, grads, own, table)
+    )(rows, weight, shift, cotangent, tokens, table)
 
 
 def attend_back_kernel(
@@ -940,10 +1149,13 @@
     hid_ref,
     fall_ref,
     first_ref,
+    residual_ref,
+    table_ref,
     full_ref,
     result_ref,
-    sum_ref,
+    low_ref,
     head_grad_ref,
+    residual_v,
     weight_v,
     qkv_v,
     mixed_v,
@@ -990,13 +1202,14 @@
                 (mixed_ref, mixed_v),
                 (own_ref, full_ref.at[pl.ds(0, size)]),
                 (first_ref, big_v),
+                (residual_ref.at[:, pl.ds(0, narrow)], residual_v),
             )
         )
     ]
     for copy in loads:
         copy.start()
     loads[0].wait()
-    out_terms(links, hid_ref, hid_v, fall_v, kept_v, send_v, load_sem, 7)
+    out_terms(links, hid_ref, hid_v, fall_v, kept_v, send_v, load_sem, 8)
     for i in range(count):
         if i == 0:
             loads[1].wait()
@@ -1005,7 +1218,7 @@
             for part in (0, 1):
                 shares[(i, part)].wait_recv()
             links.pass_on(shares, i)
-            unit_loads = links.loads(full_ref, rows_v, i, load_sem, 7)
+            unit_loads = links.loads(full_ref, rows_v, i, load_sem, 8)
             for copy in unit_loads:
                 copy.start()
             for copy in unit_loads:
@@ -1026,7 +1239,7 @@
     def one_head(head, _):
         @pl.when(head == heads // 2)
         def _():
-            links.combine(sums, kept_v, send_v, recv_v, None, count // 2 - 1, 1)
+            links.combine(sums, kept_v, send_v, recv_v, count // 2 - 1, 1)
 
         attend_backward_head(
             here, head, size, count, qkv_v, grad_v, mixed_v, log_ref, result_ref, key_v, value_v
@@ -1049,7 +1262,12 @@
     )
     again = pltpu.make_async_copy(full_ref, big_v, load_sem.at[6])
     again.start()
-    links.combine(sums, kept_v, send_v, recv_v, sum_ref, 0, 0)
+    loads[7].wait()
+
+    def low(part, at, to, value):
+        low_ref[to, :] = (residual_v[to, :] + (value + table_ref[5:6, 0:narrow])).astype(BF16)
+
+    links.combine(sums, kept_v, send_v, recv_v, 0, 0, low)
     again.wait()
     end_second = weight_grads(
         partner,
@@ -1135,7 +1353,9 @@
         result_ref[there, value_at] = value_v[place, :].astype(BF16)
 
 
-def attend_back(own, weight, qkv, mixed, log_total, hid, fall_weight, first, count):
+def attend_back(
+    own, weight, qkv, mixed, log_total, hid, fall_weight, first, residual, table, count
+):
     rows, width = own.shape
     length, columns = qkv.shape
     heads = columns // (3 * HEAD_DIM)
@@ -1152,12 +1372,13 @@
         out_shape=(
             jax.ShapeDtypeStruct((length, width), BF16),
             jax.ShapeDtypeStruct((length, columns), BF16),
-            jax.ShapeDtypeStruct((rows, narrow), F32),
+            jax.ShapeDtypeStruct((rows, narrow), BF16),
             jax.ShapeDtypeStruct((width, 2 * heads * HEAD_DIM), BF16),
         ),
-        in_specs=[anywhere] * 4 + [inside, anywhere, anywhere, anywhere],
+        in_specs=[anywhere] * 4 + [inside] + [anywhere] * 4 + [inside],
         out_specs=(anywhere, inside, inside, anywhere),
         scratch_shapes=[
+            pltpu.VMEM((rows, narrow), F32),
             pltpu.VMEM((2, width, heads * HEAD_DIM // 2), BF16),
             pltpu.VMEM(qkv.shape, BF16),
             pltpu.VMEM(mixed.shape, BF16),
@@ -1173,7 +1394,7 @@
             pltpu.VMEM((count, half, narrow), F32),
             pltpu.VMEM((copies, half, narrow), BF16),
             pltpu.VMEM((copies, half, narrow), BF16),
-            dma((11,)),
+            dma((12,)),
             dma((2, width // 256)),
             dma((2, width // 256)),
             dma((2, width // 256)),
@@ -1191,7 +1412,7 @@
             transcendentals=pairs,
         ),
         name="attend_back",
-    )(own, weight, qkv, mixed, log_total, hid, fall_weight, first)
+    )(own, weight, qkv, mixed, log_total, hid, fall_weight, first, residual, table)
 
 
 def first_back_kernel(
@@ -1200,8 +1421,18 @@
     weight_ref,
     hid_ref,
     fall_ref,
-    first_ref,
-    sum_ref,
+    low_ref,
+    residual_ref,
+    back_ref,
+    tokens_ref,
+    table_ref,
+    hidden_ref,
+    out_ref,
+    input_ref,
+    vector_ref,
+    bias_ref,
+    fall_grad_ref,
+    rise_grad_ref,
     grads_v,
     weight_v,
     hid_v,
@@ -1212,33 +1443,80 @@
     kept_w,
     send_w,
     recv_w,
+    residual_v,
+    tokens_v,
+    high_v,
+    block_v,
     load_sem,
+    pair_send,
+    pair_recv,
+    piece_send,
+    piece_recv,
     sum_send,
     sum_recv,
     late_send,
     late_recv,
 ):
     count, half = links.count, links.half
+    size = 2 * half
     wide = weight_v.shape[2]
-    links.greet()
+    thin = hidden_ref.shape[0] // count
+    hidden = hidden_ref.shape[1] // 2
+    narrow = fall_v.shape[0]
+    core = lax.axis_index("tp")
+    partner = {"tp": 1 - core}
+    links.greet([partner], range(1, count))
     sums = links.summing(send_v, recv_v, sum_send, sum_recv)
     lates = links.summing(send_w, recv_w, late_send, late_recv)
-    narrow = fall_v.shape[0]
+    pieces = piece_copies(
+        count,
+        lambda i: hidden_ref.at[pl.ds(pl.multiple_of(i * thin, thin), thin)],
+        block_v,
+        piece_send,
+        piece_recv,
+        load_sem.at[10],
+    )
+    right = pl.ds(narrow, narrow)
+    left = pl.ds(0, narrow)
+
+    def both_cores(n, source, target_ref, rows, columns):
+        target = target_ref.at[core, rows, columns]
+        return [
+            pltpu.make_async_copy(source, target, load_sem.at[11 + n]),
+            pltpu.make_async_remote_copy(
+                src_ref=source,
+                dst_ref=target,
+                send_sem=pair_send.at[n],
+                recv_sem=pair_recv.at[n],
+                device_id=partner,
+                device_id_type=MESH,
+            ),
+        ]
+
+    outs = both_cores(0, low_ref, out_ref, pl.ds(0, size), left)
     loads = [
         pltpu.make_async_copy(source, target, load_sem.at[n])
         for n, (source, target) in enumerate(
             (
                 (weight_ref.at[:, :, pl.ds(0, wide)], weight_v),
-                (fall_ref.at[pl.ds(fall_ref.shape[0] - narrow, narrow)], fall_v),
+                (fall_ref.at[right], fall_v),
             )
+        )
+    ]
+    more = [
+        pltpu.make_async_copy(source, target, load_sem.at[15 + n])
+        for n, (source, target) in enumerate(
+            ((residual_ref.at[:, right], residual_v), (tokens_ref.at[core], tokens_v))
         )
     ]
     for copy in loads:
         copy.start()
     order = list(range(count - 1, -1, -1))
     unit_loads = links.loads(grads_ref, grads_v.at[0], order[0], load_sem, 2)
-    for copy in unit_loads:
+    for copy in unit_loads + pieces + more + outs:
         copy.start()
+    bias_ref[...] = jnp.zeros_like(bias_ref)
+    vector_ref[...] = jnp.zeros_like(vector_ref)
     loads[0].wait()
     for n, i in enumerate(order):
         for copy in unit_loads:
@@ -1260,37 +1538,97 @@
         if i >= count // 2:
             for part in (0, 1):
                 sums[(i, part)].start()
+        chunk = min(64, half)
+
+        def bias(step, _, n=n):
+            rows = pl.ds(pl.multiple_of(step * chunk, chunk), chunk)
+            value = grads_v[n % 2, rows, :].astype(F32)
+            bias_ref[0:1, :] += jnp.sum(value, axis=0, keepdims=True)
+            return 0
+
+        lax.fori_loop(0, size // chunk, bias, 0)
     loads[1].wait()
     out_terms(links, hid_ref, hid_v, fall_v, kept_w, send_w, load_sem, 6)
-    links.combine(sums, kept_v, send_v, recv_v, None, count // 2 - 1, 1)
+    for copy in pieces:
+        copy.wait()
+    for c in range(count):
+        rows = slice(c * hidden, (c + 1) * hidden)
+        fall_grad_ref[rows, :] = block_v[c, :, 0:hidden].astype(F32).T
+        rise_grad_ref[:, rows] = block_v[c, :, hidden : 2 * hidden].astype(F32)
+    links.combine(sums, kept_v, send_v, recv_v, count // 2 - 1, 1)
+    backs = [
+        pltpu.make_async_copy(
+            back_ref.at[pl.ds(part * half, half)], kept_v.at[2 + part], load_sem.at[2 + part]
+        )
+        for part in (0, 1)
+    ]
+    for copy in backs:
+        copy.start()
     for i in range(count - 1, count // 2 - 1, -1):
         for part in (0, 1):
             lates[(i, part)].start()
-    links.combine(sums, kept_v, send_v, recv_v, first_ref, 0, 0)
-    links.combine(lates, kept_w, send_w, recv_w, sum_ref, count // 2 - 1, 0)
+    for copy in more + backs:
+        copy.wait()
+
+    def last(part, at, to, first):
+        normed, spread = normalize(tokens_v[to, :].astype(F32))
+        grad = kept_v[2 + part, at, :] + norm_back(first * table_ref[0:1, :], normed, spread)
+        tokens_v[to, :] = grad.astype(BF16)
+        for n, value in enumerate((first * normed, first)):
+            vector_ref[n : n + 1, :] += jnp.sum(value, axis=0, keepdims=True)
+
+    def send_part(part):
+        rows = pl.ds(part * half, half)
+        copies = both_cores(
+            1 + part, tokens_v.at[rows], input_ref, rows, pl.ds(0, 2 * narrow)
+        )
+        for copy in copies:
+            copy.start()
+        outs.extend(copies)
+
+    links.combine(sums, kept_v, send_v, recv_v, 0, 0, last, send_part)
+
+    def high(part, at, to, value):
+        high_v[to, :] = (
+            residual_v[to, :] + (value + table_ref[5:6, narrow : 2 * narrow])
+        ).astype(BF16)
+
+    links.combine(lates, kept_w, send_w, recv_w, count // 2 - 1, 0, high)
+    copies = both_cores(3, high_v, out_ref, pl.ds(0, size), right)
+    for copy in copies:
+        copy.start()
+    for copy in outs + copies:
+        copy.wait()
     for pair in links.pairs:
         sums[pair].wait_send()
         lates[pair].wait_send()
 
 
-def first_back(grads, weight, hid, fall_weight, count):
+def first_back(
+    grads, weight, hid, fall_weight, low, residual, back, tokens, table, hidden_rows, count
+):
     length, columns = grads.shape
     width, hidden = fall_weight.shape
     rows = length // count
     links = Links(count, rows // 2)
     half, copies = links.half, len(links.pairs)
     narrow = width // 2
+    thin, piece = hidden_rows.shape[0] // count, hidden_rows.shape[1] // 2
     anywhere = pl.BlockSpec(memory_space=pl.ANY)
     inside = pl.BlockSpec(memory_space=pltpu.VMEM)
     dma = pltpu.SemaphoreType.DMA
     return pl.pallas_call(
         functools.partial(first_back_kernel, links),
         out_shape=(
-            jax.ShapeDtypeStruct((rows, width), F32),
-            jax.ShapeDtypeStruct((rows, narrow), F32),
+            jax.ShapeDtypeStruct((2, rows, width), BF16),
+            jax.ShapeDtypeStruct((2, rows, width), BF16),
+            jax.ShapeDtypeStruct((8, width), F32),
+            jax.ShapeDtypeStruct((1, columns), F32),
+            jax.ShapeDtypeStruct((count * piece, thin), F32),
+            jax.ShapeDtypeStruct((thin, count * piece), F32),
         ),
-        in_specs=[anywhere] * 4,
-        out_specs=(inside, inside),
+        in_specs=[anywhere] * 8 + [inside, anywhere],
+        out_specs=(anywhere, anywhere, inside, inside, inside, inside),
         scratch_shapes=[
             pltpu.VMEM((2, rows, columns), BF16),
             pltpu.VMEM((2, width, columns // 2), BF16),
@@ -1302,14 +1640,22 @@
             pltpu.VMEM((count, half, narrow), F32),
             pltpu.VMEM((copies, half, narrow), BF16),
             pltpu.VMEM((copies, half, narrow), BF16),
-            dma((10,)),
+            pltpu.VMEM((rows, narrow), F32),
+            pltpu.VMEM((rows, width), BF16),
+            pltpu.VMEM((rows, narrow), BF16),
+            pltpu.VMEM((count, thin, 2 * piece), BF16),
+            dma((17,)),
+            dma((4,)),
+            dma((4,)),
+            dma((count - 1,)),
+            dma((count - 1,)),
             dma((copies,)),
             dma((copies,)),
             dma((copies,)),
             dma((copies,)),
         ],
         compiler_params=pltpu.CompilerParams(
-            collective_id=5, has_side_effects=True, vmem_limit_bytes=58 * 1024 * 1024
+            collective_id=5, has_side_effects=True, vmem_limit_bytes=63 * 1024 * 1024
         ),
         cost_estimate=pl.CostEstimate(
             flops=2 * length * width * (columns + hidden // 2),
@@ -1317,7 +1663,7 @@
             transcendentals=0,
         ),
         name="first_back",
-    )(grads, weight, hid, fall_weight)
+    )(grads, weight, hid, fall_weight, low, residual, back, tokens, table, hidden_rows)
 
 
 def body(
@@ -1342,13 +1688,9 @@
     _, local_rows, model_width = tokens.shape
     ctx, dp = lax.axis_size("ctx"), lax.axis_size("dp")
     here, core = lax.axis_index("ctx"), lax.axis_index("tp")
-    shard = lax.axis_index("dp") * ctx + here
     thin = query_weight.shape[0]
     heads = query_weight.shape[1] // (HEAD_DIM * ctx)
     hidden = up_weight.shape[1] // ctx
-    inputs = lax.dynamic_index_in_dim(tokens, core, 0, keepdims=False)
-    incoming = lax.dynamic_index_in_dim(cotangent, core, 0, keepdims=False)
-
     packed = jnp.stack(
         [w.reshape(thin, ctx, heads, HEAD_DIM) for w in (query_weight, key_weight, value_weight)],
         axis=3,
@@ -1367,20 +1709,11 @@
         ],
         axis=2,
     )
-    head_block = exchange(head_pieces).reshape(ctx * thin, -1)
-    head_weights = lax.all_gather(head_block, "dp", axis=0, tiled=True)
 
     small = jnp.stack(
         [attention_gain, attention_bias, feedforward_gain, feedforward_bias, output_bias, down_bias]
     ).astype(F32)
     small = jnp.concatenate([small, jnp.zeros((2, thin), F32)])
-    table = jnp.zeros((8, model_width), F32)
-    table = lax.dynamic_update_slice(table, small, (0, shard * thin))
-    table = summed(table, ("dp", "ctx"))
-    gain_one, shift_one, gain_two, shift_two, output_shift, down_shift = [
-        table[n : n + 1] for n in range(6)
-    ]
-
     def own_columns(vector):
         return lax.dynamic_index_in_dim(vector.reshape(ctx, -1), here, 0, keepdims=False)
 
@@ -1393,86 +1726,65 @@
     qkv_shift = jnp.concatenate([shifts[:wide], other_shifts[:wide]]).astype(F32)
     rise_shift = jnp.concatenate([shifts[wide:], other_shifts[wide:]]).astype(F32)
 
-    wide_inputs = inputs.astype(F32)
-    normed_one, spread_one = normalize(wide_inputs)
-    ones, hidden_block = front(after(inputs, head_block), hidden_pieces, table, ctx)
+    ones, head_weights, hidden_block, table = front(
+        tokens, head_pieces, hidden_pieces, small, ctx, dp
+    )
+    head_weights = head_weights.reshape(model_width, -1)
     hidden_weights = lax.all_gather(
         hidden_block.reshape(ctx * thin, -1), "dp", axis=0, tiled=True
     )
     qkv, mixed, log_total, grads_in, residual, input_two, head_whole = attend(
-        ones, head_weights, qkv_shift[None], incoming, inputs, table, 2 * heads, ctx
-    )
-    _, all_hid, _, hidden_both, residual_grad, branch_grad, vectors, rise_bias, fall_weight = (
+        ones, head_weights, qkv_shift[None], cotangent, tokens, table, 2 * heads, ctx
+    )
+    _, hid, _, hidden_both, residual_grad, branch_grad, vectors, rise_bias, fall_weight = (
         feed_forward(input_two, grads_in, hidden_weights, rise_shift[None], residual, table, ctx)
     )
     hidden_rows = over_dp(hidden_both)
 
     _, qkv_grads, low_columns, head_both = attend_back(
-        branch_grad, head_whole, qkv, mixed, log_total, all_hid, fall_weight, ones, ctx
-    )
-    qkv_bias = jnp.sum(qkv_grads.astype(F32), axis=0)
-    head_both = after(head_both, hidden_rows)
-    late_grads = after(qkv_grads, head_both)
-    first_grad, high_columns = first_back(late_grads, head_whole, all_hid, fall_weight, ctx)
-    block_out = residual + (jnp.concatenate([low_columns, high_columns], axis=1) + down_shift)
-    own_out = block_out.astype(BF16)
-    late_both = head_both
-    width = hidden
-    hidden_grad = to_shards(hidden_rows)
-    fall_grad, rise_grad = hidden_grad[:, :, :width], hidden_grad[:, :, width:]
-    late_grad = to_shards(over_dp(late_both))
-    qkv_grad, out_grad = late_grad[:, :, :wide], late_grad[:, :, wide:]
-    gain_one_sum = jnp.sum(first_grad * normed_one, axis=0)
-    bias_one_sum = jnp.sum(first_grad, axis=0)
-    token_grad = residual_grad + norm_back(first_grad * gain_one, normed_one, spread_one)
-    own_grad = token_grad.astype(BF16)
-
-    def both_sequences(own):
-        other = swap(own, "tp", 1)
-        first = core == 0
-        return jnp.stack([jnp.where(first, own, other), jnp.where(first, other, own)])
-
-    def spread_columns(vector):
-        own, other = jnp.split(vector, 2)
-        whole = jnp.zeros((2, ctx, own.shape[0]), F32)
-        whole = lax.dynamic_update_slice(whole, own[None, None], (core, here, 0))
-        return lax.dynamic_update_slice(whole, other[None, None], (1 - core, here, 0))
-
-    everywhere = ("tp", "ctx", "dp")
-    early = vectors[:4]
-    features = jnp.concatenate(
-        [
-            summed(jnp.stack([gain_one_sum, bias_one_sum]), everywhere),
-            summed(early, everywhere),
-        ]
-    )
-    qkv_bias = summed(spread_columns(qkv_bias), everywhere)
-    rise_bias = summed(spread_columns(rise_bias[0]), everywhere)
-    features = lax.dynamic_slice(features, (0, shard * thin), (6, thin))
-    qkv_bias = lax.dynamic_index_in_dim(qkv_bias, core, 0, keepdims=False)
-    qkv_bias = qkv_bias.reshape(ctx * heads, 3, HEAD_DIM)
-    rise_bias = lax.dynamic_index_in_dim(rise_bias, core, 0, keepdims=False).reshape(-1)
-
-    qkv_grad = qkv_grad.reshape(ctx, thin, heads, 3, HEAD_DIM).transpose(3, 1, 0, 2, 4)
-    qkv_grad = qkv_grad.reshape(3, thin, ctx * heads * HEAD_DIM).astype(F32)
+        branch_grad, head_whole, qkv, mixed, log_total, hid, fall_weight, ones, residual, table, ctx
+    )
+    head_both, hidden_rows = lax.optimization_barrier((head_both, hidden_rows))
+    head_rows = over_dp(head_both)
+    outputs, input_grads, firsts, qkv_bias, fall_grad, rise_grad = first_back(
+        qkv_grads,
+        head_whole,
+        hid,
+        fall_weight,
+        low_columns,
+        residual,
+        residual_grad,
+        tokens,
+        table,
+        hidden_rows,
+        ctx,
+    )
+    biases = jnp.concatenate(
+        [rise_bias.reshape(2, 1, hidden), qkv_bias.reshape(2, 1, wide)], axis=2
+    )
+    query_grad, key_grad, value_grad, out_grad, features, totals = end(
+        head_rows, vectors, firsts, biases, heads, ctx, dp
+    )
+    totals = totals[:, 0]
+    qkv_bias = totals[:, hidden:].reshape(ctx * heads, 3, HEAD_DIM)
     return (
-        both_sequences(own_out),
-        both_sequences(own_grad),
+        outputs,
+        input_grads,
+        features[4],
+        features[5],
         features[0],
         features[1],
+        query_grad,
+        qkv_bias[:, 0].reshape(-1),
+        key_grad,
+        value_grad,
+        qkv_bias[:, 2].reshape(-1),
+        out_grad,
         features[2],
+        rise_grad,
+        totals[:, :hidden].reshape(-1),
+        fall_grad,
         features[3],
-        qkv_grad[0],
-        qkv_bias[:, 0].reshape(-1),
-        qkv_grad[1],
-        qkv_grad[2],
-        qkv_bias[:, 2].reshape(-1),
-        out_grad.transpose(0, 2, 1).reshape(-1, thin).astype(F32),
-        features[4],
-        rise_grad.transpose(1, 0, 2).reshape(thin, -1).astype(F32),
-        rise_bias,
-        fall_grad.transpose(0, 2, 1).reshape(-1, thin).astype(F32),
-        features[5],
     )
 
 

time: 839 us -> 768 us (0.915)
  Pallas kernels: 646 us -> 711 us
  waiting for transfers between devices: 65.7 us -> 7.24 us
  starting transfers between devices: 42.1 us -> 0.37 us
  other arithmetic: 37.1 us -> 2.41 us
    ppermute x36 -> x1, waiting for transfers between devices: 65.6 us -> 1.13 us  [swap(): return lax.ppermute(value, axis, [(i, i ^ mask) for i in range(size)])]
    pallas_call x1 -> x2, Pallas kernels: 93.2 us -> 137 us  [the longest x1 117 us: front(): pl.pallas_call(functools.partial(front_kernel, links, depth), out_shape=(...]
    ppermute x36 -> x1, starting transfers between devices: 42 us -> 0.07 us  [swap(): return lax.ppermute(value, axis, [(i, i ^ mask) for i in range(size)])]
    pallas_call x1, Pallas kernels: 111 us -> 133 us  [first_back(): pl.pallas_call(functools.partial(first_back_kernel, links), out_shape=(ja...]
    unnamed x58 -> x45, local copies, waits for them, and re-layouts: 9.08 us -> 24.2 us
    another operation x5 -> x0, other arithmetic: 12.8 us -> none  [the longest x4 12.8 us: both_sequences(): jnp.stack([jnp.where(first, own, other), jnp.where(first, other, own)])]
    reduce_sum x4 -> x0, other arithmetic: 10.3 us -> none  [the longest x1 3.87 us: body(): qkv_bias = jnp.sum(qkv_grads.astype(F32), axis=0)]
    convert_element_type x5 -> x0, other arithmetic: 9.56 us -> none  [the longest x1 4.48 us: body(): own_grad = token_grad.astype(BF16)]
  transfers between devices with their start and end apart: 40 -> 4, of which waited for: 19 -> 2; matrix products, arithmetic and copies ran while one was open for 6% -> 0% of each run, Pallas kernels for 59% -> 54%
where the time goes in v4:
time: 768 us; the launch traced here: 764 us
  Pallas kernels  711 us (93%)
  local copies, waits for them, and re-layouts  28.8 us (4%)
  between operations  14.3 us (2%)
    pallas_call x1, Pallas kernels, feed_forward(): pl.pallas_call(functools.partial(feed_forward_kernel, links), out_shape=(...  157 us
    pallas_call x1, Pallas kernels, attend(): pl.pallas_call(functools.partial(attend_kernel, links, heads), out_shape=...  146 us
    pallas_call x1, Pallas kernels, attend_back(): pl.pallas_call(functools.partial(attend_back_kernel, links, heads), out_s...  137 us
    pallas_call x1, Pallas kernels, first_back(): pl.pallas_call(functools.partial(first_back_kernel, links), out_shape=(ja...  133 us
    pallas_call x1, Pallas kernels, front(): pl.pallas_call(functools.partial(front_kernel, links, depth), out_shape=(...  117 us
    unnamed x45, local copies, waits for them, and re-layouts  24.2 us
    pallas_call x1, Pallas kernels, end(): pl.pallas_call(functools.partial(end_kernel, count, depth, heads), out_sh...  20.2 us
  transfers between devices with their start and end apart: 4, of which 2 were waited for; matrix products, arithmetic and copies ran while one was open for 0% of the time, Pallas kernels for 54%

profile of v4, /device:TPU:0, one launch (start us, length us, event | category | flops | bytes accessed | tf_op | source)
XLA Modules:
  0.0 764.1 jit_solution(3444593607476402770)
XLA Ops:
  7.3 0.9 stack.34
  8.1 1.1 copy.37
  9.2 1.1 copy.38
  10.4 1.1 copy.39
  12.1 0.7 copy.43
  13.3 1.5 copy.42
  15.2 1.9 copy-done
  17.0 116.9 %front.1 = (bf16[2048,2048]{1,0:T(8,128)(2,1)}, bf16[4,4,128,1024]{3,2,1,0:T(8,128)(2,1)S(1)}, bf16[4,128,2048]{2,1,0:T(8,128)(2,1)}, f32[8,2048]{1,0:T(8,128)S(1)}) custom-call(bf16[2,512,2048]{2,1,0:T(8,128)(2,1)S(1)} %copy-done, bf16[4,128,1024]{2,1,0:T(8,128)(2,1)S(1)} %pad_maximum_fusion.1.head_pieces_ref, ...), custom_call_target="tpu_custom_call" | custom-call | flops 83886080 | bytes 120000000 | tf_op jit(solution)/shard_map/front/pallas_call | solution.py:704
  134.0 2.0 copy-done.4
  136.0 0.6 copy-done.5
  137.2 1.1 collective-permute-done
  138.4 0.6 maximum_convert_fusion.1.shift_ref
  139.0 0.6 maximum_convert_fusion.shift_ref
  139.6 146.3 %attend.1 = (bf16[2048,1536]{1,0:T(8,128)(2,1)}, bf16[2048,512]{1,0:T(8,128)(2,1)}, f32[4,8,2048]{2,1,0:T(8,128)}, bf16[2048,2048]{1,0:T(8,128)(2,1)}, f32[512,2...) custom-call(bf16[2048,2048]{1,0:T(8,128)(2,1)} %get-tuple-element.52.rows_ref.first_ref, ...), custom_call_target="tpu_custom_call" | custom-call | flops 27917287424 | bytes 33554432 | tf_op jit(solution)/shard_map/attend/pallas_call | solution.py:1097
  286.0 157.5 %feed_forward.1 = (bf16[2048,2048]{1,0:T(8,128)(2,1)}, bf16[2048,2048]{1,0:T(8,128)(2,1)}, bf16[2048,2048]{1,0:T(8,128)(2,1)}, bf16[2048,2048]{1,0:T(8,128)(2,1)...) custom-call(bf16[512,2048]{1,0:T(8,128)(2,1)} %get-tuple-element.55., ...), custom_call_target="tpu_custom_call" | custom-call | flops 85899345920 | bytes 67108864 | tf_op jit(solution)/shard_map/feed_forward/pallas_call | solution.py:451
  443.5 136.6 %attend_back.1 = (bf16[2048,2048]{1,0:T(8,128)(2,1)}, bf16[2048,1536]{1,0:T(8,128)(2,1)}, bf16[512,1024]{1,0:T(8,128)(2,1)}, bf16[2048,1024]{1,0:T(8,128)(2,1)}) custom-call(bf16[512,2048]{1,0:T(8,128)(2,1)} %get-tuple-element.59.own_ref, bf16[2,2048,1024]{2,1,0:T(8,128)(2,1)} %get-tuple-element.60.weight_ref, bf16[2048,1536]{1,0:T(8,128)(2,1)} %get-tuple-element.61.qkv_ref, ...), custom_call_target="tpu_custom_call" | custom-call | flops 39728447488 | bytes 46137344 | tf_op jit(solution)/shard_map/attend_back/pallas_call | solution.py:1370
  580.1 6.0 reduce-scatter.3.cloned.1.call-done.hidden_ref
  586.2 133.4 %first_back.1 = (bf16[2,512,2048]{2,1,0:T(8,128)(2,1)}, bf16[2,512,2048]{2,1,0:T(8,128)(2,1)}, f32[8,2048]{1,0:T(8,128)}, f32[1,1536]{1,0:T(1,128)}, f32[4096,128]{1,0:T(8,128)}, /*index=5*/f32[128,4096]{1,0:T(8,128)}) custom-call(bf16[2048,1536]{1,0:T(8,128)(2,1)} %get-tuple-element.66.grads_ref, bf16[2,2048,1024]{2,1,0:T(8,128)(2,1)} %get-tuple-element.60.weight_ref, ...), custom_call_target="tpu_custom_call" | custom-call | flops 21474836480 | bytes 29360128 | tf_op jit(solution)/shard_map/first_back/pallas_call | solution.py:1620
  719.6 0.7 pad_maximum_fusion.3.biases_ref
  720.4 1.2 copy-done.1
  721.6 0.8 copy-done.3
  722.5 20.2 %end.1 = (f32[128,1024]{1,0:T(8,128)S(1)}, f32[128,1024]{1,0:T(8,128)S(1)}, f32[128,1024]{1,0:T(8,128)S(1)}, f32[1024,128]{1,0:T(8,128)S(1)}, f32[8,128]{1,0:T(8,128)S(1)}, /*index=5*/f32[4,1,1792]{2,1,0:T(1,128)S(1)}) custom-call(bf16[512,1024]{1,0:T(8,128)(2,1)S(1)} %copy-done.1, f32[8,2048]{1,0:T(8,128)S(1)} %copy-done.2, f32[8,2048]{1,0:T(8,128)S(1)} %copy-done.3, ...), custom_call_target="tpu_custom_call" | custom-call | bytes 40000000 | tf_op jit(solution)/shard_map/end/pallas_call | solution.py:868
  743.2 0.6 copy.50
  743.9 0.6 fusion.1
  744.5 4.9 copy.59
  749.4 2.1 copy.60
  751.6 0.8 copy.61
  752.4 0.8 copy.62
  753.1 0.8 copy.63
  753.9 0.8 copy.64
  754.7 1.3 copy.65
  756.1 1.3 copy.66
  (60 shorter events, 2.7 us)
Async XLA Ops:
  7.2 4.7 copy-start.10
  7.2 4.9 copy-start.9
  7.2 278.7 %all-gather.2.cloned.1.call-start = ((), (), s32[]{:S(2)}) async-start(), calls=%async_computation.2 | async-start | bytes 10485760 | tf_op jit(solution)/shard_map/all_gather | solution.py:1733
  14.8 2.2 copy-start
  17.0 119.8 %copy-start.13 = (bf16[1024]{0:T(1024)(128)(2,1)S(1)}, bf16[1024]{0:T(1024)(128)(2,1)}, u32[]{:S(2)}) copy-start(bf16[1024]{0:T(1024)(128)(2,1)} %param.24) | copy-start | bytes 6148
  17.0 119.9 %copy-start.14 = (bf16[1024]{0:T(1024)(128)(2,1)S(1)}, bf16[1024]{0:T(1024)(128)(2,1)}, u32[]{:S(2)}) copy-start(bf16[1024]{0:T(1024)(128)(2,1)} %param.27) | copy-start | bytes 6148
  17.0 120.1 %copy-start.12 = (bf16[4096]{0:T(1024)(128)(2,1)S(1)}, bf16[4096]{0:T(1024)(128)(2,1)}, u32[]{:S(2)}) copy-start(bf16[4096]{0:T(1024)(128)(2,1)} %param.31) | copy-start | bytes 24580
  134.0 2.0 copy-start.4
  136.0 0.6 copy-start.5
  136.6 449.5 %reduce-scatter.3.cloned.1.call-start = ((), (), s32[]{:S(2)}) async-start(), calls=%async_computation.3 | async-start | bytes 10485760 | tf_op jit(solution)/shard_map/reduce_scatter | solution.py:49
  137.1 1.2 collective-permute-start
  443.5 276.9 %reduce-scatter.5.cloned.1.call-start = ((), (), s32[]{:S(2)}) async-start(), calls=%async_computation.4 | async-start | bytes 5242880 | tf_op jit(solution)/shard_map/reduce_scatter | solution.py:49
  586.2 133.5 %copy-start.11 = (f32[1,2048]{1,0:T(1,128)S(1)}, f32[1,2048]{1,0:T(1,128)}, u32[]{:S(2)}) copy-start(f32[1,2048]{1,0:T(1,128)} %get-tuple-element.77) | copy-start | bytes 24580
  586.2 134.2 %copy-start.2 = (f32[8,2048]{1,0:T(8,128)S(1)}, f32[8,2048]{1,0:T(8,128)}, u32[]{:S(2)}) copy-start(f32[8,2048]{1,0:T(8,128)} %get-tuple-element.75.vectors_ref) | copy-start | bytes 196612
  720.4 1.2 copy-start.1
  721.6 0.8 copy-start.3
  744.5 4.9 copy-start.6
  749.4 5.3 copy-start.8
  751.6 4.5 copy-start.7
Sparse Core Ops, SparseCore 0:
  136.7 147.7 all-gather.1
  443.6 142.4 reduce-scatter.2
  588.5 77.5 reduce-scatter.4

commit v5 on v4

--- a/solution.py
+++ b/solution.py
@@ -143,7 +143,7 @@
         ]
 
     def terms(self, i, columns, width, kept_v, send_v):
-        tile = min(256, width)
+        tile = min(512, width)
 
         def step(n, _):
             at = pl.ds(pl.multiple_of(n * tile, tile), tile)
@@ -184,8 +184,8 @@
                     then(part)
 
 
-def weight_grads(partner, rows_v, columns_v, theirs_v, came_v, result_ref, send_sem, recv_sem, store_sem):
-    tile = 256
+def weight_grads(partner, rows_v, columns_v, theirs_v, came_v, results, send_sem, recv_sem, store_sem):
+    tile = 512
     width = rows_v.shape[1]
     own = columns_v.shape[1] // 2
 
@@ -203,7 +203,16 @@
         )
 
     def store_tile(m):
-        return pltpu.make_async_copy(came_v.at[place(m)], result_ref.at[place(m)], store_sem.at[m])
+        copies, column = [], 0
+        for n, result in enumerate(results):
+            count = result.shape[1]
+            copies.append(
+                pltpu.make_async_copy(
+                    came_v.at[place(m), pl.ds(column, count)], result.at[place(m)], store_sem[n].at[m]
+                )
+            )
+            column += count
+        return copies
 
     def first(m, _):
         term = inner(rows_v[:, place(m)], columns_v[:, own : 2 * own])
@@ -215,11 +224,13 @@
         swap_tile(m).wait_recv()
         term = inner(rows_v[:, place(m)], columns_v[:, 0:own])
         came_v[place(m), :] = (term + came_v[place(m), :].astype(F32)).astype(BF16)
-        store_tile(m).start()
+        for copy in store_tile(m):
+            copy.start()
         return 0
 
     def end(m, _):
-        store_tile(m).wait()
+        for copy in store_tile(m):
+            copy.wait()
         swap_tile(m).wait_send()
         return 0
 
@@ -240,6 +251,7 @@
     hid_ref,
     slope_ref,
     both_grad_ref,
+    late_grad_ref,
     back_ref,
     branch_ref,
     vector_ref,
@@ -293,8 +305,7 @@
     shares = links.sharing(own_ref, full_ref, share_send, share_recv)
     sums = links.summing(send_v, recv_v, sum_send, sum_recv)
     links.pass_on(shares, 0)
-    keep = pltpu.make_async_copy(own_ref, full_ref.at[pl.ds(0, 2 * half)], load_sem.at[0])
-    keep.start()
+    keep = pltpu.make_async_copy(rows_v, full_ref.at[pl.ds(0, 2 * half)], load_sem.at[0])
     first = pltpu.make_async_copy(own_ref, rows_v, load_sem.at[1])
     first.start()
     rise = pltpu.make_async_copy(both_ref.at[:, other_half], rise_v.at[:, own_half], load_sem.at[2])
@@ -307,10 +318,11 @@
     for copy in grad_loads:
         copy.start()
     stores = []
-    tile = min(256, hidden)
+    tile = min(512, hidden)
     for i in range(count):
         if i == 0:
             first.wait()
+            keep.start()
             rise.wait()
             fall.wait()
             for copy in swaps:
@@ -321,6 +333,8 @@
             for part in (0, 1):
                 shares[(i, part)].wait_recv()
             links.pass_on(shares, i)
+            if i == 1:
+                keep.wait()
             row_loads = links.loads(full_ref, rows_v, i, load_sem, 8)
             for copy in row_loads:
                 copy.start()
@@ -363,11 +377,16 @@
                 sums[(i, part)].start()
     for copy in stores:
         copy.wait()
-    keep.wait()
     keep_fall.wait()
     rows_big = rise_big.at[pl.ds(0, length), pl.ds(0, width)]
     columns_big = fall_big.at[pl.ds(0, length), pl.ds(0, hidden)]
     ends = []
+    quarter = hidden // 4
+    results = (
+        (both_grad_ref.at[:, own_half],),
+        (both_grad_ref.at[:, pl.ds(hidden // 2, quarter)], late_grad_ref),
+    )
+    stores = ((grad_store.at[0],), (grad_store.at[1], grad_store.at[2]))
     for n, (left, right) in enumerate(((full_ref, slope_ref), (grads_ref, hid_ref))):
         lefts = pltpu.make_async_copy(left, rows_big, load_sem.at[0])
         rights = pltpu.make_async_copy(right, columns_big, load_sem.at[1])
@@ -384,10 +403,10 @@
                 columns_big,
                 theirs_v,
                 came_v.at[n],
-                both_grad_ref.at[:, pl.ds((1 - n) * (hidden // 2), hidden // 2)],
+                results[n],
                 grad_send.at[n],
                 grad_recv.at[n],
-                grad_store.at[n],
+                stores[n],
             )
         ]
         if n == 0:
@@ -454,7 +473,8 @@
             jax.ShapeDtypeStruct((length, width), BF16),
             jax.ShapeDtypeStruct((length, hidden), BF16),
             jax.ShapeDtypeStruct((length, hidden), BF16),
-            jax.ShapeDtypeStruct((width, hidden), BF16),
+            jax.ShapeDtypeStruct((width, hidden * 3 // 4), BF16),
+            jax.ShapeDtypeStruct((width, hidden // 4), BF16),
             jax.ShapeDtypeStruct((rows, width), F32),
             jax.ShapeDtypeStruct((rows, width), BF16),
             jax.ShapeDtypeStruct((8, width), F32),
@@ -462,7 +482,7 @@
             jax.ShapeDtypeStruct((width, hidden), BF16),
         ),
         in_specs=[anywhere, anywhere, anywhere, inside, anywhere, inside],
-        out_specs=(anywhere,) * 6 + (inside, inside, anywhere),
+        out_specs=(anywhere,) * 7 + (inside, inside, anywhere),
         scratch_shapes=[
             pltpu.VMEM((max(width, length), max(width, hidden)), BF16),
             pltpu.VMEM((max(width, length), hidden), BF16),
@@ -479,9 +499,9 @@
             dma((5,)),
             dma((2,)),
             dma((2,)),
-            dma((2, width // 256)),
-            dma((2, width // 256)),
-            dma((2, width // 256)),
+            dma((3, width // 512)),
+            dma((3, width // 512)),
+            dma((3, width // 512)),
             dma((copies,)),
             dma((copies,)),
             dma((copies,)),
@@ -517,9 +537,9 @@
     ]
 
 
-def piece_copies(count, source, target_ref, send_sem, recv_sem, local_sem):
+def piece_copies(count, source, target_ref, send_sem, recv_sem):
     here = lax.axis_index("ctx")
-    copies = [
+    return [
         pltpu.make_async_remote_copy(
             src_ref=source(lax.bitwise_xor(here, mask)),
             dst_ref=target_ref.at[here],
@@ -530,7 +550,6 @@
         )
         for mask in range(1, count)
     ]
-    return copies + [pltpu.make_async_copy(source(here), target_ref.at[here], local_sem)]
 
 
 class Line:
@@ -593,6 +612,8 @@
     table_ref,
     rows_v,
     normed_v,
+    head_v,
+    piece_v,
     shards_v,
     load_sem,
     store_sem,
@@ -615,9 +636,18 @@
     own_ref = tokens_ref.at[lax.axis_index("tp")]
     greet_all(others("ctx", count) + others("dp", depth))
     heads = piece_copies(
-        count, lambda i: head_pieces_ref.at[i], head_ref.at[layer], head_send, head_recv, load_sem.at[2]
+        count, lambda i: head_pieces_ref.at[i], head_ref.at[layer], head_send, head_recv
+    )
+    pieces = piece_copies(
+        count, lambda i: pieces_ref.at[i], block_ref, piece_send, piece_recv
     )
     for copy in heads:
+        copy.start()
+    own_pieces = [
+        pltpu.make_async_copy(head_pieces_ref.at[here], head_v, load_sem.at[2]),
+        pltpu.make_async_copy(pieces_ref.at[here], piece_v, load_sem.at[0]),
+    ]
+    for copy in own_pieces:
         copy.start()
     first = pltpu.make_async_copy(own_ref, rows_v.at[pl.ds(0, size)], load_sem.at[1])
     first.start()
@@ -643,12 +673,17 @@
     shares = links.sharing(own_ref, rows_v, share_send, share_recv)
     links.pass_on(shares, 0)
     line = Line(head_ref, depth, line_send, line_recv)
+    own_stores = [
+        pltpu.make_async_copy(head_v, head_ref.at[layer, here], load_sem.at[2]),
+        pltpu.make_async_copy(piece_v, block_ref.at[here], load_sem.at[0]),
+    ]
+    for load, store in zip(own_pieces, own_stores):
+        load.wait()
+        store.start()
     for copy in heads:
         copy.wait()
+    own_stores[0].wait()
     line.start(1)
-    pieces = piece_copies(
-        count, lambda i: pieces_ref.at[i], block_ref, piece_send, piece_recv, load_sem.at[0]
-    )
     for copy in pieces:
         copy.start()
     for c in range(count):
@@ -685,7 +720,7 @@
             )
             store.start()
             stores.append(store)
-    for copy in stores + pieces:
+    for copy in stores + pieces + own_stores[1:]:
         copy.wait()
     line.finish()
     for pair in links.pairs:
@@ -714,6 +749,8 @@
         scratch_shapes=[
             pltpu.VMEM((length, width), BF16),
             pltpu.VMEM((length, width), BF16),
+            pltpu.VMEM(head_pieces.shape[1:], BF16),
+            pltpu.VMEM(pieces.shape[1:], BF16),
             pltpu.VMEM((count * depth, *small.shape), F32),
             dma((3,)),
             dma((2 * count,)),
@@ -750,6 +787,7 @@
     key_ref,
     value_ref,
     out_ref,
+    fall_ref,
     features_ref,
     totals_ref,
     block_v,
@@ -780,7 +818,11 @@
         block_v,
         piece_send,
         piece_recv,
-        load_sem.at[0],
+    )
+    pieces.append(
+        pltpu.make_async_copy(
+            rows_ref.at[pl.ds(pl.multiple_of(here * thin, thin), thin)], block_v.at[here], load_sem.at[0]
+        )
     )
     for copy in pieces:
         copy.start()
@@ -854,7 +896,8 @@
                 column = (3 * j + n) * HEAD_DIM
                 ref[:, to] = block_v[c, :, column : column + HEAD_DIM].astype(F32)
         rows = slice(c * heads * HEAD_DIM, (c + 1) * heads * HEAD_DIM)
-        out_ref[rows, :] = block_v[c, :, wide:].astype(F32).T
+        out_ref[rows, :] = block_v[c, :, wide : wide + heads * HEAD_DIM].astype(F32).T
+        fall_ref[c] = block_v[c, :, wide + heads * HEAD_DIM :].astype(F32).T
 
 
 def end(rows, vectors, firsts, biases, heads, count, depth):
@@ -872,11 +915,12 @@
             jax.ShapeDtypeStruct((thin, local), F32),
             jax.ShapeDtypeStruct((thin, local), F32),
             jax.ShapeDtypeStruct((local, thin), F32),
+            jax.ShapeDtypeStruct((count, columns - heads * 4 * HEAD_DIM, thin), F32),
             jax.ShapeDtypeStruct((8, thin), F32),
             jax.ShapeDtypeStruct((count, 1, biases.shape[2]), F32),
         ),
         in_specs=[pl.BlockSpec(memory_space=pl.ANY), inside, inside, inside],
-        out_specs=(inside,) * 6,
+        out_specs=(inside,) * 7,
         scratch_shapes=[
             pltpu.VMEM((count, thin, columns), BF16),
             pltpu.VMEM(shards, F32),
@@ -958,8 +1002,6 @@
     links.pass_on(shares, 0)
     ours = pltpu.make_async_copy(weight_ref, weight_v.at[0], load_sem.at[0])
     ours.start()
-    keep = pltpu.make_async_copy(grads_ref, grads_full_ref.at[pl.ds(0, size)], load_sem.at[1])
-    keep.start()
     own = pltpu.make_async_copy(tokens_ref.at[core], own_v, load_sem.at[4])
     own.start()
 
@@ -995,6 +1037,9 @@
             lax.fori_loop(0, wide // tile, step, 0)
     keep_qkv = pltpu.make_async_copy(qkv_v, qkv_ref, store_sem.at[2])
     keep_qkv.start()
+    own_grads = pltpu.make_async_copy(grads_ref, rows_v.at[0], load_sem.at[1])
+    own_grads.start()
+    keep = pltpu.make_async_copy(rows_v.at[0], grads_full_ref.at[pl.ds(0, size)], load_sem.at[1])
 
     def one_head(head, _):
         @pl.when(head == heads // 2)
@@ -1010,6 +1055,8 @@
     lax.fori_loop(0, heads, one_head, 0)
     keep_mixed = pltpu.make_async_copy(mixed_v, mixed_ref, store_sem.at[3])
     keep_mixed.start()
+    own_grads.wait()
+    keep.start()
     chip = heads * HEAD_DIM // 2
     for i in range(count - 1, -1, -1):
 
@@ -1150,22 +1197,22 @@
     fall_ref,
     first_ref,
     residual_ref,
+    late_ref,
     table_ref,
     full_ref,
     result_ref,
     low_ref,
-    head_grad_ref,
+    late_grad_ref,
     residual_v,
     weight_v,
     qkv_v,
     mixed_v,
     big_v,
-    theirs_v,
+    shared_v,
     came_v,
     grad_v,
     rows_v,
     hid_v,
-    fall_v,
     key_v,
     value_v,
     kept_v,
@@ -1185,89 +1232,134 @@
     here = lax.axis_index("ctx")
     chip = weight_v.shape[2]
     wide = heads * 3 * HEAD_DIM // 2
+    narrow = residual_v.shape[1]
+    middle = hid_v.shape[2] // 2
     partner = {"tp": 1 - lax.axis_index("tp")}
     links.greet([partner])
     shares = links.sharing(own_ref, full_ref, share_send, share_recv)
     sums = links.summing(send_v, recv_v, sum_send, sum_recv)
     links.pass_on(shares, 0)
-    narrow = fall_v.shape[0]
+    falls = [shared_v.at[pl.ds(n * narrow, narrow), pl.ds(0, middle)] for n in (0, 1)]
+    theirs_v = shared_v.at[pl.ds(0, big_v.shape[1])]
+    late_v = shared_v.at[pl.ds(0, big_v.shape[1]), pl.ds(0, late_ref.shape[1])]
     loads = [
         pltpu.make_async_copy(source, target, load_sem.at[n])
         for n, (source, target) in enumerate(
             (
-                (fall_ref.at[pl.ds(0, narrow)], fall_v),
+                (fall_ref.at[pl.ds(0, narrow), pl.ds(0, middle)], falls[0]),
+                (fall_ref.at[pl.ds(0, narrow), pl.ds(middle, middle)], falls[1]),
                 (own_ref, rows_v),
                 (weight_ref.at[:, :, pl.ds(weight_ref.shape[2] - chip, chip)], weight_v),
                 (qkv_ref, qkv_v),
                 (mixed_ref, mixed_v),
-                (own_ref, full_ref.at[pl.ds(0, size)]),
+                (rows_v, full_ref.at[pl.ds(0, size)]),
                 (first_ref, big_v),
                 (residual_ref.at[:, pl.ds(0, narrow)], residual_v),
+                (late_ref, late_v),
+                (late_v, late_grad_ref.at[:, pl.ds(wide + chip, late_ref.shape[1])]),
             )
         )
     ]
-    for copy in loads:
-        copy.start()
-    loads[0].wait()
-    out_terms(links, hid_ref, hid_v, fall_v, kept_v, send_v, load_sem, 8)
+    for n in (0, 1, 2, 3, 4, 5, 7, 8):
+        loads[n].start()
+    key_v[...] = jnp.zeros_like(key_v)
+    value_v[...] = jnp.zeros_like(value_v)
+    for copy in loads[:2]:
+        copy.wait()
+    out_terms(
+        links,
+        hid_ref,
+        hid_v,
+        lambda rows, at: across(rows[:, 0:middle], falls[0][at, :])
+        + across(rows[:, middle : 2 * middle], falls[1][at, :]),
+        narrow,
+        kept_v,
+        send_v,
+        load_sem,
+        11,
+    )
+    loads[9].start()
+    for copy in loads[2:6]:
+        copy.wait()
+    loads[6].start()
+    loads[9].wait()
+    loads[10].start()
+    together = min(2, heads)
     for i in range(count):
-        if i == 0:
-            loads[1].wait()
-            loads[2].wait()
-        else:
+        if i:
             for part in (0, 1):
                 shares[(i, part)].wait_recv()
             links.pass_on(shares, i)
-            unit_loads = links.loads(full_ref, rows_v, i, load_sem, 8)
+            if i == 1:
+                loads[6].wait()
+            unit_loads = links.loads(full_ref, rows_v, i, load_sem, 11)
             for copy in unit_loads:
                 copy.start()
             for copy in unit_loads:
                 copy.wait()
+        if i + 1 == count:
+            for j in range(count - 1, count // 2 - 1, -1):
+                for part in (0, 1):
+                    sums[(j, part)].start()
         for core in (0, 1):
             term = product(rows_v[...], weight_v[core]).astype(BF16)
             for part in (0, 1):
-                first = links.start_row(i, part)
-                grad_v[first : first + half, core * chip : (core + 1) * chip] = term[
+                row = links.start_row(i, part)
+                grad_v[row : row + half, core * chip : (core + 1) * chip] = term[
                     part * half : (part + 1) * half
                 ]
-    for i in range(count - 1, count // 2 - 1, -1):
-        for part in (0, 1):
-            sums[(i, part)].start()
-    loads[3].wait()
-    loads[4].wait()
-
-    def one_head(head, _):
-        @pl.when(head == heads // 2)
-        def _():
-            links.combine(sums, kept_v, send_v, recv_v, count // 2 - 1, 1)
-
-        attend_backward_head(
-            here, head, size, count, qkv_v, grad_v, mixed_v, log_ref, result_ref, key_v, value_v
-        )
+        blocks = [links.block(i, part) for part in (0, 1)]
+        firsts = [links.start_row(i, part) for part in (0, 1)]
+
+        def one(n, _, blocks=blocks, firsts=firsts):
+            part, first_head = n // (heads // together), n % (heads // together) * together
+            row = pl.multiple_of(firsts[0] + part * (firsts[1] - firsts[0]), half)
+            block = lax.bitwise_xor(here, blocks[0] + part * (blocks[1] - blocks[0]))
+            attend_backward_unit(
+                here,
+                [first_head + m for m in range(together)],
+                block,
+                part * half,
+                row,
+                half,
+                qkv_v,
+                grad_v,
+                mixed_v,
+                log_ref,
+                result_ref,
+                key_v,
+                value_v,
+            )
+            return 0
+
+        lax.fori_loop(0, 2 * heads // together, one, 0)
+
+    def store_head(head, _):
+        at = pl.ds(pl.multiple_of(head * HEAD_DIM, HEAD_DIM), HEAD_DIM)
+        column = head * (3 * HEAD_DIM)
+        key_at = pl.ds(pl.multiple_of(column + HEAD_DIM, HEAD_DIM), HEAD_DIM)
+        value_at = pl.ds(pl.multiple_of(column + 2 * HEAD_DIM, HEAD_DIM), HEAD_DIM)
+        result_ref[:, key_at] = (key_v[:, at] * HEAD_DIM ** (-0.5)).astype(BF16)
+        result_ref[:, value_at] = value_v[:, at].astype(BF16)
         return 0
 
-    lax.fori_loop(0, heads, one_head, 0)
-    loads[5].wait()
-    loads[6].wait()
+    lax.fori_loop(0, heads, store_head, 0)
+    loads[10].wait()
+    loads[7].wait()
     end_first = weight_grads(
         partner,
         big_v,
         result_ref,
         theirs_v.at[:, pl.ds(0, wide)],
         came_v.at[:, pl.ds(0, wide)],
-        head_grad_ref.at[:, pl.ds(0, wide)],
+        (late_grad_ref.at[:, pl.ds(0, wide)],),
         grad_send.at[0],
         grad_recv.at[0],
-        grad_store.at[0],
-    )
-    again = pltpu.make_async_copy(full_ref, big_v, load_sem.at[6])
+        (grad_store.at[0],),
+    )
+    again = pltpu.make_async_copy(full_ref, big_v, load_sem.at[7])
     again.start()
-    loads[7].wait()
-
-    def low(part, at, to, value):
-        low_ref[to, :] = (residual_v[to, :] + (value + table_ref[5:6, 0:narrow])).astype(BF16)
-
-    links.combine(sums, kept_v, send_v, recv_v, 0, 0, low)
+    links.combine(sums, kept_v, send_v, recv_v, count // 2 - 1, 1)
     again.wait()
     end_second = weight_grads(
         partner,
@@ -1275,11 +1367,17 @@
         mixed_v,
         theirs_v.at[:, pl.ds(wide, chip)],
         came_v.at[:, pl.ds(wide, chip)],
-        head_grad_ref.at[:, pl.ds(wide, chip)],
+        (late_grad_ref.at[:, pl.ds(wide, chip)],),
         grad_send.at[1],
         grad_recv.at[1],
-        grad_store.at[1],
-    )
+        (grad_store.at[1],),
+    )
+    loads[8].wait()
+
+    def low(part, at, to, value):
+        low_ref[to, :] = (residual_v[to, :] + (value + table_ref[5:6, 0:narrow])).astype(BF16)
+
+    links.combine(sums, kept_v, send_v, recv_v, 0, 0, low)
     end_first()
     end_second()
     for pair in links.pairs:
@@ -1287,74 +1385,76 @@
         shares[pair].wait_send()
 
 
-def out_terms(links, hid_ref, hid_v, fall_v, kept_v, send_v, load_sem, base):
-    count, half = links.count, links.half
+def attend_backward_unit(
+    here, heads, block, offset, row, half, qkv_v, grad_v, mixed_v, log_ref, result_ref, key_v, value_v
+):
+    size = 2 * half
+    scaling = HEAD_DIM ** (-0.5)
+    at = pl.ds(row, half)
+
+    def columns(head, n):
+        return pl.ds(pl.multiple_of(head * (3 * HEAD_DIM) + n * HEAD_DIM, HEAD_DIM), HEAD_DIM)
+
+    places = [pl.ds(pl.multiple_of(head * HEAD_DIM, HEAD_DIM), HEAD_DIM) for head in heads]
+    queries = [qkv_v[at, columns(head, 0)] for head in heads]
+    grads = [grad_v[at, place] for place in places]
+    centres = [
+        jnp.sum((grad.astype(F32) * mixed_v[at, place].astype(F32)).T, axis=0, keepdims=True)
+        for grad, place in zip(grads, places)
+    ]
+    logs = [log_ref[head, 0:1, at] for head in heads]
+
+    def step(j, query_grads, last):
+        there = pl.ds(rows_of(here, j, size), size)
+        results = []
+        for n, head in enumerate(heads):
+            keys = qkv_v[there, columns(head, 1)]
+            values = qkv_v[there, columns(head, 2)]
+            weights = jnp.exp(across(keys, queries[n]) * scaling - logs[n])
+            if last:
+                behind = lax.broadcasted_iota(jnp.int32, (size, half), 0) <= offset + (
+                    lax.broadcasted_iota(jnp.int32, (size, half), 1)
+                )
+                weights = jnp.where(behind, weights, 0.0)
+            slopes = (weights * (across(values, grads[n]) - centres[n])).astype(BF16)
+            value_v[there, places[n]] += product(weights.astype(BF16), grads[n])
+            key_v[there, places[n]] += product(slopes, queries[n])
+            results.append(query_grads[n] + inner(slopes, keys))
+        return tuple(results)
+
+    query_grads = lax.fori_loop(
+        0,
+        block,
+        lambda j, found: step(j, found, False),
+        tuple(jnp.zeros((half, HEAD_DIM), F32) for _ in heads),
+    )
+    query_grads = step(block, query_grads, True)
+    for n, head in enumerate(heads):
+        result_ref[at, columns(head, 0)] = (query_grads[n] * scaling).astype(BF16)
+
+
+def out_terms(links, hid_ref, hid_v, columns, narrow, kept_v, send_v, load_sem, base):
+    count, slots = links.count, hid_v.shape[0]
     order = list(range(count - 1, -1, -1))
-    unit_loads = links.loads(hid_ref, hid_v.at[0], order[0], load_sem, base)
-    for copy in unit_loads:
-        copy.start()
+
+    def load(n):
+        slot = n % slots
+        copies = links.loads(hid_ref, hid_v.at[slot], order[n], load_sem, base + 2 * slot)
+        for copy in copies:
+            copy.start()
+        return copies
+
+    coming = [load(n) for n in range(slots)]
     for n, i in enumerate(order):
-        for copy in unit_loads:
+        for copy in coming[n]:
             copy.wait()
-        if n + 1 < count:
-            unit_loads = links.loads(
-                hid_ref, hid_v.at[(n + 1) % 2], order[n + 1], load_sem, base + 2 * ((n + 1) % 2)
-            )
-            for copy in unit_loads:
-                copy.start()
-        links.terms(
-            i, lambda at, n=n: across(hid_v[n % 2], fall_v[at, :]), fall_v.shape[0], kept_v, send_v
-        )
-
-
-def attend_backward_head(
-    here, head, size, blocks, qkv_v, grad_v, mixed_v, log_ref, result_ref, key_v, value_v
-):
-    scaling = HEAD_DIM ** (-0.5)
-    behind = lax.broadcasted_iota(jnp.int32, (size, size), 0) <= lax.broadcasted_iota(
-        jnp.int32, (size, size), 1
-    )
-    column = pl.multiple_of(head * (3 * HEAD_DIM), HEAD_DIM)
-    query_at = pl.ds(column, HEAD_DIM)
-    key_at = pl.ds(pl.multiple_of(column + HEAD_DIM, HEAD_DIM), HEAD_DIM)
-    value_at = pl.ds(pl.multiple_of(column + 2 * HEAD_DIM, HEAD_DIM), HEAD_DIM)
-    head_at = pl.ds(pl.multiple_of(head * HEAD_DIM, HEAD_DIM), HEAD_DIM)
-    for i in range(blocks):
-        at = pl.ds(rows_of(here, i, size), size)
-        queries = qkv_v[at, query_at]
-        grads = grad_v[at, head_at]
-        both = grads.astype(F32) * mixed_v[at, head_at].astype(F32)
-        centre = jnp.sum(both.T, axis=0, keepdims=True)
-        log_total = log_ref[head, 0:1, at]
-        query_grad = jnp.zeros((size, HEAD_DIM), F32)
-        for j in range(i + 1):
-            there = pl.ds(rows_of(here, j, size), size)
-            keys = qkv_v[there, key_at]
-            values = qkv_v[there, value_at]
-            weights = jnp.exp(across(keys, queries) * scaling - log_total)
-            if j == i:
-                weights = jnp.where(behind, weights, 0.0)
-            slopes = (weights * (across(values, grads) - centre)).astype(BF16)
-            value_term = product(weights.astype(BF16), grads)
-            key_term = product(slopes, queries)
-            query_grad = query_grad + inner(slopes, keys)
-            place = slice(j * size, (j + 1) * size)
-            if i == j:
-                value_v[place, :] = value_term
-                key_v[place, :] = key_term
-            else:
-                value_v[place, :] += value_term
-                key_v[place, :] += key_term
-        result_ref[at, query_at] = (query_grad * scaling).astype(BF16)
-    for j in range(blocks):
-        there = pl.ds(rows_of(here, j, size), size)
-        place = slice(j * size, (j + 1) * size)
-        result_ref[there, key_at] = (key_v[place, :] * scaling).astype(BF16)
-        result_ref[there, value_at] = value_v[place, :].astype(BF16)
+        links.terms(i, lambda at, n=n: columns(hid_v.at[n % slots], at), narrow, kept_v, send_v)
+        if n + slots < count:
+            coming.append(load(n + slots))
 
 
 def attend_back(
-    own, weight, qkv, mixed, log_total, hid, fall_weight, first, residual, table, count
+    own, weight, qkv, mixed, log_total, hid, fall_weight, first, residual, late, table, count
 ):
     rows, width = own.shape
     length, columns = qkv.shape
@@ -1373,9 +1473,9 @@
             jax.ShapeDtypeStruct((length, width), BF16),
             jax.ShapeDtypeStruct((length, columns), BF16),
             jax.ShapeDtypeStruct((rows, narrow), BF16),
-            jax.ShapeDtypeStruct((width, 2 * heads * HEAD_DIM), BF16),
+            jax.ShapeDtypeStruct((width, 2 * heads * HEAD_DIM + late.shape[1]), BF16),
         ),
-        in_specs=[anywhere] * 4 + [inside] + [anywhere] * 4 + [inside],
+        in_specs=[anywhere] * 4 + [inside] + [anywhere] * 5 + [inside],
         out_specs=(anywhere, inside, inside, anywhere),
         scratch_shapes=[
             pltpu.VMEM((rows, narrow), F32),
@@ -1383,21 +1483,20 @@
             pltpu.VMEM(qkv.shape, BF16),
             pltpu.VMEM(mixed.shape, BF16),
             pltpu.VMEM((length, width), BF16),
-            pltpu.VMEM((width, 2 * heads * HEAD_DIM), BF16),
+            pltpu.VMEM((width, max(2 * heads * HEAD_DIM, hidden // 2)), BF16),
             pltpu.VMEM((width, 2 * heads * HEAD_DIM), BF16),
             pltpu.VMEM(mixed.shape, BF16),
             pltpu.VMEM((rows, width), BF16),
-            pltpu.VMEM((2, rows, hidden), BF16),
-            pltpu.VMEM((narrow, hidden), BF16),
-            pltpu.VMEM((length, HEAD_DIM), F32),
-            pltpu.VMEM((length, HEAD_DIM), F32),
+            pltpu.VMEM((1, rows, hidden), BF16),
+            pltpu.VMEM(mixed.shape, F32),
+            pltpu.VMEM(mixed.shape, F32),
             pltpu.VMEM((count, half, narrow), F32),
             pltpu.VMEM((copies, half, narrow), BF16),
             pltpu.VMEM((copies, half, narrow), BF16),
-            dma((12,)),
-            dma((2, width // 256)),
-            dma((2, width // 256)),
-            dma((2, width // 256)),
+            dma((13,)),
+            dma((3, width // 512)),
+            dma((3, width // 512)),
+            dma((3, width // 512)),
             dma((copies,)),
             dma((copies,)),
             dma((copies,)),
@@ -1412,7 +1511,7 @@
             transcendentals=pairs,
         ),
         name="attend_back",
-    )(own, weight, qkv, mixed, log_total, hid, fall_weight, first, residual, table)
+    )(own, weight, qkv, mixed, log_total, hid, fall_weight, first, residual, late, table)
 
 
 def first_back_kernel(
@@ -1461,7 +1560,7 @@
     size = 2 * half
     wide = weight_v.shape[2]
     thin = hidden_ref.shape[0] // count
-    hidden = hidden_ref.shape[1] // 2
+    hidden = hidden_ref.shape[1] * 2 // 3
     narrow = fall_v.shape[0]
     core = lax.axis_index("tp")
     partner = {"tp": 1 - core}
@@ -1474,7 +1573,14 @@
         block_v,
         piece_send,
         piece_recv,
-        load_sem.at[10],
+    )
+    here = lax.axis_index("ctx")
+    pieces.append(
+        pltpu.make_async_copy(
+            hidden_ref.at[pl.ds(pl.multiple_of(here * thin, thin), thin)],
+            block_v.at[here],
+            load_sem.at[10],
+        )
     )
     right = pl.ds(narrow, narrow)
     left = pl.ds(0, narrow)
@@ -1493,7 +1599,10 @@
             ),
         ]
 
-    outs = both_cores(0, low_ref, out_ref, pl.ds(0, size), left)
+    lows = both_cores(0, high_v, out_ref, pl.ds(0, size), left)
+    low = pltpu.make_async_copy(low_ref, high_v, load_sem.at[11])
+    low.start()
+    outs = []
     loads = [
         pltpu.make_async_copy(source, target, load_sem.at[n])
         for n, (source, target) in enumerate(
@@ -1513,7 +1622,10 @@
         copy.start()
     order = list(range(count - 1, -1, -1))
     unit_loads = links.loads(grads_ref, grads_v.at[0], order[0], load_sem, 2)
-    for copy in unit_loads + pieces + more + outs:
+    for copy in unit_loads + pieces + more:
+        copy.start()
+    low.wait()
+    for copy in lows:
         copy.start()
     bias_ref[...] = jnp.zeros_like(bias_ref)
     vector_ref[...] = jnp.zeros_like(vector_ref)
@@ -1548,13 +1660,22 @@
 
         lax.fori_loop(0, size // chunk, bias, 0)
     loads[1].wait()
-    out_terms(links, hid_ref, hid_v, fall_v, kept_w, send_w, load_sem, 6)
+    out_terms(
+        links,
+        hid_ref,
+        hid_v,
+        lambda rows, at: across(rows[...], fall_v[at, :]),
+        narrow,
+        kept_w,
+        send_w,
+        load_sem,
+        6,
+    )
     for copy in pieces:
         copy.wait()
     for c in range(count):
-        rows = slice(c * hidden, (c + 1) * hidden)
-        fall_grad_ref[rows, :] = block_v[c, :, 0:hidden].astype(F32).T
-        rise_grad_ref[:, rows] = block_v[c, :, hidden : 2 * hidden].astype(F32)
+        rise_grad_ref[:, c * hidden : (c + 1) * hidden] = block_v[c, :, 0:hidden].astype(F32)
+        fall_grad_ref[c] = block_v[c, :, hidden:].astype(F32).T
     links.combine(sums, kept_v, send_v, recv_v, count // 2 - 1, 1)
     backs = [
         pltpu.make_async_copy(
@@ -1593,6 +1714,8 @@
             residual_v[to, :] + (value + table_ref[5:6, narrow : 2 * narrow])
         ).astype(BF16)
 
+    for copy in lows:
+        copy.wait()
     links.combine(lates, kept_w, send_w, recv_w, count // 2 - 1, 0, high)
     copies = both_cores(3, high_v, out_ref, pl.ds(0, size), right)
     for copy in copies:
@@ -1613,7 +1736,7 @@
     links = Links(count, rows // 2)
     half, copies = links.half, len(links.pairs)
     narrow = width // 2
-    thin, piece = hidden_rows.shape[0] // count, hidden_rows.shape[1] // 2
+    thin, piece = hidden_rows.shape[0] // count, hidden_rows.shape[1] * 2 // 3
     anywhere = pl.BlockSpec(memory_space=pl.ANY)
     inside = pl.BlockSpec(memory_space=pltpu.VMEM)
     dma = pltpu.SemaphoreType.DMA
@@ -1624,7 +1747,7 @@
             jax.ShapeDtypeStruct((2, rows, width), BF16),
             jax.ShapeDtypeStruct((8, width), F32),
             jax.ShapeDtypeStruct((1, columns), F32),
-            jax.ShapeDtypeStruct((count * piece, thin), F32),
+            jax.ShapeDtypeStruct((count, piece // 2, thin), F32),
             jax.ShapeDtypeStruct((thin, count * piece), F32),
         ),
         in_specs=[anywhere] * 8 + [inside, anywhere],
@@ -1643,7 +1766,7 @@
             pltpu.VMEM((rows, narrow), F32),
             pltpu.VMEM((rows, width), BF16),
             pltpu.VMEM((rows, narrow), BF16),
-            pltpu.VMEM((count, thin, 2 * piece), BF16),
+            pltpu.VMEM((count, thin, piece * 3 // 2), BF16),
             dma((17,)),
             dma((4,)),
             dma((4,)),
@@ -1736,17 +1859,28 @@
     qkv, mixed, log_total, grads_in, residual, input_two, head_whole = attend(
         ones, head_weights, qkv_shift[None], cotangent, tokens, table, 2 * heads, ctx
     )
-    _, hid, _, hidden_both, residual_grad, branch_grad, vectors, rise_bias, fall_weight = (
+    _, hid, _, hidden_both, late, residual_grad, branch_grad, vectors, rise_bias, fall_weight = (
         feed_forward(input_two, grads_in, hidden_weights, rise_shift[None], residual, table, ctx)
     )
     hidden_rows = over_dp(hidden_both)
 
     _, qkv_grads, low_columns, head_both = attend_back(
-        branch_grad, head_whole, qkv, mixed, log_total, hid, fall_weight, ones, residual, table, ctx
+        branch_grad,
+        head_whole,
+        qkv,
+        mixed,
+        log_total,
+        hid,
+        fall_weight,
+        ones,
+        residual,
+        late,
+        table,
+        ctx,
     )
     head_both, hidden_rows = lax.optimization_barrier((head_both, hidden_rows))
     head_rows = over_dp(head_both)
-    outputs, input_grads, firsts, qkv_bias, fall_grad, rise_grad = first_back(
+    outputs, input_grads, firsts, qkv_bias, fall_first, rise_grad = first_back(
         qkv_grads,
         head_whole,
         hid,
@@ -1762,9 +1896,10 @@
     biases = jnp.concatenate(
         [rise_bias.reshape(2, 1, hidden), qkv_bias.reshape(2, 1, wide)], axis=2
     )
-    query_grad, key_grad, value_grad, out_grad, features, totals = end(
+    query_grad, key_grad, value_grad, out_grad, fall_second, features, totals = end(
         head_rows, vectors, firsts, biases, heads, ctx, dp
     )
+    fall_grad = jnp.concatenate([fall_first, fall_second], axis=1).reshape(-1, thin)
     totals = totals[:, 0]
     qkv_bias = totals[:, hidden:].reshape(ctx * heads, 3, HEAD_DIM)
     return (

time: 768 us -> 741 us (0.965)
  Pallas kernels: 711 us -> 689 us
    pallas_call x1, Pallas kernels: 137 us -> 120 us  [attend_back(): pl.pallas_call(functools.partial(attend_back_kernel, links, heads), out_s...]
    unnamed x45 -> x44, local copies, waits for them, and re-layouts: 24.2 us -> 21.7 us
  transfers between devices with their start and end apart: 4 -> 4, of which waited for: 2 -> 1; matrix products, arithmetic and copies ran while one was open for 0% -> 0% of each run, Pallas kernels for 54% -> 54%
where the time goes in v5:
time: 741 us; the launch traced here: 737 us
  Pallas kernels  689 us (93%)
  local copies, waits for them, and re-layouts  26.3 us (4%)
  between operations  14.5 us (2%)
    pallas_call x1, Pallas kernels, feed_forward(): pl.pallas_call(functools.partial(feed_forward_kernel, links), out_shape=(...  153 us
    pallas_call x1, Pallas kernels, attend(): pl.pallas_call(functools.partial(attend_kernel, links, heads), out_shape=...  146 us
    pallas_call x1, Pallas kernels, first_back(): pl.pallas_call(functools.partial(first_back_kernel, links), out_shape=(ja...  129 us
    pallas_call x1, Pallas kernels, attend_back(): pl.pallas_call(functools.partial(attend_back_kernel, links, heads), out_s...  120 us
    pallas_call x1, Pallas kernels, front(): pl.pallas_call(functools.partial(front_kernel, links, depth), out_shape=(...  117 us
    pallas_call x1, Pallas kernels, end(): pl.pallas_call(functools.partial(end_kernel, count, depth, heads), out_sh...  24.1 us
    unnamed x44, local copies, waits for them, and re-layouts  21.7 us
  transfers between devices with their start and end apart: 4, of which 1 were waited for; matrix products, arithmetic and copies ran while one was open for 0% of the time, Pallas kernels for 54%

profile of v5, /device:TPU:0, one launch (start us, length us, event | category | flops | bytes accessed | tf_op | source)
XLA Modules:
  0.0 736.6 jit_solution(6068076228141202234)
XLA Ops:
  7.3 0.9 stack.34
  8.1 1.1 copy.37
  9.2 1.1 copy.38
  10.4 1.1 copy.39
  12.1 0.7 copy.43
  13.3 1.5 copy.42
  15.2 1.9 copy-done
  17.0 116.9 %front.1 = (bf16[2048,2048]{1,0:T(8,128)(2,1)}, bf16[4,4,128,1024]{3,2,1,0:T(8,128)(2,1)S(1)}, bf16[4,128,2048]{2,1,0:T(8,128)(2,1)}, f32[8,2048]{1,0:T(8,128)S(1)}) custom-call(bf16[2,512,2048]{2,1,0:T(8,128)(2,1)S(1)} %copy-done, bf16[4,128,1024]{2,1,0:T(8,128)(2,1)S(1)} %pad_maximum_fusion.2.head_pieces_ref, ...), custom_call_target="tpu_custom_call" | custom-call | flops 83886080 | bytes 120000000 | tf_op jit(solution)/shard_map/front/pallas_call | solution.py:739
  134.0 2.0 copy-done.4
  136.0 0.6 copy-done.5
  137.3 1.1 collective-permute-done
  138.4 0.6 maximum_convert_fusion.1.shift_ref
  139.0 0.6 maximum_convert_fusion.shift_ref
  139.7 146.3 %attend.1 = (bf16[2048,1536]{1,0:T(8,128)(2,1)}, bf16[2048,512]{1,0:T(8,128)(2,1)}, f32[4,8,2048]{2,1,0:T(8,128)}, bf16[2048,2048]{1,0:T(8,128)(2,1)}, f32[512,2...) custom-call(bf16[2048,2048]{1,0:T(8,128)(2,1)} %get-tuple-element.54.rows_ref.first_ref, ...), custom_call_target="tpu_custom_call" | custom-call | flops 27917287424 | bytes 33554432 | tf_op jit(solution)/shard_map/attend/pallas_call | solution.py:1144
  286.0 152.9 %feed_forward.1 = (bf16[2048,2048]{1,0:T(8,128)(2,1)}, bf16[2048,2048]{1,0:T(8,128)(2,1)}, bf16[2048,2048]{1,0:T(8,128)(2,1)}, bf16[2048,1536]{1,0:T(8,128)(2,1)...) custom-call(bf16[512,2048]{1,0:T(8,128)(2,1)} %get-tuple-element.57., ...), custom_call_target="tpu_custom_call" | custom-call | flops 85899345920 | bytes 67108864 | tf_op jit(solution)/shard_map/feed_forward/pallas_call | solution.py:470
  439.0 119.8 %attend_back.1 = (bf16[2048,2048]{1,0:T(8,128)(2,1)}, bf16[2048,1536]{1,0:T(8,128)(2,1)}, bf16[512,1024]{1,0:T(8,128)(2,1)}, bf16[2048,1536]{1,0:T(8,128)(2,1)}) custom-call(bf16[512,2048]{1,0:T(8,128)(2,1)} %get-tuple-element.61.own_ref, bf16[2,2048,1024]{2,1,0:T(8,128)(2,1)} %get-tuple-element.62.weight_ref, bf16[2048,1536]{1,0:T(8,128)(2,1)} %get-tuple-element.63.qkv_ref, ...), custom_call_target="tpu_custom_call" | custom-call | flops 39728447488 | bytes 46137344 | tf_op jit(solution)/shard_map/attend_back/pallas_call | solution.py:1470
  558.9 128.6 %first_back.1 = (bf16[2,512,2048]{2,1,0:T(8,128)(2,1)}, bf16[2,512,2048]{2,1,0:T(8,128)(2,1)}, f32[8,2048]{1,0:T(8,128)}, f32[1,1536]{1,0:T(1,128)}, f32[4,512,128]{2,1,0:T(8,128)}, /*index=5*/f32[128,4096]{1,0:T(8,128)}) custom-call(bf16[2048,1536]{1,0:T(8,128)(2,1)} %get-tuple-element.69.grads_ref, bf16[2,2048,1024]{2,1,0:T(8,128)(2,1)} %get-tuple-element.62.weight_ref, ...), custom_call_target="tpu_custom_call" | custom-call | flops 21474836480 | bytes 29360128 | tf_op jit(solution)/shard_map/first_back/pallas_call | solution.py:1743
  687.5 0.7 pad_maximum_fusion.4.biases_ref
  688.3 1.4 copy-done.1
  689.7 0.8 copy-done.3
  690.5 24.1 %end.1 = (f32[128,1024]{1,0:T(8,128)S(1)}, f32[128,1024]{1,0:T(8,128)S(1)}, f32[128,1024]{1,0:T(8,128)S(1)}, f32[1024,128]{1,0:T(8,128)S(1)}, f32[4,512,128]{2,1...) custom-call(bf16[512,1536]{1,0:T(8,128)(2,1)S(1)} %copy-done.1, f32[8,2048]{1,0:T(8,128)S(1)} %copy-done.2, ...), custom_call_target="tpu_custom_call" | custom-call | bytes 40000000 | tf_op jit(solution)/shard_map/end/pallas_call | solution.py:911
  715.2 0.6 copy.50
  715.8 0.6 fusion.1
  716.4 3.0 pad_maximum_fusion.1
  719.4 2.1 copy.58
  721.5 1.6 copy-done.6
  723.1 2.0 copy.59
  725.1 0.8 copy.60
  725.9 0.8 copy.61
  726.7 0.8 copy.62
  727.5 0.8 copy.63
  728.3 1.3 copy.64
  (60 shorter events, 2.8 us)
Async XLA Ops:
  7.2 4.7 copy-start.10
  7.2 4.9 copy-start.9
  7.2 278.8 %all-gather.2.cloned.1.call-start = ((), (), s32[]{:S(2)}) async-start(), calls=%async_computation.2 | async-start | bytes 10485760 | tf_op jit(solution)/shard_map/all_gather | solution.py:1856
  14.8 2.2 copy-start
  17.0 119.9 %copy-start.13 = (bf16[1024]{0:T(1024)(128)(2,1)S(1)}, bf16[1024]{0:T(1024)(128)(2,1)}, u32[]{:S(2)}) copy-start(bf16[1024]{0:T(1024)(128)(2,1)} %param.24) | copy-start | bytes 6148
  17.0 119.9 %copy-start.14 = (bf16[1024]{0:T(1024)(128)(2,1)S(1)}, bf16[1024]{0:T(1024)(128)(2,1)}, u32[]{:S(2)}) copy-start(bf16[1024]{0:T(1024)(128)(2,1)} %param.27) | copy-start | bytes 6148
  17.0 120.1 %copy-start.12 = (bf16[4096]{0:T(1024)(128)(2,1)S(1)}, bf16[4096]{0:T(1024)(128)(2,1)}, u32[]{:S(2)}) copy-start(bf16[4096]{0:T(1024)(128)(2,1)} %param.31) | copy-start | bytes 24580
  134.0 2.0 copy-start.4
  136.0 0.6 copy-start.5
  136.6 422.2 %reduce-scatter.3.cloned.1.call-start = ((), (), s32[]{:S(2)}) async-start(), calls=%async_computation.3 | async-start | bytes 7864320 | tf_op jit(solution)/shard_map/reduce_scatter | solution.py:49
  137.2 1.2 collective-permute-start
  439.0 249.3 %reduce-scatter.5.cloned.1.call-start = ((), (), s32[]{:S(2)}) async-start(), calls=%async_computation.4 | async-start | bytes 7864320 | tf_op jit(solution)/shard_map/reduce_scatter | solution.py:49
  558.9 128.6 %copy-start.11 = (f32[1,2048]{1,0:T(1,128)S(1)}, f32[1,2048]{1,0:T(1,128)}, u32[]{:S(2)}) copy-start(f32[1,2048]{1,0:T(1,128)} %get-tuple-element.80) | copy-start | bytes 24580
  558.9 129.3 %copy-start.2 = (f32[8,2048]{1,0:T(8,128)S(1)}, f32[8,2048]{1,0:T(8,128)}, u32[]{:S(2)}) copy-start(f32[8,2048]{1,0:T(8,128)} %get-tuple-element.78.vectors_ref) | copy-start | bytes 196612
  688.2 1.4 copy-start.1
  689.7 0.8 copy-start.3
  715.8 3.6 copy-start.7
  719.4 3.7 copy-start.6
  725.1 3.2 copy-start.8
Sparse Core Ops, SparseCore 0:
  136.7 147.7 all-gather.1
  439.1 108.8 reduce-scatter.2
  559.0 110.4 reduce-scatter.4

commit v6 on v5

--- a/solution.py
+++ b/solution.py
@@ -318,17 +318,16 @@
     for copy in grad_loads:
         copy.start()
     stores = []
-    tile = min(512, hidden)
+    tile = min(512, hidden // 2)
+    rows_big = rise_big.at[pl.ds(0, length), pl.ds(0, width)]
+    columns_big = fall_big.at[pl.ds(0, length), pl.ds(0, hidden)]
+    early = pltpu.make_async_copy(slope_ref, columns_big, load_sem.at[1])
     for i in range(count):
         if i == 0:
             first.wait()
             keep.start()
             rise.wait()
             fall.wait()
-            for copy in swaps:
-                copy.wait_recv()
-            keep_fall = pltpu.make_async_copy(fall_v, fall_ref, store_sem.at[4])
-            keep_fall.start()
         else:
             for part in (0, 1):
                 shares[(i, part)].wait_recv()
@@ -355,7 +354,13 @@
             bias_ref[0:1, at] += jnp.sum(slope.astype(F32), axis=0, keepdims=True)
             return 0
 
-        lax.fori_loop(0, hidden // tile, rise_step, 0)
+        lax.fori_loop(0, hidden // 2 // tile, rise_step, 0)
+        if i == 0:
+            for copy in swaps:
+                copy.wait_recv()
+            keep_fall = pltpu.make_async_copy(fall_v, fall_ref, store_sem.at[4])
+            keep_fall.start()
+        lax.fori_loop(hidden // 2 // tile, hidden // tile, rise_step, 0)
         if i + 1 < count:
             grad_loads = links.loads(grads_ref, grads_v, i + 1, load_sem, 4)
             for copy in grad_loads:
@@ -371,27 +376,27 @@
                 copy.start()
                 stores.append(copy)
 
+        if i + 1 == count:
+            for copy in stores + [keep_fall]:
+                copy.wait()
+            early.start()
         links.terms(i, lambda at: across(slope_v[...], rise_v[at, :]), width, kept_v, send_v)
         if i >= count // 2:
             for part in (0, 1):
                 sums[(i, part)].start()
-    for copy in stores:
-        copy.wait()
-    keep_fall.wait()
-    rows_big = rise_big.at[pl.ds(0, length), pl.ds(0, width)]
-    columns_big = fall_big.at[pl.ds(0, length), pl.ds(0, hidden)]
     ends = []
     quarter = hidden // 4
     results = (
         (both_grad_ref.at[:, own_half],),
         (both_grad_ref.at[:, pl.ds(hidden // 2, quarter)], late_grad_ref),
     )
-    stores = ((grad_store.at[0],), (grad_store.at[1], grad_store.at[2]))
+    grad_stores = ((grad_store.at[0],), (grad_store.at[1], grad_store.at[2]))
     for n, (left, right) in enumerate(((full_ref, slope_ref), (grads_ref, hid_ref))):
         lefts = pltpu.make_async_copy(left, rows_big, load_sem.at[0])
-        rights = pltpu.make_async_copy(right, columns_big, load_sem.at[1])
+        rights = pltpu.make_async_copy(right, columns_big, load_sem.at[1]) if n else early
         lefts.start()
-        rights.start()
+        if n:
+            rights.start()
         for end in ends:
             end()
         lefts.wait()
@@ -406,7 +411,7 @@
                 results[n],
                 grad_send.at[n],
                 grad_recv.at[n],
-                stores[n],
+                grad_stores[n],
             )
         ]
         if n == 0:
@@ -631,10 +636,43 @@
     count, half = links.count, links.half
     size = 2 * half
     here, layer = lax.axis_index("ctx"), lax.axis_index("dp")
-    shard = here * depth + layer
+    shards = count * depth
+    shard = layer * count + here
     thin = small_ref.shape[1]
     own_ref = tokens_ref.at[lax.axis_index("tp")]
-    greet_all(others("ctx", count) + others("dp", depth))
+
+    def peer(mask):
+        other = lax.bitwise_xor(shard, mask)
+        return {"dp": other // count, "ctx": other % count}
+
+    barrier = pltpu.get_barrier_semaphore()
+
+    def greet_peer(mask, _):
+        pl.semaphore_signal(barrier, 1, device_id=peer(mask), device_id_type=MESH)
+        return 0
+
+    lax.fori_loop(1, shards, greet_peer, 0)
+    pl.semaphore_wait(barrier, shards - 1)
+
+    def gains(mask):
+        return pltpu.make_async_remote_copy(
+            src_ref=small_ref,
+            dst_ref=shards_v.at[shard],
+            send_sem=shard_send.at[mask],
+            recv_sem=shard_recv.at[mask],
+            device_id=peer(mask),
+            device_id_type=MESH,
+        )
+
+    def gains_start(mask, _):
+        gains(mask).start()
+        return 0
+
+    def gains_wait(mask, _):
+        gains(mask).wait()
+        return 0
+
+    lax.fori_loop(1, shards, gains_start, 0)
     heads = piece_copies(
         count, lambda i: head_pieces_ref.at[i], head_ref.at[layer], head_send, head_recv
     )
@@ -651,25 +689,6 @@
         copy.start()
     first = pltpu.make_async_copy(own_ref, rows_v.at[pl.ds(0, size)], load_sem.at[1])
     first.start()
-    shards_v[shard] = small_ref[...]
-    for bit, device in enumerate(axis_bits("dp", depth) + axis_bits("ctx", count)):
-        reach = 1 << bit
-        mine = pl.ds(shard // reach * reach, reach)
-        theirs = pl.ds((shard // reach ^ 1) * reach, reach)
-        copies = [
-            pltpu.make_async_remote_copy(
-                src_ref=shards_v.at[mine],
-                dst_ref=shards_v.at[place],
-                send_sem=shard_send.at[bit],
-                recv_sem=shard_recv.at[bit],
-                device_id=device,
-                device_id_type=MESH,
-            )
-            for place in (mine, theirs)
-        ]
-        copies[0].start()
-        copies[0].wait_send()
-        copies[1].wait_recv()
     shares = links.sharing(own_ref, rows_v, share_send, share_recv)
     links.pass_on(shares, 0)
     line = Line(head_ref, depth, line_send, line_recv)
@@ -686,10 +705,10 @@
     line.start(1)
     for copy in pieces:
         copy.start()
-    for c in range(count):
-        for d in range(depth):
-            n = d * count + c
-            table_ref[:, n * thin : (n + 1) * thin] = shards_v[c * depth + d]
+    shards_v[shard] = small_ref[...]
+    lax.fori_loop(1, shards, gains_wait, 0)
+    for n in range(shards):
+        table_ref[:, n * thin : (n + 1) * thin] = shards_v[n]
     chunk = min(32, half)
     stores = []
     for i in range(max(count, depth)):
@@ -732,7 +751,6 @@
     length = rows * count
     links = Links(count, rows // 2)
     copies = len(links.pairs)
-    bits = (count - 1).bit_length() + (depth - 1).bit_length()
     anywhere = pl.BlockSpec(memory_space=pl.ANY)
     inside = pl.BlockSpec(memory_space=pltpu.VMEM)
     dma = pltpu.SemaphoreType.DMA
@@ -762,8 +780,8 @@
             dma((count - 1,)),
             dma((2, depth - 1)),
             dma((2, depth - 1)),
-            dma((bits,)),
-            dma((bits,)),
+            dma((count * depth,)),
+            dma((count * depth,)),
         ],
         compiler_params=pltpu.CompilerParams(
             collective_id=1, has_side_effects=True, vmem_limit_bytes=40 * 1024 * 1024

time: 741 us -> 739 us (level)
  no operation moved by 1% of the time
where the time goes in v6:
time: 739 us; the launch traced here: 735 us
  Pallas kernels  687 us (93%)
  local copies, waits for them, and re-layouts  26.3 us (4%)
  between operations  14.4 us (2%)
    pallas_call x1, Pallas kernels, feed_forward(): pl.pallas_call(functools.partial(feed_forward_kernel, links), out_shape=(...  153 us
    pallas_call x1, Pallas kernels, attend(): pl.pallas_call(functools.partial(attend_kernel, links, heads), out_shape=...  146 us
    pallas_call x1, Pallas kernels, first_back(): pl.pallas_call(functools.partial(first_back_kernel, links), out_shape=(ja...  129 us
    pallas_call x1, Pallas kernels, attend_back(): pl.pallas_call(functools.partial(attend_back_kernel, links, heads), out_s...  120 us
    pallas_call x1, Pallas kernels, front(): pl.pallas_call(functools.partial(front_kernel, links, depth), out_shape=(...  115 us
    pallas_call x1, Pallas kernels, end(): pl.pallas_call(functools.partial(end_kernel, count, depth, heads), out_sh...  24.1 us
    unnamed x44, local copies, waits for them, and re-layouts  21.7 us
  transfers between devices with their start and end apart: 4, of which 1 were waited for; matrix products, arithmetic and copies ran while one was open for 0% of the time, Pallas kernels for 54%

profile of v6, /device:TPU:0, one launch (start us, length us, event | category | flops | bytes accessed | tf_op | source)
XLA Modules:
  0.0 735.1 jit_solution(9892429989268326965)
XLA Ops:
  7.3 0.9 stack.34
  8.1 1.1 copy.37
  9.2 1.1 copy.38
  10.4 1.1 copy.39
  12.1 0.7 copy.43
  13.3 1.5 copy.42
  15.2 1.9 copy-done
  17.0 115.5 %front.1 = (bf16[2048,2048]{1,0:T(8,128)(2,1)}, bf16[4,4,128,1024]{3,2,1,0:T(8,128)(2,1)S(1)}, bf16[4,128,2048]{2,1,0:T(8,128)(2,1)}, f32[8,2048]{1,0:T(8,128)S(1)}) custom-call(bf16[2,512,2048]{2,1,0:T(8,128)(2,1)S(1)} %copy-done, bf16[4,128,1024]{2,1,0:T(8,128)(2,1)S(1)} %pad_maximum_fusion.2.head_pieces_ref, ...), custom_call_target="tpu_custom_call" | custom-call | flops 83886080 | bytes 120000000 | tf_op jit(solution)/shard_map/front/pallas_call | solution.py:757
  132.5 2.0 copy-done.4
  134.5 0.6 copy-done.5
  135.8 1.1 collective-permute-done
  136.9 0.6 maximum_convert_fusion.1.shift_ref
  137.5 0.6 maximum_convert_fusion.shift_ref
  138.1 146.4 %attend.1 = (bf16[2048,1536]{1,0:T(8,128)(2,1)}, bf16[2048,512]{1,0:T(8,128)(2,1)}, f32[4,8,2048]{2,1,0:T(8,128)}, bf16[2048,2048]{1,0:T(8,128)(2,1)}, f32[512,2...) custom-call(bf16[2048,2048]{1,0:T(8,128)(2,1)} %get-tuple-element.54.rows_ref.first_ref, ...), custom_call_target="tpu_custom_call" | custom-call | flops 27917287424 | bytes 33554432 | tf_op jit(solution)/shard_map/attend/pallas_call | solution.py:1162
  284.5 153.3 %feed_forward.1 = (bf16[2048,2048]{1,0:T(8,128)(2,1)}, bf16[2048,2048]{1,0:T(8,128)(2,1)}, bf16[2048,2048]{1,0:T(8,128)(2,1)}, bf16[2048,1536]{1,0:T(8,128)(2,1)...) custom-call(bf16[512,2048]{1,0:T(8,128)(2,1)} %get-tuple-element.57., ...), custom_call_target="tpu_custom_call" | custom-call | flops 85899345920 | bytes 67108864 | tf_op jit(solution)/shard_map/feed_forward/pallas_call | solution.py:475
  437.9 119.5 %attend_back.1 = (bf16[2048,2048]{1,0:T(8,128)(2,1)}, bf16[2048,1536]{1,0:T(8,128)(2,1)}, bf16[512,1024]{1,0:T(8,128)(2,1)}, bf16[2048,1536]{1,0:T(8,128)(2,1)}) custom-call(bf16[512,2048]{1,0:T(8,128)(2,1)} %get-tuple-element.61.own_ref, bf16[2,2048,1024]{2,1,0:T(8,128)(2,1)} %get-tuple-element.62.weight_ref, bf16[2048,1536]{1,0:T(8,128)(2,1)} %get-tuple-element.63.qkv_ref, ...), custom_call_target="tpu_custom_call" | custom-call | flops 39728447488 | bytes 46137344 | tf_op jit(solution)/shard_map/attend_back/pallas_call | solution.py:1488
  557.5 128.6 %first_back.1 = (bf16[2,512,2048]{2,1,0:T(8,128)(2,1)}, bf16[2,512,2048]{2,1,0:T(8,128)(2,1)}, f32[8,2048]{1,0:T(8,128)}, f32[1,1536]{1,0:T(1,128)}, f32[4,512,128]{2,1,0:T(8,128)}, /*index=5*/f32[128,4096]{1,0:T(8,128)}) custom-call(bf16[2048,1536]{1,0:T(8,128)(2,1)} %get-tuple-element.69.grads_ref, bf16[2,2048,1024]{2,1,0:T(8,128)(2,1)} %get-tuple-element.62.weight_ref, ...), custom_call_target="tpu_custom_call" | custom-call | flops 21474836480 | bytes 29360128 | tf_op jit(solution)/shard_map/first_back/pallas_call | solution.py:1761
  686.1 0.7 pad_maximum_fusion.4.biases_ref
  686.9 1.4 copy-done.1
  688.3 0.8 copy-done.3
  689.1 24.1 %end.1 = (f32[128,1024]{1,0:T(8,128)S(1)}, f32[128,1024]{1,0:T(8,128)S(1)}, f32[128,1024]{1,0:T(8,128)S(1)}, f32[1024,128]{1,0:T(8,128)S(1)}, f32[4,512,128]{2,1...) custom-call(bf16[512,1536]{1,0:T(8,128)(2,1)S(1)} %copy-done.1, f32[8,2048]{1,0:T(8,128)S(1)} %copy-done.2, ...), custom_call_target="tpu_custom_call" | custom-call | bytes 40000000 | tf_op jit(solution)/shard_map/end/pallas_call | solution.py:929
  713.8 0.6 copy.50
  714.4 0.6 fusion.1
  715.0 3.0 pad_maximum_fusion.1
  718.0 2.1 copy.58
  720.2 1.6 copy-done.6
  721.7 2.0 copy.59
  723.8 0.8 copy.60
  724.6 0.8 copy.61
  725.4 0.8 copy.62
  726.1 0.8 copy.63
  726.9 1.3 copy.64
  (60 shorter events, 2.8 us)
Async XLA Ops:
  7.2 4.7 copy-start.10
  7.2 4.9 copy-start.9
  7.2 277.3 %all-gather.2.cloned.1.call-start = ((), (), s32[]{:S(2)}) async-start(), calls=%async_computation.2 | async-start | bytes 10485760 | tf_op jit(solution)/shard_map/all_gather | solution.py:1874
  14.8 2.2 copy-start
  17.0 118.4 %copy-start.13 = (bf16[1024]{0:T(1024)(128)(2,1)S(1)}, bf16[1024]{0:T(1024)(128)(2,1)}, u32[]{:S(2)}) copy-start(bf16[1024]{0:T(1024)(128)(2,1)} %param.24) | copy-start | bytes 6148
  17.0 118.4 %copy-start.14 = (bf16[1024]{0:T(1024)(128)(2,1)S(1)}, bf16[1024]{0:T(1024)(128)(2,1)}, u32[]{:S(2)}) copy-start(bf16[1024]{0:T(1024)(128)(2,1)} %param.27) | copy-start | bytes 6148
  17.0 118.6 %copy-start.12 = (bf16[4096]{0:T(1024)(128)(2,1)S(1)}, bf16[4096]{0:T(1024)(128)(2,1)}, u32[]{:S(2)}) copy-start(bf16[4096]{0:T(1024)(128)(2,1)} %param.31) | copy-start | bytes 24580
  132.5 2.0 copy-start.4
  134.5 0.6 copy-start.5
  135.2 422.3 %reduce-scatter.3.cloned.1.call-start = ((), (), s32[]{:S(2)}) async-start(), calls=%async_computation.3 | async-start | bytes 7864320 | tf_op jit(solution)/shard_map/reduce_scatter | solution.py:49
  135.7 1.2 collective-permute-start
  437.9 249.0 %reduce-scatter.5.cloned.1.call-start = ((), (), s32[]{:S(2)}) async-start(), calls=%async_computation.4 | async-start | bytes 7864320 | tf_op jit(solution)/shard_map/reduce_scatter | solution.py:49
  557.5 128.6 %copy-start.11 = (f32[1,2048]{1,0:T(1,128)S(1)}, f32[1,2048]{1,0:T(1,128)}, u32[]{:S(2)}) copy-start(f32[1,2048]{1,0:T(1,128)} %get-tuple-element.80) | copy-start | bytes 24580
  557.5 129.3 %copy-start.2 = (f32[8,2048]{1,0:T(8,128)S(1)}, f32[8,2048]{1,0:T(8,128)}, u32[]{:S(2)}) copy-start(f32[8,2048]{1,0:T(8,128)} %get-tuple-element.78.vectors_ref) | copy-start | bytes 196612
  686.9 1.4 copy-start.1
  688.3 0.8 copy-start.3
  714.4 3.6 copy-start.7
  718.0 3.7 copy-start.6
  723.8 3.2 copy-start.8
Sparse Core Ops, SparseCore 0:
  135.3 146.8 all-gather.1
  438.0 107.9 reduce-scatter.2
  557.6 109.4 reduce-scatter.4

commit v7 on v5

--- a/solution.py
+++ b/solution.py
@@ -1343,6 +1343,7 @@
         result_ref[:, value_at] = value_v[:, at].astype(BF16)
         return 0
 
+    links.combine(sums, kept_v, send_v, recv_v, count // 2 - 1, 1)
     lax.fori_loop(0, heads, store_head, 0)
     loads[10].wait()
     loads[7].wait()
@@ -1359,7 +1360,6 @@
     )
     again = pltpu.make_async_copy(full_ref, big_v, load_sem.at[7])
     again.start()
-    links.combine(sums, kept_v, send_v, recv_v, count // 2 - 1, 1)
     again.wait()
     end_second = weight_grads(
         partner,

time: 741 us -> 736 us (level)
  transfers between devices with their start and end apart: 4 -> 4, of which waited for: 1 -> 1; matrix products, arithmetic and copies ran while one was open for 0% -> 0% of each run, Pallas kernels for 54% -> 53%
where the time goes in v7:
time: 736 us; the launch traced here: 732 us
  Pallas kernels  684 us (93%)
  local copies, waits for them, and re-layouts  26.3 us (4%)
  between operations  14.5 us (2%)
    pallas_call x1, Pallas kernels, feed_forward(): pl.pallas_call(functools.partial(feed_forward_kernel, links), out_shape=(...  153 us
    pallas_call x1, Pallas kernels, attend(): pl.pallas_call(functools.partial(attend_kernel, links, heads), out_shape=...  146 us
    pallas_call x1, Pallas kernels, first_back(): pl.pallas_call(functools.partial(first_back_kernel, links), out_shape=(ja...  126 us
    pallas_call x1, Pallas kernels, attend_back(): pl.pallas_call(functools.partial(attend_back_kernel, links, heads), out_s...  119 us
    pallas_call x1, Pallas kernels, front(): pl.pallas_call(functools.partial(front_kernel, links, depth), out_shape=(...  117 us
    pallas_call x1, Pallas kernels, end(): pl.pallas_call(functools.partial(end_kernel, count, depth, heads), out_sh...  23.3 us
    unnamed x44, local copies, waits for them, and re-layouts  21.7 us
  transfers between devices with their start and end apart: 4, of which 1 were waited for; matrix products, arithmetic and copies ran while one was open for 0% of the time, Pallas kernels for 53%

profile of v7, /device:TPU:0, one launch (start us, length us, event | category | flops | bytes accessed | tf_op | source)
XLA Modules:
  0.0 732.3 jit_solution(6938683988288097312)
XLA Ops:
  7.3 0.9 stack.34
  8.1 1.1 copy.37
  9.2 1.1 copy.38
  10.4 1.1 copy.39
  12.1 0.7 copy.43
  13.3 1.5 copy.42
  15.2 1.9 copy-done
  17.0 116.9 %front.1 = (bf16[2048,2048]{1,0:T(8,128)(2,1)}, bf16[4,4,128,1024]{3,2,1,0:T(8,128)(2,1)S(1)}, bf16[4,128,2048]{2,1,0:T(8,128)(2,1)}, f32[8,2048]{1,0:T(8,128)S(1)}) custom-call(bf16[2,512,2048]{2,1,0:T(8,128)(2,1)S(1)} %copy-done, bf16[4,128,1024]{2,1,0:T(8,128)(2,1)S(1)} %pad_maximum_fusion.2.head_pieces_ref, ...), custom_call_target="tpu_custom_call" | custom-call | flops 83886080 | bytes 120000000 | tf_op jit(solution)/shard_map/front/pallas_call | solution.py:739
  134.0 2.0 copy-done.4
  136.0 0.6 copy-done.5
  137.3 1.1 collective-permute-done
  138.4 0.6 maximum_convert_fusion.1.shift_ref
  139.0 0.6 maximum_convert_fusion.shift_ref
  139.7 146.3 %attend.1 = (bf16[2048,1536]{1,0:T(8,128)(2,1)}, bf16[2048,512]{1,0:T(8,128)(2,1)}, f32[4,8,2048]{2,1,0:T(8,128)}, bf16[2048,2048]{1,0:T(8,128)(2,1)}, f32[512,2...) custom-call(bf16[2048,2048]{1,0:T(8,128)(2,1)} %get-tuple-element.54.rows_ref.first_ref, ...), custom_call_target="tpu_custom_call" | custom-call | flops 27917287424 | bytes 33554432 | tf_op jit(solution)/shard_map/attend/pallas_call | solution.py:1144
  286.0 152.9 %feed_forward.1 = (bf16[2048,2048]{1,0:T(8,128)(2,1)}, bf16[2048,2048]{1,0:T(8,128)(2,1)}, bf16[2048,2048]{1,0:T(8,128)(2,1)}, bf16[2048,1536]{1,0:T(8,128)(2,1)...) custom-call(bf16[512,2048]{1,0:T(8,128)(2,1)} %get-tuple-element.57., ...), custom_call_target="tpu_custom_call" | custom-call | flops 85899345920 | bytes 67108864 | tf_op jit(solution)/shard_map/feed_forward/pallas_call | solution.py:470
  439.0 118.8 %attend_back.1 = (bf16[2048,2048]{1,0:T(8,128)(2,1)}, bf16[2048,1536]{1,0:T(8,128)(2,1)}, bf16[512,1024]{1,0:T(8,128)(2,1)}, bf16[2048,1536]{1,0:T(8,128)(2,1)}) custom-call(bf16[512,2048]{1,0:T(8,128)(2,1)} %get-tuple-element.61.own_ref, bf16[2,2048,1024]{2,1,0:T(8,128)(2,1)} %get-tuple-element.62.weight_ref, bf16[2048,1536]{1,0:T(8,128)(2,1)} %get-tuple-element.63.qkv_ref, ...), custom_call_target="tpu_custom_call" | custom-call | flops 39728447488 | bytes 46137344 | tf_op jit(solution)/shard_map/attend_back/pallas_call | solution.py:1470
  557.8 126.1 %first_back.1 = (bf16[2,512,2048]{2,1,0:T(8,128)(2,1)}, bf16[2,512,2048]{2,1,0:T(8,128)(2,1)}, f32[8,2048]{1,0:T(8,128)}, f32[1,1536]{1,0:T(1,128)}, f32[4,512,128]{2,1,0:T(8,128)}, /*index=5*/f32[128,4096]{1,0:T(8,128)}) custom-call(bf16[2048,1536]{1,0:T(8,128)(2,1)} %get-tuple-element.69.grads_ref, bf16[2,2048,1024]{2,1,0:T(8,128)(2,1)} %get-tuple-element.62.weight_ref, ...), custom_call_target="tpu_custom_call" | custom-call | flops 21474836480 | bytes 29360128 | tf_op jit(solution)/shard_map/first_back/pallas_call | solution.py:1743
  684.0 0.7 pad_maximum_fusion.4.biases_ref
  684.8 1.4 copy-done.1
  686.2 0.8 copy-done.3
  687.0 23.3 %end.1 = (f32[128,1024]{1,0:T(8,128)S(1)}, f32[128,1024]{1,0:T(8,128)S(1)}, f32[128,1024]{1,0:T(8,128)S(1)}, f32[1024,128]{1,0:T(8,128)S(1)}, f32[4,512,128]{2,1...) custom-call(bf16[512,1536]{1,0:T(8,128)(2,1)S(1)} %copy-done.1, f32[8,2048]{1,0:T(8,128)S(1)} %copy-done.2, ...), custom_call_target="tpu_custom_call" | custom-call | bytes 40000000 | tf_op jit(solution)/shard_map/end/pallas_call | solution.py:911
  710.9 0.6 copy.50
  711.5 0.6 fusion.1
  712.1 3.0 pad_maximum_fusion.1
  715.1 2.1 copy.58
  717.2 1.6 copy-done.6
  718.8 2.0 copy.59
  720.8 0.8 copy.60
  721.6 0.8 copy.61
  722.4 0.8 copy.62
  723.2 0.8 copy.63
  724.0 1.3 copy.64
  (60 shorter events, 2.8 us)
Async XLA Ops:
  7.2 4.7 copy-start.10
  7.2 4.9 copy-start.9
  7.2 278.8 %all-gather.2.cloned.1.call-start = ((), (), s32[]{:S(2)}) async-start(), calls=%async_computation.2 | async-start | bytes 10485760 | tf_op jit(solution)/shard_map/all_gather | solution.py:1856
  14.8 2.2 copy-start
  17.0 119.9 %copy-start.13 = (bf16[1024]{0:T(1024)(128)(2,1)S(1)}, bf16[1024]{0:T(1024)(128)(2,1)}, u32[]{:S(2)}) copy-start(bf16[1024]{0:T(1024)(128)(2,1)} %param.24) | copy-start | bytes 6148
  17.0 119.9 %copy-start.14 = (bf16[1024]{0:T(1024)(128)(2,1)S(1)}, bf16[1024]{0:T(1024)(128)(2,1)}, u32[]{:S(2)}) copy-start(bf16[1024]{0:T(1024)(128)(2,1)} %param.27) | copy-start | bytes 6148
  17.0 120.1 %copy-start.12 = (bf16[4096]{0:T(1024)(128)(2,1)S(1)}, bf16[4096]{0:T(1024)(128)(2,1)}, u32[]{:S(2)}) copy-start(bf16[4096]{0:T(1024)(128)(2,1)} %param.31) | copy-start | bytes 24580
  134.0 2.0 copy-start.4
  136.0 0.6 copy-start.5
  136.6 421.2 %reduce-scatter.3.cloned.1.call-start = ((), (), s32[]{:S(2)}) async-start(), calls=%async_computation.3 | async-start | bytes 7864320 | tf_op jit(solution)/shard_map/reduce_scatter | solution.py:49
  137.2 1.2 collective-permute-start
  439.0 245.8 %reduce-scatter.5.cloned.1.call-start = ((), (), s32[]{:S(2)}) async-start(), calls=%async_computation.4 | async-start | bytes 7864320 | tf_op jit(solution)/shard_map/reduce_scatter | solution.py:49
  557.8 126.2 %copy-start.11 = (f32[1,2048]{1,0:T(1,128)S(1)}, f32[1,2048]{1,0:T(1,128)}, u32[]{:S(2)}) copy-start(f32[1,2048]{1,0:T(1,128)} %get-tuple-element.80) | copy-start | bytes 24580
  557.8 126.9 %copy-start.2 = (f32[8,2048]{1,0:T(8,128)S(1)}, f32[8,2048]{1,0:T(8,128)}, u32[]{:S(2)}) copy-start(f32[8,2048]{1,0:T(8,128)} %get-tuple-element.78.vectors_ref) | copy-start | bytes 196612
  684.7 1.4 copy-start.1
  686.2 0.8 copy-start.3
  711.5 3.6 copy-start.7
  715.1 3.7 copy-start.6
  720.8 3.2 copy-start.8
Sparse Core Ops, SparseCore 0:
  136.7 147.7 all-gather.1
  439.1 108.8 reduce-scatter.2
  557.9 108.0 reduce-scatter.4
